TPU v7x, 256 devices: a whole 4x4x8 slice. The times are simulated.
256 devices in a mesh: gx: 16 (over y, z_hi), gy: 8 (over x, core), ha: 2 (over z_lo).
Axes of the slice: x: 4, y: 4, z: 8 (z_hi: 4, z_lo: 2; z = z_hi * 2 + z_lo), core: 2. Of those that a mesh axis runs over, the one named last changes fastest.
Arguments:
- coupling: bfloat16 [16, 16, 4, 768, 768], P('gx', ('gy', 'ha')), may hold values from -0.125 to 0.125
- interior_inverse: bfloat16 [16, 16, 4, 768, 768], P('gx', ('gy', 'ha')), as said below
- boundary_stiffness: bfloat16 [16, 16, 768, 768], P('gx', ('gy', 'ha')), as said below
- block_counts: int32 [16, 16], P('gx', ('gy', 'ha')), may hold values from 1 to 4, as said below
- initial_traces: float32 [16, 16, 768, 128], P('gx', ('gy', 'ha')), may hold values from -2 to 2
- trace_loads: float32 [16, 16, 768, 128], P('gx', ('gy', 'ha')), may hold values from -18 to 18
Outputs:
- traces: float32 [16, 16, 768, 128], P('gx', ('gy', 'ha'))
- residual: float32 [16, 16, 768, 128], P('gx', ('gy', 'ha'))
Inputs may be any that keep to these rules, and one draw needn't show every extreme that they name: `block_counts`: the two cells in columns 2m and 2m+1 of one grid row hold at most 5 blocks together; some cell holds 4. `interior_inverse`: symmetric in its last two dimensions. `boundary_stiffness`: symmetric in its last two dimensions.
All inputs are finite; a program needn't handle non-finite values.
Results may differ from a plain program's by a relative error of at most 0.00095.
Values may be sent and summed in bfloat16 or wider, within the bound.
No kernel may reach another device: no remote copies, remote signals or barrier semaphores. Data moves between devices by JAX's collectives and lax.ppermute only.
A program may use at most 128 MiB of HBM per device.

v0:
```python
import jax
import jax.numpy as jnp
from jax import lax
from jax.sharding import PartitionSpec as P

SWEEPS = 3


penalty_weight = 2.0
lower_bound = 1.0
upper_bound = 14.0
spectrum_centre = (upper_bound + lower_bound) / 2.0
spectrum_half = (upper_bound - lower_bound) / 2.0
sigma_ratio = spectrum_centre / spectrum_half


def from_behind(block, axis, distance):
    devices = range(lax.axis_size(axis))
    route = [(i - distance, i) for i in devices if i - distance in devices]
    return lax.ppermute(block, axis, route)


def schur_block(coupling_block, inverse_block):
    product = jnp.dot(coupling_block, inverse_block, preferred_element_type=jnp.float32).astype(
        jnp.bfloat16
    )
    return jnp.dot(product, coupling_block.T, preferred_element_type=jnp.float32)


def apply_operator(condensed, traces):
    trace_width, load_width = traces.shape
    mode_width = trace_width // 6
    coupled = jnp.dot(
        condensed, traces, precision=lax.Precision.HIGHEST, preferred_element_type=jnp.float32
    )
    face_traces = traces.reshape(6, mode_width, load_width)
    from_below_x = from_behind(face_traces[1], "gx", 1)
    from_above_x = from_behind(face_traces[0], "gx", -1)
    from_below_y = from_behind(face_traces[3], ("gy", "ha"), 1)
    from_above_y = from_behind(face_traces[2], ("gy", "ha"), -1)
    absent = jnp.zeros_like(from_below_x)
    neighbours = jnp.stack(
        [from_below_x, from_above_x, from_below_y, from_above_y, absent, absent], 0
    )
    neighbours = neighbours.reshape(trace_width, load_width)
    return coupled + penalty_weight * (traces - neighbours)


def on_device(
    coupling, interior_inverse, boundary_stiffness, block_counts, initial_traces, trace_loads
):
    blocks = block_counts[0, 0]
    own_coupling = coupling[0, 0]
    own_inverse = interior_inverse[0, 0]
    slot_total = own_coupling.shape[0]
    trace_width = own_coupling.shape[1]
    empty = jnp.zeros((trace_width, trace_width), jnp.float32)
    condensed = boundary_stiffness[0, 0].astype(jnp.float32)
    for slot_index in range(slot_total):
        term = lax.cond(
            blocks > slot_index,
            lambda: schur_block(own_coupling[slot_index], own_inverse[slot_index]),
            lambda: empty,
        )
        condensed = condensed - term
    loads_local = trace_loads[0, 0]
    traces = initial_traces[0, 0]
    residual = loads_local - apply_operator(condensed, traces)
    direction = residual / spectrum_centre
    weight_old = 1.0 / sigma_ratio
    for sweep_index in range(SWEEPS):
        traces = traces + direction
        residual = loads_local - apply_operator(condensed, traces)
        if sweep_index + 1 < SWEEPS:
            weight_new = 1.0 / (2.0 * sigma_ratio - weight_old)
            direction = (
                weight_new * weight_old * direction + 2.0 * weight_new / spectrum_half * residual
            )
            weight_old = weight_new
    return (traces[None, None], residual[None, None])


def solution(mesh):
    in_specs = (
        P("gx", ("gy", "ha"), None, None, None),
        P("gx", ("gy", "ha"), None, None, None),
        P("gx", ("gy", "ha"), None, None),
        P("gx", ("gy", "ha")),
        P("gx", ("gy", "ha"), None, None),
        P("gx", ("gy", "ha"), None, None),
    )
    out_specs = (P("gx", ("gy", "ha"), None, None), P("gx", ("gy", "ha"), None, None))
    return jax.shard_map(
        on_device, mesh=mesh, in_specs=in_specs, out_specs=out_specs, check_vma=False
    )
```

profile of v0, /device:TPU:27, one launch (start us, length us, event | category | flops | bytes accessed | tf_op | source)
XLA Modules:
  0.0 109.0 jit_solution(6063158666728812904)
XLA Ops:
  0.6 1.6 %slice_bitcast_fusion = (f32[128,128]{1,0:T(8,128)}, f32[128,128]{1,0:T(8,128)}, f32[128,128]{1,0:T(8,128)}, f32[128,128]{1,0:T(8,128)}) fusion(f32[1,1,768,128]{3,2,1,0:T(8,128)} %param.18), kind=kLoop, calls=%fused_computation.80 | loop fusion | bytes 524288 | tf_op jit(solution)/shard_map/squeeze | solution.py:40
  2.3 4.9 %collective-permute-start = (f32[128,128]{1,0:T(8,128)}, f32[128,128]{1,0:T(8,128)}, u32[]{:S(2)}, u32[]{:S(2)}) collective-permute-start(f32[128,128]{1,0:T(8,128)} %get-tuple-element.52), channel_id=1, source_target_pairs={{0,16},{16,32},{32,48},{48,64},{64,80},{80,96},{96,112},{112,128},... | collective-permute-start | bytes 196616 | tf_op jit(solution)/shard_map/ppermute | solution.py:20
  7.1 5.1 %collective-permute-start.1 = (f32[128,128]{1,0:T(8,128)}, f32[128,128]{1,0:T(8,128)}, u32[]{:S(2)}, u32[]{:S(2)}) collective-permute-start(f32[128,128]{1,0:T(8,128)} %get-tuple-element.51), channel_id=1, source_target_pairs={{16,0},{32,16},{48,32},{64,48},{80,64},{96,80},{112,96},{128,112},... | collective-permute-start | bytes 196616 | tf_op jit(solution)/shard_map/ppermute | solution.py:20
  12.3 2.6 %collective-permute-start.2 = (f32[128,128]{1,0:T(8,128)}, f32[128,128]{1,0:T(8,128)}, u32[]{:S(2)}, u32[]{:S(2)}) collective-permute-start(f32[128,128]{1,0:T(8,128)} %get-tuple-element.53), channel_id=1, source_target_pairs={{0,1},{1,2},{2,3},{3,4},{4,5},{5,6},{6,7},{7,8},{8,9},{9,10},{10,1... | collective-permute-start | bytes 196616 | tf_op jit(solution)/shard_map/ppermute | solution.py:20
  14.9 2.9 %collective-permute-start.3 = (f32[128,128]{1,0:T(8,128)}, f32[128,128]{1,0:T(8,128)}, u32[]{:S(2)}, u32[]{:S(2)}) collective-permute-start(f32[128,128]{1,0:T(8,128)} %get-tuple-element.50), channel_id=1, source_target_pairs={{1,0},{2,1},{3,2},{4,3},{5,4},{6,5},{7,6},{8,7},{9,8},{10,9},{11,1... | collective-permute-start | bytes 196616 | tf_op jit(solution)/shard_map/ppermute | solution.py:20
  18.5 4.1 %conditional.4 = (f32[768,768]{1,0:T(8,128)S(1)}) conditional(s32[]{:T(128)} %bitcast.11, () %tuple.32, (bf16[4,768,768]{2,1,0:T(8,128)(2,1)}, bf16[4,768,768]{2,1,0:T(8,128)(2,1)}) %tuple.64), branch_computations={%region_0.0_spmd, %region_1.0_spmd} | conditional | flops 1812529152 | bytes 5898248 | solution.py:60
  18.5 4.1 %fusion.1 = f32[768,768]{1,0:T(8,128)S(1)} fusion(bf16[4,768,768]{2,1,0:T(8,128)(2,1)} %get-tuple-element.24, bf16[4,768,768]{2,1,0:T(8,128)(2,1)} %get-tuple-element.26), kind=kOutput, calls=%fused_computation.2 | convolution fusion | flops 1812529152 | bytes 5898240 | tf_op jit(solution)/shard_map/cond/branch_1_fun/dot_general | solution.py:27
  22.6 5.5 %conditional.5 = (f32[768,768]{1,0:T(8,128)}) conditional(s32[]{:T(128)} %bitcast.14, () %tuple.34, (bf16[4,768,768]{2,1,0:T(8,128)(2,1)}, bf16[4,768,768]{2,1,0:T(8,128)(2,1)}) %tuple.65), branch_computations={%region_2.0_spmd, %region_3.0_spmd} | conditional | flops 1812529152 | bytes 5898248 | solution.py:60
  22.7 5.5 %fusion.12 = f32[768,768]{1,0:T(8,128)} fusion(bf16[4,768,768]{2,1,0:T(8,128)(2,1)} %get-tuple-element.27, bf16[4,768,768]{2,1,0:T(8,128)(2,1)} %get-tuple-element.28), kind=kOutput, calls=%fused_computation.10 | convolution fusion | flops 1812529152 | bytes 5898240 | tf_op jit(solution)/shard_map/cond/branch_1_fun/dot_general | solution.py:27
  28.2 5.5 %conditional.6 = (f32[768,768]{1,0:T(8,128)}) conditional(s32[]{:T(128)} %bitcast.15, () %tuple.35, (bf16[4,768,768]{2,1,0:T(8,128)(2,1)}, bf16[4,768,768]{2,1,0:T(8,128)(2,1)}) %tuple.66), branch_computations={%region_4.0_spmd, %region_5.0_spmd} | conditional | flops 1812529152 | bytes 5898248 | solution.py:60
  28.2 5.5 %fusion.23 = f32[768,768]{1,0:T(8,128)} fusion(bf16[4,768,768]{2,1,0:T(8,128)(2,1)} %get-tuple-element.32, bf16[4,768,768]{2,1,0:T(8,128)(2,1)} %get-tuple-element.33), kind=kOutput, calls=%fused_computation.18 | convolution fusion | flops 1812529152 | bytes 5898240 | tf_op jit(solution)/shard_map/cond/branch_1_fun/dot_general | solution.py:27
  33.7 0.0 copy-start.3
  33.7 1.6 %conditional.7 = (f32[768,768]{1,0:T(8,128)}) conditional(s32[]{:T(128)} %bitcast.16, () %tuple.36, (bf16[4,768,768]{2,1,0:T(8,128)(2,1)}, bf16[4,768,768]{2,1,0:T(8,128)(2,1)}) %tuple.67), branch_computations={%region_6.0_spmd, %region_7.0_spmd} | conditional | flops 1812529152 | bytes 5898248 | solution.py:60
  33.7 1.6 %broadcast_in_dim.15 = f32[768,768]{1,0:T(8,128)} broadcast(f32[]{:T(128)} %constant.11.clone), dimensions={} | broadcast | bytes 2359300 | tf_op jit(solution)/shard_map/broadcast_in_dim | solution.py:57
  35.3 0.1 copy-done.3
  35.5 0.0 copy-start.2
  35.5 0.0 copy-start
  35.5 3.8 %fusion.46 = f32[768,768]{1,0:T(8,128)S(1)} fusion(f32[768,768]{1,0:T(8,128)} %get-tuple-element.61, f32[768,768]{1,0:T(8,128)} %get-tuple-element.60, f32[768,768]{1,0:T(8,128)} %get-tuple-element.59, f32[768,768]{1,0:T(8,128)S(1)} %get-tuple-element.58, bf16[1,1,768,768]{3,2,1,0:T(8,128)(2,1)S(1)} %copy-done.3), kind=kLoop, calls=%fused_computation.35 | loop fusion | flops 2949120 | bytes 12976128 | tf_op jit(solution)/shard_map/sub | solution.py:65
  39.3 0.0 collective-permute-done
  39.3 0.8 bitcast_dynamic-update-slice_fusion.15
  40.1 0.0 collective-permute-done.1
  40.1 0.8 bitcast_dynamic-update-slice_fusion.14
  41.0 0.0 collective-permute-done.2
  41.0 0.8 bitcast_dynamic-update-slice_fusion.13
  41.8 0.0 collective-permute-done.3
  41.8 0.8 bitcast_dynamic-update-slice_fusion.12
  42.7 0.0 copy-done.2
  42.8 0.0 copy-done
  42.8 2.0 %bitcast_add_fusion = (f32[768,128]{1,0:T(8,128)S(1)}, f32[768,128]{1,0:T(8,128)S(1)}) fusion(f32[1,1,768,128]{3,2,1,0:T(8,128)S(1)} %copy-done.2, f32[768,128]{1,0:T(8,128)S(1)} %fusion.60, f32[768,768]{1,0:T(8,128)S(1)} %fusion.46, f32[1,1,768,128]{3,2,1,0:T(8,128)S(1)} %copy-done), kind=kOutput, calls=%fused_computation.58 | convolution fusion | flops 906362880 | bytes 4325376 | tf_op jit(solution)/shard_map/dot_general | solution.py:33
  44.8 1.9 %collective-permute-start.4 = (f32[128,128]{1,0:T(8,128)S(1)}, f32[128,128]{1,0:T(8,128)S(1)}, u32[]{:S(2)}, u32[]{:S(2)}) collective-permute-start(f32[128,128]{1,0:T(8,128)S(1)} %get-tuple-element.49), channel_id=1, source_target_pairs={{0,16},{16,32},{32,48},{48,64},{64,80},{80,96},{96,112},{112,128},... | collective-permute-start | bytes 196616 | tf_op jit(solution)/shard_map/ppermute | solution.py:20
  46.8 6.4 %collective-permute-start.5 = (f32[128,128]{1,0:T(8,128)S(1)}, f32[128,128]{1,0:T(8,128)S(1)}, u32[]{:S(2)}, u32[]{:S(2)}) collective-permute-start(f32[128,128]{1,0:T(8,128)S(1)} %get-tuple-element.48), channel_id=1, source_target_pairs={{16,0},{32,16},{48,32},{64,48},{80,64},{96,80},{112,96},{128,112},... | collective-permute-start | bytes 196616 | tf_op jit(solution)/shard_map/ppermute | solution.py:20
  53.2 1.9 %collective-permute-start.6 = (f32[128,128]{1,0:T(8,128)S(1)}, f32[128,128]{1,0:T(8,128)S(1)}, u32[]{:S(2)}, u32[]{:S(2)}) collective-permute-start(f32[128,128]{1,0:T(8,128)S(1)} %get-tuple-element.47), channel_id=1, source_target_pairs={{0,1},{1,2},{2,3},{3,4},{4,5},{5,6},{6,7},{7,8},{8,9},{9,10},{10,1... | collective-permute-start | bytes 196616 | tf_op jit(solution)/shard_map/ppermute | solution.py:20
  55.1 3.8 %collective-permute-start.7 = (f32[128,128]{1,0:T(8,128)S(1)}, f32[128,128]{1,0:T(8,128)S(1)}, u32[]{:S(2)}, u32[]{:S(2)}) collective-permute-start(f32[128,128]{1,0:T(8,128)S(1)} %get-tuple-element.46), channel_id=1, source_target_pairs={{1,0},{2,1},{3,2},{4,3},{5,4},{6,5},{7,6},{8,7},{9,8},{10,9},{11,1... | collective-permute-start | bytes 196616 | tf_op jit(solution)/shard_map/ppermute | solution.py:20
  58.9 0.0 collective-permute-done.4
  58.9 0.1 collective-permute-done.5
  59.0 0.4 collective-permute-done.6
  59.4 5.7 %collective-permute-done.7 = f32[128,128]{1,0:T(8,128)S(1)} collective-permute-done((f32[128,128]{1,0:T(8,128)S(1)}, f32[128,128]{1,0:T(8,128)S(1)}, u32[]{:S(2)}, u32[]{:S(2)}) %collective-permute-start.7) | collective-permute-done | bytes 65568 | tf_op jit(solution)/shard_map/ppermute | solution.py:20
  65.2 0.1 fusion.59
  65.2 2.1 %fusion.65 = (f32[768,128]{1,0:T(8,128)S(1)}, f32[768,128]{1,0:T(8,128)S(1)}) fusion(f32[768,128]{1,0:T(8,128)S(1)} %get-tuple-element.54, f32[768,128]{1,0:T(8,128)S(1)} %fusion.59, f32[768,768]{1,0:T(8,128)S(1)} %fusion.46, f32[1,1,768,128]{3,2,1,0:T(8,128)S(1)} %copy-done, f32[768,128]{1,0:T(8,128)S(1)} %get-tuple-element.55), kind=kOutput, calls=%fused_computation.87 | convolution fusion | flops 906559488 | bytes 4718592 | tf_op jit(solution)/shard_map/dot_general | solution.py:33
  67.3 3.3 %collective-permute-start.8 = (f32[128,128]{1,0:T(8,128)S(1)}, f32[128,128]{1,0:T(8,128)S(1)}, u32[]{:S(2)}, u32[]{:S(2)}) collective-permute-start(f32[128,128]{1,0:T(8,128)S(1)} %get-tuple-element.45), channel_id=1, source_target_pairs={{0,16},{16,32},{32,48},{48,64},{64,80},{80,96},{96,112},{112,128},... | collective-permute-start | bytes 196616 | tf_op jit(solution)/shard_map/ppermute | solution.py:20
  70.6 5.0 %collective-permute-start.9 = (f32[128,128]{1,0:T(8,128)S(1)}, f32[128,128]{1,0:T(8,128)S(1)}, u32[]{:S(2)}, u32[]{:S(2)}) collective-permute-start(f32[128,128]{1,0:T(8,128)S(1)} %get-tuple-element.44), channel_id=1, source_target_pairs={{16,0},{32,16},{48,32},{64,48},{80,64},{96,80},{112,96},{128,112},... | collective-permute-start | bytes 196616 | tf_op jit(solution)/shard_map/ppermute | solution.py:20
  75.6 4.8 %collective-permute-start.10 = (f32[128,128]{1,0:T(8,128)S(1)}, f32[128,128]{1,0:T(8,128)S(1)}, u32[]{:S(2)}, u32[]{:S(2)}) collective-permute-start(f32[128,128]{1,0:T(8,128)S(1)} %get-tuple-element.43), channel_id=1, source_target_pairs={{0,1},{1,2},{2,3},{3,4},{4,5},{5,6},{6,7},{7,8},{8,9},{9,10},{10,1... | collective-permute-start | bytes 196616 | tf_op jit(solution)/shard_map/ppermute | solution.py:20
  80.5 1.9 %collective-permute-start.11 = (f32[128,128]{1,0:T(8,128)S(1)}, f32[128,128]{1,0:T(8,128)S(1)}, u32[]{:S(2)}, u32[]{:S(2)}) collective-permute-start(f32[128,128]{1,0:T(8,128)S(1)} %get-tuple-element.42), channel_id=1, source_target_pairs={{1,0},{2,1},{3,2},{4,3},{5,4},{6,5},{7,6},{8,7},{9,8},{10,9},{11,1... | collective-permute-start | bytes 196616 | tf_op jit(solution)/shard_map/ppermute | solution.py:20
  82.4 0.0 collective-permute-done.8
  82.4 0.0 collective-permute-done.9
  82.4 0.0 collective-permute-done.10
  82.5 3.0 %collective-permute-done.11 = f32[128,128]{1,0:T(8,128)S(1)} collective-permute-done((f32[128,128]{1,0:T(8,128)S(1)}, f32[128,128]{1,0:T(8,128)S(1)}, u32[]{:S(2)}, u32[]{:S(2)}) %collective-permute-start.11) | collective-permute-done | bytes 65568 | tf_op jit(solution)/shard_map/ppermute | solution.py:20
  85.5 0.1 fusion.58
  85.6 2.1 %fusion.54 = f32[768,128]{1,0:T(8,128)S(1)} fusion(f32[768,128]{1,0:T(8,128)S(1)} %get-tuple-element.56, f32[768,128]{1,0:T(8,128)S(1)} %fusion.58, f32[768,768]{1,0:T(8,128)S(1)} %fusion.46, f32[1,1,768,128]{3,2,1,0:T(8,128)S(1)} %copy-done, f32[768,128]{1,0:T(8,128)S(1)} %get-tuple-element.57), kind=kOutput, calls=%fused_computation.47 | convolution fusion | flops 906559488 | bytes 4325376 | tf_op jit(solution)/shard_map/dot_general | solution.py:33
  87.6 0.0 copy-start.1
  87.7 1.9 %collective-permute-start.12 = (f32[128,128]{1,0:T(8,128)S(1)}, f32[128,128]{1,0:T(8,128)S(1)}, u32[]{:S(2)}, u32[]{:S(2)}) collective-permute-start(f32[128,128]{1,0:T(8,128)S(1)} %get-tuple-element.41), channel_id=1, source_target_pairs={{0,16},{16,32},{32,48},{48,64},{64,80},{80,96},{96,112},{112,128},... | collective-permute-start | bytes 196616 | tf_op jit(solution)/shard_map/ppermute | solution.py:20
  89.6 6.4 %collective-permute-start.13 = (f32[128,128]{1,0:T(8,128)S(1)}, f32[128,128]{1,0:T(8,128)S(1)}, u32[]{:S(2)}, u32[]{:S(2)}) collective-permute-start(f32[128,128]{1,0:T(8,128)S(1)} %get-tuple-element.40), channel_id=1, source_target_pairs={{16,0},{32,16},{48,32},{64,48},{80,64},{96,80},{112,96},{128,112},... | collective-permute-start | bytes 196616 | tf_op jit(solution)/shard_map/ppermute | solution.py:20
  96.0 4.3 %collective-permute-start.14 = (f32[128,128]{1,0:T(8,128)S(1)}, f32[128,128]{1,0:T(8,128)S(1)}, u32[]{:S(2)}, u32[]{:S(2)}) collective-permute-start(f32[128,128]{1,0:T(8,128)S(1)} %get-tuple-element.39), channel_id=1, source_target_pairs={{0,1},{1,2},{2,3},{3,4},{4,5},{5,6},{6,7},{7,8},{8,9},{9,10},{10,1... | collective-permute-start | bytes 196616 | tf_op jit(solution)/shard_map/ppermute | solution.py:20
  100.2 1.9 %collective-permute-start.15 = (f32[128,128]{1,0:T(8,128)S(1)}, f32[128,128]{1,0:T(8,128)S(1)}, u32[]{:S(2)}, u32[]{:S(2)}) collective-permute-start(f32[128,128]{1,0:T(8,128)S(1)} %get-tuple-element.38), channel_id=1, source_target_pairs={{1,0},{2,1},{3,2},{4,3},{5,4},{6,5},{7,6},{8,7},{9,8},{10,9},{11,1... | collective-permute-start | bytes 196616 | tf_op jit(solution)/shard_map/ppermute | solution.py:20
  102.2 0.0 collective-permute-done.12
  102.2 0.0 collective-permute-done.13
  102.2 0.0 collective-permute-done.14
  102.2 3.9 %collective-permute-done.15 = f32[128,128]{1,0:T(8,128)S(1)} collective-permute-done((f32[128,128]{1,0:T(8,128)S(1)}, f32[128,128]{1,0:T(8,128)S(1)}, u32[]{:S(2)}, u32[]{:S(2)}) %collective-permute-start.15) | collective-permute-done | bytes 65568 | tf_op jit(solution)/shard_map/ppermute | solution.py:20
  106.2 0.1 fusion.57
  106.2 2.8 %fusion.56 = f32[1,1,768,128]{3,2,1,0:T(8,128)} fusion(f32[768,128]{1,0:T(8,128)S(1)} %fusion.57, f32[768,768]{1,0:T(8,128)S(1)} %fusion.46, f32[768,128]{1,0:T(8,128)S(1)} %fusion.54, f32[1,1,768,128]{3,2,1,0:T(8,128)S(1)} %copy-done), kind=kOutput, calls=%fused_computation.49 | convolution fusion | flops 906166272 | bytes 3932160 | tf_op jit(solution)/shard_map/dot_general | solution.py:33
  109.0 0.0 copy-done.1
  (20 shorter events, 0.2 us)
Async XLA Ops:
  2.3 37.0 %collective-permute-start = (f32[128,128]{1,0:T(8,128)}, f32[128,128]{1,0:T(8,128)}, u32[]{:S(2)}, u32[]{:S(2)}) collective-permute-start(f32[128,128]{1,0:T(8,128)} %get-tuple-element.52), channel_id=1, source_target_pairs={{0,16},{16,32},{32,48},{48,64},{64,80},{80,96},{96,112},{112,128},... | collective-permute-start | bytes 196616 | tf_op jit(solution)/shard_map/ppermute | solution.py:20
  7.1 33.0 %collective-permute-start.1 = (f32[128,128]{1,0:T(8,128)}, f32[128,128]{1,0:T(8,128)}, u32[]{:S(2)}, u32[]{:S(2)}) collective-permute-start(f32[128,128]{1,0:T(8,128)} %get-tuple-element.51), channel_id=1, source_target_pairs={{16,0},{32,16},{48,32},{64,48},{80,64},{96,80},{112,96},{128,112},... | collective-permute-start | bytes 196616 | tf_op jit(solution)/shard_map/ppermute | solution.py:20
  12.3 28.7 %collective-permute-start.2 = (f32[128,128]{1,0:T(8,128)}, f32[128,128]{1,0:T(8,128)}, u32[]{:S(2)}, u32[]{:S(2)}) collective-permute-start(f32[128,128]{1,0:T(8,128)} %get-tuple-element.53), channel_id=1, source_target_pairs={{0,1},{1,2},{2,3},{3,4},{4,5},{5,6},{6,7},{7,8},{8,9},{9,10},{10,1... | collective-permute-start | bytes 196616 | tf_op jit(solution)/shard_map/ppermute | solution.py:20
  14.9 26.9 %collective-permute-start.3 = (f32[128,128]{1,0:T(8,128)}, f32[128,128]{1,0:T(8,128)}, u32[]{:S(2)}, u32[]{:S(2)}) collective-permute-start(f32[128,128]{1,0:T(8,128)} %get-tuple-element.50), channel_id=1, source_target_pairs={{1,0},{2,1},{3,2},{4,3},{5,4},{6,5},{7,6},{8,7},{9,8},{10,9},{11,1... | collective-permute-start | bytes 196616 | tf_op jit(solution)/shard_map/ppermute | solution.py:20
  33.7 1.7 %copy-start.3 = (bf16[1,1,768,768]{3,2,1,0:T(8,128)(2,1)S(1)}, bf16[1,1,768,768]{3,2,1,0:T(8,128)(2,1)}, u32[]{:S(2)}) copy-start(bf16[1,1,768,768]{3,2,1,0:T(8,128)(2,1)} %param.16) | copy-start | bytes 3538948
  35.5 7.2 %copy-start.2 = (f32[1,1,768,128]{3,2,1,0:T(8,128)S(1)}, f32[1,1,768,128]{3,2,1,0:T(8,128)}, u32[]{:S(2)}) copy-start(f32[1,1,768,128]{3,2,1,0:T(8,128)} %param.18) | copy-start | bytes 1179652
  35.5 7.3 %copy-start = (f32[1,1,768,128]{3,2,1,0:T(8,128)S(1)}, f32[1,1,768,128]{3,2,1,0:T(8,128)}, u32[]{:S(2)}) copy-start(f32[1,1,768,128]{3,2,1,0:T(8,128)} %param.19) | copy-start | bytes 1179652
  44.8 14.1 %collective-permute-start.4 = (f32[128,128]{1,0:T(8,128)S(1)}, f32[128,128]{1,0:T(8,128)S(1)}, u32[]{:S(2)}, u32[]{:S(2)}) collective-permute-start(f32[128,128]{1,0:T(8,128)S(1)} %get-tuple-element.49), channel_id=1, source_target_pairs={{0,16},{16,32},{32,48},{48,64},{64,80},{80,96},{96,112},{112,128},... | collective-permute-start | bytes 196616 | tf_op jit(solution)/shard_map/ppermute | solution.py:20
  46.8 12.3 %collective-permute-start.5 = (f32[128,128]{1,0:T(8,128)S(1)}, f32[128,128]{1,0:T(8,128)S(1)}, u32[]{:S(2)}, u32[]{:S(2)}) collective-permute-start(f32[128,128]{1,0:T(8,128)S(1)} %get-tuple-element.48), channel_id=1, source_target_pairs={{16,0},{32,16},{48,32},{64,48},{80,64},{96,80},{112,96},{128,112},... | collective-permute-start | bytes 196616 | tf_op jit(solution)/shard_map/ppermute | solution.py:20
  53.2 6.3 %collective-permute-start.6 = (f32[128,128]{1,0:T(8,128)S(1)}, f32[128,128]{1,0:T(8,128)S(1)}, u32[]{:S(2)}, u32[]{:S(2)}) collective-permute-start(f32[128,128]{1,0:T(8,128)S(1)} %get-tuple-element.47), channel_id=1, source_target_pairs={{0,1},{1,2},{2,3},{3,4},{4,5},{5,6},{6,7},{7,8},{8,9},{9,10},{10,1... | collective-permute-start | bytes 196616 | tf_op jit(solution)/shard_map/ppermute | solution.py:20
  55.1 10.1 %collective-permute-start.7 = (f32[128,128]{1,0:T(8,128)S(1)}, f32[128,128]{1,0:T(8,128)S(1)}, u32[]{:S(2)}, u32[]{:S(2)}) collective-permute-start(f32[128,128]{1,0:T(8,128)S(1)} %get-tuple-element.46), channel_id=1, source_target_pairs={{1,0},{2,1},{3,2},{4,3},{5,4},{6,5},{7,6},{8,7},{9,8},{10,9},{11,1... | collective-permute-start | bytes 196616 | tf_op jit(solution)/shard_map/ppermute | solution.py:20
  67.3 15.1 %collective-permute-start.8 = (f32[128,128]{1,0:T(8,128)S(1)}, f32[128,128]{1,0:T(8,128)S(1)}, u32[]{:S(2)}, u32[]{:S(2)}) collective-permute-start(f32[128,128]{1,0:T(8,128)S(1)} %get-tuple-element.45), channel_id=1, source_target_pairs={{0,16},{16,32},{32,48},{48,64},{64,80},{80,96},{96,112},{112,128},... | collective-permute-start | bytes 196616 | tf_op jit(solution)/shard_map/ppermute | solution.py:20
  70.6 11.8 %collective-permute-start.9 = (f32[128,128]{1,0:T(8,128)S(1)}, f32[128,128]{1,0:T(8,128)S(1)}, u32[]{:S(2)}, u32[]{:S(2)}) collective-permute-start(f32[128,128]{1,0:T(8,128)S(1)} %get-tuple-element.44), channel_id=1, source_target_pairs={{16,0},{32,16},{48,32},{64,48},{80,64},{96,80},{112,96},{128,112},... | collective-permute-start | bytes 196616 | tf_op jit(solution)/shard_map/ppermute | solution.py:20
  75.6 6.8 %collective-permute-start.10 = (f32[128,128]{1,0:T(8,128)S(1)}, f32[128,128]{1,0:T(8,128)S(1)}, u32[]{:S(2)}, u32[]{:S(2)}) collective-permute-start(f32[128,128]{1,0:T(8,128)S(1)} %get-tuple-element.43), channel_id=1, source_target_pairs={{0,1},{1,2},{2,3},{3,4},{4,5},{5,6},{6,7},{7,8},{8,9},{9,10},{10,1... | collective-permute-start | bytes 196616 | tf_op jit(solution)/shard_map/ppermute | solution.py:20
  80.5 5.0 %collective-permute-start.11 = (f32[128,128]{1,0:T(8,128)S(1)}, f32[128,128]{1,0:T(8,128)S(1)}, u32[]{:S(2)}, u32[]{:S(2)}) collective-permute-start(f32[128,128]{1,0:T(8,128)S(1)} %get-tuple-element.42), channel_id=1, source_target_pairs={{1,0},{2,1},{3,2},{4,3},{5,4},{6,5},{7,6},{8,7},{9,8},{10,9},{11,1... | collective-permute-start | bytes 196616 | tf_op jit(solution)/shard_map/ppermute | solution.py:20
  87.6 21.4 %copy-start.1 = (f32[768,128]{1,0:T(8,128)}, f32[768,128]{1,0:T(8,128)S(1)}, u32[]{:S(2)}) copy-start(f32[768,128]{1,0:T(8,128)S(1)} %fusion.54) | copy-start | bytes 1179652
  87.7 14.5 %collective-permute-start.12 = (f32[128,128]{1,0:T(8,128)S(1)}, f32[128,128]{1,0:T(8,128)S(1)}, u32[]{:S(2)}, u32[]{:S(2)}) collective-permute-start(f32[128,128]{1,0:T(8,128)S(1)} %get-tuple-element.41), channel_id=1, source_target_pairs={{0,16},{16,32},{32,48},{48,64},{64,80},{80,96},{96,112},{112,128},... | collective-permute-start | bytes 196616 | tf_op jit(solution)/shard_map/ppermute | solution.py:20
  89.6 12.6 %collective-permute-start.13 = (f32[128,128]{1,0:T(8,128)S(1)}, f32[128,128]{1,0:T(8,128)S(1)}, u32[]{:S(2)}, u32[]{:S(2)}) collective-permute-start(f32[128,128]{1,0:T(8,128)S(1)} %get-tuple-element.40), channel_id=1, source_target_pairs={{16,0},{32,16},{48,32},{64,48},{80,64},{96,80},{112,96},{128,112},... | collective-permute-start | bytes 196616 | tf_op jit(solution)/shard_map/ppermute | solution.py:20
  96.0 6.3 %collective-permute-start.14 = (f32[128,128]{1,0:T(8,128)S(1)}, f32[128,128]{1,0:T(8,128)S(1)}, u32[]{:S(2)}, u32[]{:S(2)}) collective-permute-start(f32[128,128]{1,0:T(8,128)S(1)} %get-tuple-element.39), channel_id=1, source_target_pairs={{0,1},{1,2},{2,3},{3,4},{4,5},{5,6},{6,7},{7,8},{8,9},{9,10},{10,1... | collective-permute-start | bytes 196616 | tf_op jit(solution)/shard_map/ppermute | solution.py:20
  100.2 5.9 %collective-permute-start.15 = (f32[128,128]{1,0:T(8,128)S(1)}, f32[128,128]{1,0:T(8,128)S(1)}, u32[]{:S(2)}, u32[]{:S(2)}) collective-permute-start(f32[128,128]{1,0:T(8,128)S(1)} %get-tuple-element.38), channel_id=1, source_target_pairs={{1,0},{2,1},{3,2},{4,3},{5,4},{6,5},{7,6},{8,7},{9,8},{10,9},{11,1... | collective-permute-start | bytes 196616 | tf_op jit(solution)/shard_map/ppermute | solution.py:20
where the time goes:
time: 110 us; the launch traced here: 109 us
  starting transfers between devices  59.1 us (54%)
  matrix products  24.1 us (22%)
  waiting for transfers between devices  13.1 us (12%)
  local copies, waits for them, and re-layouts  6.91 us (6%)
  other arithmetic  4.04 us (4%)
  between operations  1.64 us (1%)
    ppermute x16, starting transfers between devices, from_behind(): return lax.ppermute(block, axis, route)  59.1 us
    dot_general x3, matrix products, schur_block(): jnp.dot(product, coupling_block.T, preferred_element_type=jnp.float32)  15.2 us
    ppermute x16, waiting for transfers between devices, from_behind(): return lax.ppermute(block, axis, route)  13.1 us
    dot_general x4, matrix products, apply_operator(): jnp.dot(condensed, traces, precision=lax.Precision.HIGHEST, preferred_ele...  8.94 us
    sub x1, other arithmetic, on_device(): condensed = condensed - term  3.82 us
    unnamed x24, local copies, waits for them, and re-layouts  3.58 us
  transfers between devices with their start and end apart: 16, of which 5 were waited for; matrix products, arithmetic and copies ran while one was open for 21% of the time, Pallas kernels for 0%

commit v1 on v0

v1 whole, which is shorter than its diff:
```python
import jax
import jax.numpy as jnp
from jax import lax
from jax.experimental import pallas as pl
from jax.experimental.pallas import tpu as pltpu
from jax.sharding import PartitionSpec as P

SWEEPS = 3
TILE = 256
FACE = 128

lower_bound = 1.0
upper_bound = 14.0
centre = (upper_bound + lower_bound) / 2.0
half = (upper_bound - lower_bound) / 2.0
sigma = centre / half
rho0 = 1.0 / sigma
rho1 = 1.0 / (2.0 * sigma - rho0)
rho2 = 1.0 / (2.0 * sigma - rho1)
keep = (rho1 * rho0, rho2 * rho1)
gain = (2.0 * rho1 / half, 2.0 * rho2 / half)

f32, bf16 = jnp.float32, jnp.bfloat16
VMEM_LIMIT = 48 << 20


def split(value):
    high = value.astype(bf16)
    return high, (value - high.astype(f32)).astype(bf16)


def times(high_ref, low_ref, traces):
    high, low = split(traces)
    both = jnp.concatenate([high, low], axis=1)
    out = jnp.dot(high_ref[...], both, preferred_element_type=f32)
    out = out + jnp.dot(low_ref[...], both, preferred_element_type=f32)
    return out[:, : traces.shape[1]] + out[:, traces.shape[1] :]


def condense_kernel(
    info, coupling, inverse, stiffness, start, loads, high, low, rest, msg_a, msg_b, msg_c, msg_d,
    c_buf, i_buf, p_buf, acc, sems,
):
    blocks = info[0]
    slots, width, _ = coupling.shape
    tiles = width // TILE

    def fetch(slot):
        return (
            pltpu.make_async_copy(inverse.at[slot], i_buf.at[slot], sems.at[0, slot]),
            pltpu.make_async_copy(coupling.at[slot], c_buf.at[slot], sems.at[1, slot]),
        )

    for slot in range(slots):
        @pl.when(slot < blocks)
        def _():
            for copy in fetch(slot):
                copy.start()

    for i in range(tiles):
        rows = slice(i * TILE, (i + 1) * TILE)
        acc[rows, i * TILE :] = stiffness[rows, i * TILE :].astype(f32)

    def one_slot(slot, carry):
        for copy in fetch(slot):
            copy.wait()
        c_ref, i_ref = c_buf.at[slot], i_buf.at[slot]
        for i in range(tiles):
            rows = slice(i * TILE, (i + 1) * TILE)
            p_buf[rows] = jnp.dot(c_ref[rows], i_ref[...], preferred_element_type=f32).astype(bf16)
            term = lax.dot_general(
                p_buf[rows], c_ref[i * TILE :], (((1,), (1,)), ((), ())), preferred_element_type=f32
            )
            acc[rows, i * TILE :] = acc[rows, i * TILE :] - term
        return carry

    lax.fori_loop(0, blocks, one_slot, 0)

    for i in range(tiles):
        rows = slice(i * TILE, (i + 1) * TILE)
        for j in range(i, tiles):
            cols = slice(j * TILE, (j + 1) * TILE)
            block = acc[rows, cols]
            upper_high, upper_low = split(block)
            high[rows, cols] = upper_high
            low[rows, cols] = upper_low
            if j > i:
                mirror_high, mirror_low = split(block.T)
                high[cols, rows] = mirror_high
                low[cols, rows] = mirror_low

    x0 = start[...]
    y0 = loads[...] - times(high, low, x0) - 2.0 * x0
    rest[...] = y0
    for k, msg in enumerate((msg_a, msg_b, msg_c, msg_d)):
        face = pl.ds(pl.multiple_of(info[1 + k] * FACE, FACE), FACE)
        msg[:FACE] = start[face]
        msg[FACE:] = start[face] + rest[face] * (1.0 / centre)


def sweep_kernel(
    info, high, low, start, loads, rest, got_a, got_b, got_c, got_d,
    ahead, fix2, fix3, msg_a, msg_b, msg_c, msg_d, v0, v1, x1, x2, x2p,
):
    v0[...] = jnp.zeros_like(v0)
    v1[...] = jnp.zeros_like(v1)
    faces = [pl.ds(pl.multiple_of(info[1 + k] * FACE, FACE), FACE) for k in range(4)]
    alive = [info[5 + k].astype(f32) for k in range(4)]
    for k, got in enumerate((got_a, got_b, got_c, got_d)):
        v0[faces[k]] = got[:FACE]
        v1[faces[k]] = got[FACE:] + (alive[k] * (2.0 / centre)) * start[faces[k]]
    d0 = (rest[...] + 2.0 * v0[...]) * (1.0 / centre)
    x1[...] = start[...] + d0
    y1 = loads[...] - times(high, low, x1[...]) - 2.0 * x1[...]
    x2p[...] = x1[...] + keep[0] * d0 + gain[0] * y1
    x2[...] = x2p[...] + (2.0 * gain[0]) * v1[...]
    y2 = loads[...] - times(high, low, x2[...]) - 2.0 * x2[...]
    ahead[...] = x2[...] + keep[1] * (x2[...] - x1[...]) + gain[1] * y2
    for k, msg in enumerate((msg_a, msg_b, msg_c, msg_d)):
        msg[:FACE] = x2p[faces[k]]
        msg[FACE:] = ahead[faces[k]]
        fix2[faces[k]] = (alive[k] * 2.0 * gain[0]) * x1[faces[k]]
        fix3[faces[k]] = (alive[k] * 2.0 * gain[1]) * x2[faces[k]]


def final_kernel(
    info, high, low, loads, ahead, fix2, fix3, got_a, got_b, got_c, got_d, traces, residual
):
    traces[...] = ahead[...]
    faces = [pl.ds(pl.multiple_of(info[1 + k] * FACE, FACE), FACE) for k in range(4)]
    for k, got in enumerate((got_a, got_b, got_c, got_d)):
        traces[faces[k]] = ahead[faces[k]] + (2.0 * gain[1]) * (got[:FACE] + fix2[faces[k]])
    x3 = traces[...]
    residual[...] = loads[...] - times(high, low, x3) - 2.0 * x3
    for k, got in enumerate((got_a, got_b, got_c, got_d)):
        residual[faces[k]] = residual[faces[k]] + 2.0 * (got[FACE:] + fix3[faces[k]])


def swap(block, axes, first, extent):
    route = []
    for i in range(first, extent - 1, 2):
        route += [(i, i + 1), (i + 1, i)]
    return lax.ppermute(block, axes, route)


def exchange(messages, rows, columns):
    msg_a, msg_b, msg_c, msg_d = messages
    return (
        swap(msg_a, "gx", 1, rows),
        swap(msg_b, "gx", 0, rows),
        swap(msg_c, ("gy", "ha"), 0, columns),
        swap(msg_d, ("gy", "ha"), 1, columns),
    )


def on_device(coupling, inverse, stiffness, block_counts, initial_traces, trace_loads):
    rows = lax.axis_size("gx")
    columns = lax.axis_size(("gy", "ha"))
    row = lax.axis_index("gx")
    column = lax.axis_index(("gy", "ha"))
    odd_row, odd_col = row % 2, column % 2
    info = jnp.stack(
        [
            block_counts[0, 0],
            odd_row,
            1 - odd_row,
            3 - odd_col,
            2 + odd_col,
            jnp.where(odd_row == 1, row + 1 < rows, row > 0).astype(jnp.int32),
            jnp.where(odd_row == 1, 1, row + 1 < rows).astype(jnp.int32),
            jnp.where(odd_col == 1, 1, column + 1 < columns).astype(jnp.int32),
            jnp.where(odd_col == 1, column + 1 < columns, column > 0).astype(jnp.int32),
        ]
    ).astype(jnp.int32)
    coupling, inverse, stiffness = coupling[0, 0], inverse[0, 0], stiffness[0, 0]
    start, loads = initial_traces[0, 0], trace_loads[0, 0]
    slots, width, _ = coupling.shape
    lanes = start.shape[1]
    smem = pl.BlockSpec(memory_space=pltpu.SMEM)
    vmem = pl.BlockSpec(memory_space=pltpu.VMEM)
    anywhere = pl.BlockSpec(memory_space=pl.ANY)
    square = jax.ShapeDtypeStruct((width, width), bf16)
    field = jax.ShapeDtypeStruct((width, lanes), f32)
    faces = jax.ShapeDtypeStruct((4 * FACE, lanes), f32)
    message = jax.ShapeDtypeStruct((2 * FACE, lanes), f32)
    params = pltpu.CompilerParams(vmem_limit_bytes=VMEM_LIMIT)

    high, low, rest, *out = pl.pallas_call(
        condense_kernel,
        out_shape=(square, square, field, message, message, message, message),
        in_specs=[smem, anywhere, anywhere, vmem, vmem, vmem],
        out_specs=(vmem,) * 7,
        scratch_shapes=[
            pltpu.VMEM((slots, width, width), bf16),
            pltpu.VMEM((slots, width, width), bf16),
            pltpu.VMEM((width, width), bf16),
            pltpu.VMEM((width, width), f32),
            pltpu.SemaphoreType.DMA((2, slots)),
        ],
        compiler_params=params,
        name="condense",
    )(info, coupling, inverse, stiffness, start, loads)
    got = exchange(out, rows, columns)
    ahead, fix2, fix3, *out = pl.pallas_call(
        sweep_kernel,
        out_shape=(field, faces, faces, message, message, message, message),
        in_specs=[smem] + [vmem] * 9,
        out_specs=(vmem,) * 7,
        scratch_shapes=[pltpu.VMEM((width, lanes), f32)] * 5,
        compiler_params=params,
        name="sweep",
    )(info, high, low, start, loads, rest, *got)
    got = exchange(out, rows, columns)
    traces, residual = pl.pallas_call(
        final_kernel,
        out_shape=(field, field),
        in_specs=[smem] + [vmem] * 10,
        out_specs=(vmem,) * 2,
        compiler_params=params,
        name="final",
    )(info, high, low, loads, ahead, fix2, fix3, *got)
    return traces[None, None], residual[None, None]


def solution(mesh):
    cells = P("gx", ("gy", "ha"))
    return jax.shard_map(
        on_device, mesh=mesh, in_specs=(cells,) * 6, out_specs=(cells, cells), check_vma=False
    )
```

time: 110 us -> 56.7 us (0.52)
  the two profiles are of different devices: /device:TPU:27 before, /device:TPU:49 now
where the time goes in v1:
time: 56.7 us; the launch traced here: 56.2 us
  starting transfers between devices  26.1 us (46%)
  waiting for transfers between devices  15 us (26%)
  Pallas kernels  10.4 us (18%)
  local copies, waits for them, and re-layouts  3.35 us (6%)
  between operations  1.41 us (2%)
    ppermute x8, starting transfers between devices, swap(): return lax.ppermute(block, axes, route)  26.1 us
    ppermute x8, waiting for transfers between devices, swap(): return lax.ppermute(block, axes, route)  15 us
    pallas_call x1, Pallas kernels, on_device(): pl.pallas_call(condense_kernel, out_shape=(square, square, field, message...  4.92 us
    pallas_call x1, Pallas kernels, on_device(): pl.pallas_call(sweep_kernel, out_shape=(field, faces, faces, message, mes...  3.27 us
    unnamed x6, local copies, waits for them, and re-layouts  3.26 us
    pallas_call x1, Pallas kernels, on_device(): pl.pallas_call(final_kernel, out_shape=(field, field), in_specs=[smem] +...  2.17 us
  transfers between devices with their start and end apart: 8, of which 5 were waited for; matrix products, arithmetic and copies ran while one was open for 0% of the time, Pallas kernels for 0%

profile of v1, /device:TPU:49, one launch (start us, length us, event | category | flops | bytes accessed | tf_op | source)
XLA Modules:
  0.0 56.2 jit_solution(5384070031373134190)
XLA Ops:
  1.3 0.1 stack.43.info
  1.4 0.0 copy-start
  1.4 1.0 %copy-done = f32[1,1,768,128]{3,2,1,0:T(8,128)S(1)} copy-done((f32[1,1,768,128]{3,2,1,0:T(8,128)S(1)}, f32[1,1,768,128]{3,2,1,0:T(8,128)}, u32[]{:S(2)}) %copy-start) | copy-done | bytes 393240
  2.4 0.0 copy-start.1
  2.4 1.0 %copy-done.1 = f32[1,1,768,128]{3,2,1,0:T(8,128)S(1)} copy-done((f32[1,1,768,128]{3,2,1,0:T(8,128)S(1)}, f32[1,1,768,128]{3,2,1,0:T(8,128)}, u32[]{:S(2)}) %copy-start.1) | copy-done | bytes 393240
  3.4 0.0 copy-start.2
  3.4 1.3 %copy-done.2 = bf16[1,1,768,768]{3,2,1,0:T(8,128)(2,1)S(1)} copy-done((bf16[1,1,768,768]{3,2,1,0:T(8,128)(2,1)S(1)}, bf16[1,1,768,768]{3,2,1,0:T(8,128)(2,1)}, u32[]{:S(2)}) %copy-start.2) | copy-done | bytes 1179672
  4.7 4.9 %condense.1 = (bf16[768,768]{1,0:T(8,128)(2,1)S(1)}, bf16[768,768]{1,0:T(8,128)(2,1)S(1)}, f32[768,128]{1,0:T(8,128)S(1)}, f32[256,128]{1,0:T(8,128)S(1)}, f32[2...) custom-call(s32[9]{0:T(128)S(1)} %stack.43.info, bf16[4,768,768]{2,1,0:T(8,128)(2,1)} %bitcast.23, ...), custom_call_target="tpu_custom_call" | custom-call | tf_op jit(solution)/shard_map/condense/pallas_call | solution.py:188
  9.6 6.9 %collective-permute-start = (f32[256,128]{1,0:T(8,128)S(1)}, f32[256,128]{1,0:T(8,128)S(1)}, u32[]{:S(2)}, u32[]{:S(2)}) collective-permute-start(f32[256,128]{1,0:T(8,128)S(1)} %get-tuple-element.21), channel_id=1, source_target_pairs={{16,32},{32,16},{48,64},{64,48},{80,96},{96,80},{112,128},{128,112... | collective-permute-start | bytes 393224 | tf_op jit(solution)/shard_map/ppermute | solution.py:143
  16.5 3.2 %collective-permute-start.1 = (f32[256,128]{1,0:T(8,128)S(1)}, f32[256,128]{1,0:T(8,128)S(1)}, u32[]{:S(2)}, u32[]{:S(2)}) collective-permute-start(f32[256,128]{1,0:T(8,128)S(1)} %get-tuple-element.22), channel_id=1, source_target_pairs={{0,16},{16,0},{32,48},{48,32},{64,80},{80,64},{96,112},{112,96},{1... | collective-permute-start | bytes 393224 | tf_op jit(solution)/shard_map/ppermute | solution.py:143
  19.7 3.2 %collective-permute-start.2 = (f32[256,128]{1,0:T(8,128)S(1)}, f32[256,128]{1,0:T(8,128)S(1)}, u32[]{:S(2)}, u32[]{:S(2)}) collective-permute-start(f32[256,128]{1,0:T(8,128)S(1)} %get-tuple-element.23), channel_id=1, source_target_pairs={{0,1},{1,0},{2,3},{3,2},{4,5},{5,4},{6,7},{7,6},{8,9},{9,8},{10,11... | collective-permute-start | bytes 393224 | tf_op jit(solution)/shard_map/ppermute | solution.py:143
  22.9 5.1 %collective-permute-start.3 = (f32[256,128]{1,0:T(8,128)S(1)}, f32[256,128]{1,0:T(8,128)S(1)}, u32[]{:S(2)}, u32[]{:S(2)}) collective-permute-start(f32[256,128]{1,0:T(8,128)S(1)} %get-tuple-element.24), channel_id=1, source_target_pairs={{1,2},{2,1},{3,4},{4,3},{5,6},{6,5},{7,8},{8,7},{9,10},{10,9},{11,... | collective-permute-start | bytes 393224 | tf_op jit(solution)/shard_map/ppermute | solution.py:143
  28.1 0.0 collective-permute-done.got_a
  28.1 0.0 collective-permute-done.1.got_b
  28.1 0.0 collective-permute-done.2.got_c
  28.1 5.5 %collective-permute-done.3.got_d = f32[256,128]{1,0:T(8,128)S(1)} collective-permute-done((f32[256,128]{1,0:T(8,128)S(1)}, f32[256,128]{1,0:T(8,128)S(1)}, u32[]{:S(2)}, u32[]{:S(2)}) %collective-permute-start.3) | collective-permute-done | bytes 131104 | tf_op jit(solution)/shard_map/ppermute | solution.py:143
  33.6 3.3 %sweep.1 = (f32[768,128]{1,0:T(8,128)S(1)}, f32[512,128]{1,0:T(8,128)S(1)}, f32[512,128]{1,0:T(8,128)S(1)}, f32[256,128]{1,0:T(8,128)S(1)}, f32[256,128]{1,0:T(8...) custom-call(s32[9]{0:T(128)S(1)} %stack.43.info, bf16[768,768]{1,0:T(8,128)(2,1)S(1)} %get-tuple-element.18.high, ...), custom_call_target="tpu_custom_call" | custom-call | tf_op jit(solution)/shard_map/sweep/pallas_call | solution.py:204
  36.8 3.6 %collective-permute-start.4 = (f32[256,128]{1,0:T(8,128)S(1)}, f32[256,128]{1,0:T(8,128)S(1)}, u32[]{:S(2)}, u32[]{:S(2)}) collective-permute-start(f32[256,128]{1,0:T(8,128)S(1)} %get-tuple-element.28), channel_id=1, source_target_pairs={{16,32},{32,16},{48,64},{64,48},{80,96},{96,80},{112,128},{128,112... | collective-permute-start | bytes 393224 | tf_op jit(solution)/shard_map/ppermute | solution.py:143
  40.5 0.1 collective-permute-start.5
  40.6 0.1 collective-permute-start.6
  40.7 3.8 %collective-permute-start.7 = (f32[256,128]{1,0:T(8,128)S(1)}, f32[256,128]{1,0:T(8,128)S(1)}, u32[]{:S(2)}, u32[]{:S(2)}) collective-permute-start(f32[256,128]{1,0:T(8,128)S(1)} %get-tuple-element.31), channel_id=1, source_target_pairs={{1,2},{2,1},{3,4},{4,3},{5,6},{6,5},{7,8},{8,7},{9,10},{10,9},{11,... | collective-permute-start | bytes 393224 | tf_op jit(solution)/shard_map/ppermute | solution.py:143
  44.5 2.3 %collective-permute-done.4.got_a = f32[256,128]{1,0:T(8,128)S(1)} collective-permute-done((f32[256,128]{1,0:T(8,128)S(1)}, f32[256,128]{1,0:T(8,128)S(1)}, u32[]{:S(2)}, u32[]{:S(2)}) %collective-permute-start.4) | collective-permute-done | bytes 131104 | tf_op jit(solution)/shard_map/ppermute | solution.py:143
  46.8 0.8 %collective-permute-done.5.got_b = f32[256,128]{1,0:T(8,128)S(1)} collective-permute-done((f32[256,128]{1,0:T(8,128)S(1)}, f32[256,128]{1,0:T(8,128)S(1)}, u32[]{:S(2)}, u32[]{:S(2)}) %collective-permute-start.5) | collective-permute-done | bytes 131104 | tf_op jit(solution)/shard_map/ppermute | solution.py:143
  47.5 0.8 %collective-permute-done.6.got_c = f32[256,128]{1,0:T(8,128)S(1)} collective-permute-done((f32[256,128]{1,0:T(8,128)S(1)}, f32[256,128]{1,0:T(8,128)S(1)}, u32[]{:S(2)}, u32[]{:S(2)}) %collective-permute-start.6) | collective-permute-done | bytes 131104 | tf_op jit(solution)/shard_map/ppermute | solution.py:143
  48.3 5.7 %collective-permute-done.7.got_d = f32[256,128]{1,0:T(8,128)S(1)} collective-permute-done((f32[256,128]{1,0:T(8,128)S(1)}, f32[256,128]{1,0:T(8,128)S(1)}, u32[]{:S(2)}, u32[]{:S(2)}) %collective-permute-start.7) | collective-permute-done | bytes 131104 | tf_op jit(solution)/shard_map/ppermute | solution.py:143
  54.1 2.2 %final.1 = (f32[768,128]{1,0:T(8,128)}, f32[768,128]{1,0:T(8,128)}) custom-call(s32[9]{0:T(128)S(1)} %stack.43.info, bf16[768,768]{1,0:T(8,128)(2,1)S(1)} %get-tuple-element.18.high, bf16[768,768]{1,0:T(8,128)(2,1)S(1)} %get-tuple-element.19.low, f32[768,128]{1,0:T(8,128)S(1)} %bitcast.19, f32[768,128]{1,0:T(8,128)S(1)} %get-tuple-element.25.ahead, ...), custom_call_target="tpu_custom_call" | custom-call | tf_op jit(solution)/shard_map/final/pallas_call | solution.py:214
Async XLA Ops:
  1.4 1.0 %copy-start = (f32[1,1,768,128]{3,2,1,0:T(8,128)S(1)}, f32[1,1,768,128]{3,2,1,0:T(8,128)}, u32[]{:S(2)}) copy-start(f32[1,1,768,128]{3,2,1,0:T(8,128)} %param.11) | copy-start | bytes 1179652
  2.4 1.0 %copy-start.1 = (f32[1,1,768,128]{3,2,1,0:T(8,128)S(1)}, f32[1,1,768,128]{3,2,1,0:T(8,128)}, u32[]{:S(2)}) copy-start(f32[1,1,768,128]{3,2,1,0:T(8,128)} %param.10) | copy-start | bytes 1179652
  3.4 1.3 %copy-start.2 = (bf16[1,1,768,768]{3,2,1,0:T(8,128)(2,1)S(1)}, bf16[1,1,768,768]{3,2,1,0:T(8,128)(2,1)}, u32[]{:S(2)}) copy-start(bf16[1,1,768,768]{3,2,1,0:T(8,128)(2,1)} %param.8) | copy-start | bytes 3538948
  9.6 18.5 %collective-permute-start = (f32[256,128]{1,0:T(8,128)S(1)}, f32[256,128]{1,0:T(8,128)S(1)}, u32[]{:S(2)}, u32[]{:S(2)}) collective-permute-start(f32[256,128]{1,0:T(8,128)S(1)} %get-tuple-element.21), channel_id=1, source_target_pairs={{16,32},{32,16},{48,64},{64,48},{80,96},{96,80},{112,128},{128,112... | collective-permute-start | bytes 393224 | tf_op jit(solution)/shard_map/ppermute | solution.py:143
  16.5 11.6 %collective-permute-start.1 = (f32[256,128]{1,0:T(8,128)S(1)}, f32[256,128]{1,0:T(8,128)S(1)}, u32[]{:S(2)}, u32[]{:S(2)}) collective-permute-start(f32[256,128]{1,0:T(8,128)S(1)} %get-tuple-element.22), channel_id=1, source_target_pairs={{0,16},{16,0},{32,48},{48,32},{64,80},{80,64},{96,112},{112,96},{1... | collective-permute-start | bytes 393224 | tf_op jit(solution)/shard_map/ppermute | solution.py:143
  19.7 8.4 %collective-permute-start.2 = (f32[256,128]{1,0:T(8,128)S(1)}, f32[256,128]{1,0:T(8,128)S(1)}, u32[]{:S(2)}, u32[]{:S(2)}) collective-permute-start(f32[256,128]{1,0:T(8,128)S(1)} %get-tuple-element.23), channel_id=1, source_target_pairs={{0,1},{1,0},{2,3},{3,2},{4,5},{5,4},{6,7},{7,6},{8,9},{9,8},{10,11... | collective-permute-start | bytes 393224 | tf_op jit(solution)/shard_map/ppermute | solution.py:143
  22.9 10.6 %collective-permute-start.3 = (f32[256,128]{1,0:T(8,128)S(1)}, f32[256,128]{1,0:T(8,128)S(1)}, u32[]{:S(2)}, u32[]{:S(2)}) collective-permute-start(f32[256,128]{1,0:T(8,128)S(1)} %get-tuple-element.24), channel_id=1, source_target_pairs={{1,2},{2,1},{3,4},{4,3},{5,6},{6,5},{7,8},{8,7},{9,10},{10,9},{11,... | collective-permute-start | bytes 393224 | tf_op jit(solution)/shard_map/ppermute | solution.py:143
  36.8 9.9 %collective-permute-start.4 = (f32[256,128]{1,0:T(8,128)S(1)}, f32[256,128]{1,0:T(8,128)S(1)}, u32[]{:S(2)}, u32[]{:S(2)}) collective-permute-start(f32[256,128]{1,0:T(8,128)S(1)} %get-tuple-element.28), channel_id=1, source_target_pairs={{16,32},{32,16},{48,64},{64,48},{80,96},{96,80},{112,128},{128,112... | collective-permute-start | bytes 393224 | tf_op jit(solution)/shard_map/ppermute | solution.py:143
  40.5 7.1 %collective-permute-start.5 = (f32[256,128]{1,0:T(8,128)S(1)}, f32[256,128]{1,0:T(8,128)S(1)}, u32[]{:S(2)}, u32[]{:S(2)}) collective-permute-start(f32[256,128]{1,0:T(8,128)S(1)} %get-tuple-element.29), channel_id=1, source_target_pairs={{0,16},{16,0},{32,48},{48,32},{64,80},{80,64},{96,112},{112,96},{1... | collective-permute-start | bytes 393224 | tf_op jit(solution)/shard_map/ppermute | solution.py:143
  40.6 7.7 %collective-permute-start.6 = (f32[256,128]{1,0:T(8,128)S(1)}, f32[256,128]{1,0:T(8,128)S(1)}, u32[]{:S(2)}, u32[]{:S(2)}) collective-permute-start(f32[256,128]{1,0:T(8,128)S(1)} %get-tuple-element.30), channel_id=1, source_target_pairs={{0,1},{1,0},{2,3},{3,2},{4,5},{5,4},{6,7},{7,6},{8,9},{9,8},{10,11... | collective-permute-start | bytes 393224 | tf_op jit(solution)/shard_map/ppermute | solution.py:143
  40.7 13.4 %collective-permute-start.7 = (f32[256,128]{1,0:T(8,128)S(1)}, f32[256,128]{1,0:T(8,128)S(1)}, u32[]{:S(2)}, u32[]{:S(2)}) collective-permute-start(f32[256,128]{1,0:T(8,128)S(1)} %get-tuple-element.31), channel_id=1, source_target_pairs={{1,2},{2,1},{3,4},{4,3},{5,6},{6,5},{7,8},{8,7},{9,10},{10,9},{11,... | collective-permute-start | bytes 393224 | tf_op jit(solution)/shard_map/ppermute | solution.py:143

commit v2 on v1

v2 whole, which is shorter than its diff:
```python
import jax
import jax.numpy as jnp
from jax import lax
from jax.experimental import pallas as pl
from jax.experimental.pallas import tpu as pltpu
from jax.sharding import PartitionSpec as P

SWEEPS = 3
TILE = 256
FACE = 128
EXTRA = 16

lower_bound = 1.0
upper_bound = 14.0
centre = (upper_bound + lower_bound) / 2.0
half = (upper_bound - lower_bound) / 2.0
sigma = centre / half
rho0 = 1.0 / sigma
rho1 = 1.0 / (2.0 * sigma - rho0)
rho2 = 1.0 / (2.0 * sigma - rho1)
keep = (rho1 * rho0, rho2 * rho1)
gain = (2.0 * rho1 / half, 2.0 * rho2 / half)

f32, bf16 = jnp.float32, jnp.bfloat16
VMEM_LIMIT = 48 << 20


def split(value):
    high = value.astype(bf16)
    return high, (value - high.astype(f32)).astype(bf16)


def times(high_ref, low_ref, traces):
    high, low = split(traces)
    both = jnp.concatenate([high, low], axis=1)
    out = jnp.dot(high_ref[...], both, preferred_element_type=f32)
    out = out + jnp.dot(low_ref[...], both, preferred_element_type=f32)
    return out[:, : traces.shape[1]] + out[:, traces.shape[1] :]


def round_half(value):
    big = value * 8193.0
    return big - (big - value)


def exponent_of(top):
    return jnp.floor(jnp.log2(jnp.maximum(top, 1e-30)))


def largest(value):
    return jnp.max(jnp.abs(value), keepdims=True)


def condense_kernel(
    info, coupling, inverse, stiffness, start_in, loads_in,
    high, low, rest, start, loads, msg_a, msg_b, msg_c, msg_d,
    c_buf, i_buf, p_buf, b_buf, acc, sems, side_sems,
):
    blocks = info[0]
    slots, width, _ = coupling.shape
    tiles = width // TILE

    def fetch_inverse(slot):
        return pltpu.make_async_copy(inverse.at[slot], i_buf.at[slot], sems.at[slot, tiles])

    def fetch_rows(slot, i):
        rows = pl.ds(i * TILE, TILE)
        return pltpu.make_async_copy(
            coupling.at[slot, rows], c_buf.at[slot, rows], sems.at[slot, i]
        )

    side = (
        pltpu.make_async_copy(stiffness, b_buf, side_sems.at[0]),
        pltpu.make_async_copy(start_in, start, side_sems.at[1]),
        pltpu.make_async_copy(loads_in, loads, side_sems.at[2]),
    )
    for slot in range(slots):
        @pl.when(slot < blocks)
        def _():
            fetch_inverse(slot).start()
            for i in reversed(range(tiles)):
                fetch_rows(slot, i).start()
        if slot == 0:
            for copy in side:
                copy.start()

    for i in range(tiles):
        acc[i * TILE : (i + 1) * TILE, i * TILE :] = jnp.zeros((TILE, width - i * TILE), f32)

    def one_slot(slot, carry):
        c_ref, i_ref = c_buf.at[slot], i_buf.at[slot]
        fetch_inverse(slot).wait()
        for i in reversed(range(tiles)):
            fetch_rows(slot, i).wait()
            rows = slice(i * TILE, (i + 1) * TILE)
            p_buf[rows] = jnp.dot(c_ref[rows], i_ref[...], preferred_element_type=f32).astype(bf16)
            term = lax.dot_general(
                p_buf[rows], c_ref[i * TILE :], (((1,), (1,)), ((), ())), preferred_element_type=f32
            )
            acc[rows, i * TILE :] = acc[rows, i * TILE :] + term
        return carry

    lax.fori_loop(0, blocks, one_slot, 0)

    for copy in side:
        copy.wait()
    for i in range(tiles):
        rows = slice(i * TILE, (i + 1) * TILE)
        for j in range(i, tiles):
            cols = slice(j * TILE, (j + 1) * TILE)
            block = b_buf[rows, cols].astype(f32) - acc[rows, cols]
            upper_high, upper_low = split(block)
            high[rows, cols] = upper_high
            low[rows, cols] = upper_low
            if j > i:
                mirror_high, mirror_low = split(block.T)
                high[cols, rows] = mirror_high
                low[cols, rows] = mirror_low

    x0 = start[...]
    y0 = loads[...] - times(high, low, x0) - 2.0 * x0
    rest[...] = y0
    edge = x0[: 4 * FACE] - round_half(x0[: 4 * FACE]) + y0[: 4 * FACE] * (1.0 / centre)
    power = exponent_of(largest(edge))
    scale = jnp.exp2(13.0 - power)
    for k, msg in enumerate((msg_a, msg_b, msg_c, msg_d)):
        face = pl.ds(pl.multiple_of(info[1 + k] * FACE, FACE), FACE)
        first = round_half(start[face])
        msg[:FACE] = first
        msg[FACE : 2 * FACE] = round_half(
            (start[face] - first + rest[face] * (1.0 / centre)) * scale
        )
        msg[2 * FACE :] = jnp.broadcast_to(power, (EXTRA, FACE))


def sweep_kernel(
    info, high, low, start, loads, rest, sent_a, sent_b, sent_c, sent_d,
    got_a, got_b, got_c, got_d,
    ahead, fix2, fix3, msg_a, msg_b, msg_c, msg_d, v0, v1, own, x2p,
):
    v0[...] = jnp.zeros_like(v0)
    v1[...] = jnp.zeros_like(v1)
    faces = [pl.ds(pl.multiple_of(info[1 + k] * FACE, FACE), FACE) for k in range(4)]
    alive = [info[5 + k].astype(f32) for k in range(4)]
    for k, (sent, got) in enumerate(
        zip((sent_a, sent_b, sent_c, sent_d), (got_a, got_b, got_c, got_d))
    ):
        back = jnp.exp2(got[2 * FACE : 2 * FACE + 1] - 13.0)
        mine = jnp.exp2(sent[2 * FACE : 2 * FACE + 1] - 13.0)
        first = got[:FACE]
        v0[faces[k]] = first
        v1[faces[k]] = (
            first + got[FACE : 2 * FACE] * back + (alive[k] * (2.0 / centre)) * sent[:FACE]
        )
        own[faces[k]] = sent[:FACE] + sent[FACE : 2 * FACE] * mine + (2.0 / centre) * first
    d0 = (rest[...] + 2.0 * v0[...]) * (1.0 / centre)
    x1 = start[...] + d0
    y1 = loads[...] - times(high, low, x1) - 2.0 * x1
    x2p[...] = x1 + keep[0] * d0 + gain[0] * y1
    x2 = x2p[...] + (2.0 * gain[0]) * v1[...]
    y2 = loads[...] - times(high, low, x2) - 2.0 * x2
    x3p = x2 + keep[1] * (x2 - x1) + gain[1] * y2
    ahead[...] = x3p
    edges = 4 * FACE
    first = x2p[:edges] - own[...]
    second = x3p[:edges] - x2[:edges]
    power = exponent_of(jnp.maximum(largest(first), largest(second)))
    scale = jnp.exp2(12.0 - power)
    back = jnp.exp2(power - 12.0)
    for k, msg in enumerate((msg_a, msg_b, msg_c, msg_d)):
        face = faces[k]
        first = round_half((x2p[face] - own[face]) * scale)
        known = own[face] + first * back + (2.0 * gain[0]) * v1[face]
        msg[:FACE] = first
        msg[FACE : 2 * FACE] = round_half((ahead[face] - known) * scale)
        msg[2 * FACE :] = jnp.broadcast_to(power, (EXTRA, FACE))
        fix2[face] = v1[face] + (alive[k] * 2.0 * gain[0]) * own[face]
        fix3[face] = (alive[k] * 2.0 * gain[1]) * known


def final_kernel(
    info, high, low, loads, ahead, fix2, fix3, got_a, got_b, got_c, got_d, traces, residual, v3
):
    traces[...] = ahead[...]
    faces = [pl.ds(pl.multiple_of(info[1 + k] * FACE, FACE), FACE) for k in range(4)]
    for k, got in enumerate((got_a, got_b, got_c, got_d)):
        back = jnp.exp2(got[2 * FACE : 2 * FACE + 1] - 12.0)
        v2 = got[:FACE] * back + fix2[faces[k]]
        v3[faces[k]] = v2 + got[FACE : 2 * FACE] * back + fix3[faces[k]]
        traces[faces[k]] = ahead[faces[k]] + (2.0 * gain[1]) * v2
    x3 = traces[...]
    edges = 4 * FACE
    y3 = loads[...] - times(high, low, x3) - 2.0 * x3
    residual[:edges] = y3[:edges] + 2.0 * v3[...]
    residual[edges:] = y3[edges:]


def swap(block, axes, first, extent):
    route = []
    for i in range(first, extent - 1, 2):
        route += [(i, i + 1), (i + 1, i)]
    return lax.ppermute(block.astype(jnp.float16), axes, route).astype(f32)


def exchange(messages, rows, columns):
    msg_a, msg_b, msg_c, msg_d = messages
    return (
        swap(msg_a, ("gy", "ha"), 1, columns),
        swap(msg_b, ("gy", "ha"), 0, columns),
        swap(msg_c, "gx", 0, rows),
        swap(msg_d, "gx", 1, rows),
    )


def on_device(coupling, inverse, stiffness, block_counts, initial_traces, trace_loads):
    rows = lax.axis_size("gx")
    columns = lax.axis_size(("gy", "ha"))
    row = lax.axis_index("gx")
    column = lax.axis_index(("gy", "ha"))
    odd_row, odd_col = row % 2, column % 2
    info = jnp.stack(
        [
            block_counts[0, 0],
            2 + odd_col,
            3 - odd_col,
            1 - odd_row,
            odd_row,
            jnp.where(odd_col == 1, column + 1 < columns, column > 0).astype(jnp.int32),
            jnp.where(odd_col == 1, 1, column + 1 < columns).astype(jnp.int32),
            jnp.where(odd_row == 1, 1, row + 1 < rows).astype(jnp.int32),
            jnp.where(odd_row == 1, row + 1 < rows, row > 0).astype(jnp.int32),
        ]
    ).astype(jnp.int32)
    coupling, inverse, stiffness = coupling[0, 0], inverse[0, 0], stiffness[0, 0]
    start, loads = initial_traces[0, 0], trace_loads[0, 0]
    slots, width, _ = coupling.shape
    lanes = start.shape[1]
    smem = pl.BlockSpec(memory_space=pltpu.SMEM)
    vmem = pl.BlockSpec(memory_space=pltpu.VMEM)
    anywhere = pl.BlockSpec(memory_space=pltpu.HBM)
    square = jax.ShapeDtypeStruct((width, width), bf16)
    field = jax.ShapeDtypeStruct((width, lanes), f32)
    faces = jax.ShapeDtypeStruct((4 * FACE, lanes), f32)
    message = jax.ShapeDtypeStruct((2 * FACE + EXTRA, lanes), f32)
    params = pltpu.CompilerParams(vmem_limit_bytes=VMEM_LIMIT)

    high, low, rest, start, loads, *out = pl.pallas_call(
        condense_kernel,
        out_shape=(square, square, field, field, field, message, message, message, message),
        in_specs=[smem] + [anywhere] * 5,
        out_specs=(vmem,) * 9,
        scratch_shapes=[
            pltpu.VMEM((slots, width, width), bf16),
            pltpu.VMEM((slots, width, width), bf16),
            pltpu.VMEM((width, width), bf16),
            pltpu.VMEM((width, width), bf16),
            pltpu.VMEM((width, width), f32),
            pltpu.SemaphoreType.DMA((slots, width // TILE + 1)),
            pltpu.SemaphoreType.DMA((3,)),
        ],
        compiler_params=params,
        name="condense",
    )(info, coupling, inverse, *[pltpu.with_memory_space_constraint(v, pltpu.HBM) for v in (stiffness, start, loads)])
    got = exchange(out, rows, columns)
    ahead, fix2, fix3, *out = pl.pallas_call(
        sweep_kernel,
        out_shape=(field, faces, faces, message, message, message, message),
        in_specs=[smem] + [vmem] * 13,
        out_specs=(vmem,) * 7,
        scratch_shapes=[
            pltpu.VMEM((width, lanes), f32),
            pltpu.VMEM((width, lanes), f32),
            pltpu.VMEM((4 * FACE, lanes), f32),
            pltpu.VMEM((width, lanes), f32),
        ],
        compiler_params=params,
        name="sweep",
    )(info, high, low, start, loads, rest, *out, *got)
    got = exchange(out, rows, columns)
    traces, residual = pl.pallas_call(
        final_kernel,
        out_shape=(field, field),
        in_specs=[smem] + [vmem] * 10,
        out_specs=(vmem,) * 2,
        scratch_shapes=[pltpu.VMEM((4 * FACE, lanes), f32)],
        compiler_params=params,
        name="final",
    )(info, high, low, loads, ahead, fix2, fix3, *got)
    return traces[None, None], residual[None, None]


def solution(mesh):
    cells = P("gx", ("gy", "ha"))
    return jax.shard_map(
        on_device, mesh=mesh, in_specs=(cells,) * 6, out_specs=(cells, cells), check_vma=False
    )
```

time: 56.7 us -> 48.1 us (0.85)
  the two profiles are of different devices: /device:TPU:49 before, /device:TPU:30 now
where the time goes in v2:
time: 48.1 us; the launch traced here: 47.3 us
  starting transfers between devices  22.5 us (47%)
  Pallas kernels  13.6 us (28%)
  waiting for transfers between devices  9.44 us (20%)
  between operations  1.52 us (3%)
    ppermute x8, starting transfers between devices, swap(): return lax.ppermute(block.astype(jnp.float16), axes, route).astype(f32)  22.5 us
    ppermute x8, waiting for transfers between devices, swap(): return lax.ppermute(block.astype(jnp.float16), axes, route).astype(f32)  9.44 us
    pallas_call x1, Pallas kernels, on_device(): pl.pallas_call(condense_kernel, out_shape=(square, square, field, field,...  7.84 us
    pallas_call x1, Pallas kernels, on_device(): pl.pallas_call(sweep_kernel, out_shape=(field, faces, faces, message, mes...  3.54 us
    pallas_call x1, Pallas kernels, on_device(): pl.pallas_call(final_kernel, out_shape=(field, field), in_specs=[smem] +...  2.18 us
  transfers between devices with their start and end apart: 8, of which 3 were waited for; matrix products, arithmetic and copies ran while one was open for 0% of the time, Pallas kernels for 0%

profile of v2, /device:TPU:30, one launch (start us, length us, event | category | flops | bytes accessed | tf_op | source)
XLA Modules:
  0.0 47.3 jit_solution(11020985783901059952)
XLA Ops:
  1.3 0.1 stack.43.info
  1.4 7.8 %condense.1 = (bf16[768,768]{1,0:T(8,128)(2,1)S(1)}, bf16[768,768]{1,0:T(8,128)(2,1)S(1)}, f32[768,128]{1,0:T(8,128)S(1)}, f32[768,128]{1,0:T(8,128)S(1)}, f32[7...) custom-call(s32[9]{0:T(128)S(1)} %stack.43.info, ...), custom_call_target="tpu_custom_call" | custom-call | tf_op jit(solution)/shard_map/condense/pallas_call | solution.py:247
  9.3 8.4 %collective-permute-start.3 = (f16[272,128]{1,0:T(8,128)(2,1)S(1)}, f16[272,128]{1,0:T(8,128)(2,1)S(1)}, u32[]{:S(2)}, u32[]{:S(2)}) collective-permute-start(f16[272,128]{1,0:T(8,128)(2,1)S(1)} %convert_element_type.65), channel_id=1, source_target_pairs={{16,32},{32,16},{48,64},{64,48},{80,96},{96,80},{112,128},{128,112... | collective-permute-start | bytes 208904 | tf_op jit(solution)/shard_map/ppermute | solution.py:202
  17.7 0.1 collective-permute-start.2
  17.8 7.1 %collective-permute-start.1 = (f16[272,128]{1,0:T(8,128)(2,1)S(1)}, f16[272,128]{1,0:T(8,128)(2,1)S(1)}, u32[]{:S(2)}, u32[]{:S(2)}) collective-permute-start(f16[272,128]{1,0:T(8,128)(2,1)S(1)} %convert_element_type.61), channel_id=1, source_target_pairs={{0,1},{1,0},{2,3},{3,2},{4,5},{5,4},{6,7},{7,6},{8,9},{9,8},{10,11... | collective-permute-start | bytes 208904 | tf_op jit(solution)/shard_map/ppermute | solution.py:202
  25.0 1.9 %collective-permute-start = (f16[272,128]{1,0:T(8,128)(2,1)S(1)}, f16[272,128]{1,0:T(8,128)(2,1)S(1)}, u32[]{:S(2)}, u32[]{:S(2)}) collective-permute-start(f16[272,128]{1,0:T(8,128)(2,1)S(1)} %convert_element_type.59), channel_id=1, source_target_pairs={{1,2},{2,1},{3,4},{4,3},{5,6},{6,5},{7,8},{8,7},{9,10},{10,9},{11,... | collective-permute-start | bytes 208904 | tf_op jit(solution)/shard_map/ppermute | solution.py:202
  26.9 0.0 collective-permute-done.3
  26.9 0.0 collective-permute-done.2
  27.0 0.3 collective-permute-done.1
  27.3 4.2 %collective-permute-done = f16[272,128]{1,0:T(8,128)(2,1)S(1)} collective-permute-done((f16[272,128]{1,0:T(8,128)(2,1)S(1)}, f16[272,128]{1,0:T(8,128)(2,1)S(1)}, u32[]{:S(2)}, u32[]{:S(2)}) %collective-permute-start) | collective-permute-done | bytes 69664 | tf_op jit(solution)/shard_map/ppermute | solution.py:202
  31.5 3.5 %sweep.1 = (f32[768,128]{1,0:T(8,128)S(1)}, f32[512,128]{1,0:T(8,128)S(1)}, f32[512,128]{1,0:T(8,128)S(1)}, f32[272,128]{1,0:T(8,128)S(1)}, f32[272,128]{1,0:T(8...) custom-call(s32[9]{0:T(128)S(1)} %stack.43.info, bf16[768,768]{1,0:T(8,128)(2,1)S(1)} %get-tuple-element.20.high, ...), custom_call_target="tpu_custom_call" | custom-call | tf_op jit(solution)/shard_map/sweep/pallas_call | solution.py:265
  35.1 1.9 %collective-permute-start.7 = (f16[272,128]{1,0:T(8,128)(2,1)S(1)}, f16[272,128]{1,0:T(8,128)(2,1)S(1)}, u32[]{:S(2)}, u32[]{:S(2)}) collective-permute-start(f16[272,128]{1,0:T(8,128)(2,1)S(1)} %convert_element_type.73), channel_id=1, source_target_pairs={{16,32},{32,16},{48,64},{64,48},{80,96},{96,80},{112,128},{128,112... | collective-permute-start | bytes 208904 | tf_op jit(solution)/shard_map/ppermute | solution.py:202
  37.1 0.6 %collective-permute-start.6 = (f16[272,128]{1,0:T(8,128)(2,1)S(1)}, f16[272,128]{1,0:T(8,128)(2,1)S(1)}, u32[]{:S(2)}, u32[]{:S(2)}) collective-permute-start(f16[272,128]{1,0:T(8,128)(2,1)S(1)} %convert_element_type.71), channel_id=1, source_target_pairs={{0,16},{16,0},{32,48},{48,32},{64,80},{80,64},{96,112},{112,96},{1... | collective-permute-start | bytes 208904 | tf_op jit(solution)/shard_map/ppermute | solution.py:202
  37.7 0.5 %collective-permute-start.5 = (f16[272,128]{1,0:T(8,128)(2,1)S(1)}, f16[272,128]{1,0:T(8,128)(2,1)S(1)}, u32[]{:S(2)}, u32[]{:S(2)}) collective-permute-start(f16[272,128]{1,0:T(8,128)(2,1)S(1)} %convert_element_type.69), channel_id=1, source_target_pairs={{0,1},{1,0},{2,3},{3,2},{4,5},{5,4},{6,7},{7,6},{8,9},{9,8},{10,11... | collective-permute-start | bytes 208904 | tf_op jit(solution)/shard_map/ppermute | solution.py:202
  38.2 1.9 %collective-permute-start.4 = (f16[272,128]{1,0:T(8,128)(2,1)S(1)}, f16[272,128]{1,0:T(8,128)(2,1)S(1)}, u32[]{:S(2)}, u32[]{:S(2)}) collective-permute-start(f16[272,128]{1,0:T(8,128)(2,1)S(1)} %convert_element_type.67), channel_id=1, source_target_pairs={{1,2},{2,1},{3,4},{4,3},{5,6},{6,5},{7,8},{8,7},{9,10},{10,9},{11,... | collective-permute-start | bytes 208904 | tf_op jit(solution)/shard_map/ppermute | solution.py:202
  40.1 4.9 %collective-permute-done.7 = f16[272,128]{1,0:T(8,128)(2,1)S(1)} collective-permute-done((f16[272,128]{1,0:T(8,128)(2,1)S(1)}, f16[272,128]{1,0:T(8,128)(2,1)S(1)}, u32[]{:S(2)}, u32[]{:S(2)}) %collective-permute-start.7) | collective-permute-done | bytes 69664 | tf_op jit(solution)/shard_map/ppermute | solution.py:202
  45.1 0.0 collective-permute-done.6
  45.1 0.0 collective-permute-done.5
  45.1 0.0 collective-permute-done.4
  45.2 2.2 %final.1 = (f32[768,128]{1,0:T(8,128)}, f32[768,128]{1,0:T(8,128)}) custom-call(s32[9]{0:T(128)S(1)} %stack.43.info, bf16[768,768]{1,0:T(8,128)(2,1)S(1)} %get-tuple-element.20.high, bf16[768,768]{1,0:T(8,128)(2,1)S(1)} %get-tuple-element.21.low, f32[768,128]{1,0:T(8,128)S(1)} %get-tuple-element.22.loads, f32[768,128]{1,0:T(8,128)S(1)} %get-tuple-element.29.ahead, ...), custom_call_target="tpu_custom_call" | custom-call | tf_op jit(solution)/shard_map/final/pallas_call | solution.py:280
  (16 shorter events, 0.2 us)
Async XLA Ops:
  9.3 17.6 %collective-permute-start.3 = (f16[272,128]{1,0:T(8,128)(2,1)S(1)}, f16[272,128]{1,0:T(8,128)(2,1)S(1)}, u32[]{:S(2)}, u32[]{:S(2)}) collective-permute-start(f16[272,128]{1,0:T(8,128)(2,1)S(1)} %convert_element_type.65), channel_id=1, source_target_pairs={{16,32},{32,16},{48,64},{64,48},{80,96},{96,80},{112,128},{128,112... | collective-permute-start | bytes 208904 | tf_op jit(solution)/shard_map/ppermute | solution.py:202
  17.7 9.2 %collective-permute-start.2 = (f16[272,128]{1,0:T(8,128)(2,1)S(1)}, f16[272,128]{1,0:T(8,128)(2,1)S(1)}, u32[]{:S(2)}, u32[]{:S(2)}) collective-permute-start(f16[272,128]{1,0:T(8,128)(2,1)S(1)} %convert_element_type.63), channel_id=1, source_target_pairs={{0,16},{16,0},{32,48},{48,32},{64,80},{80,64},{96,112},{112,96},{1... | collective-permute-start | bytes 208904 | tf_op jit(solution)/shard_map/ppermute | solution.py:202
  17.8 9.4 %collective-permute-start.1 = (f16[272,128]{1,0:T(8,128)(2,1)S(1)}, f16[272,128]{1,0:T(8,128)(2,1)S(1)}, u32[]{:S(2)}, u32[]{:S(2)}) collective-permute-start(f16[272,128]{1,0:T(8,128)(2,1)S(1)} %convert_element_type.61), channel_id=1, source_target_pairs={{0,1},{1,0},{2,3},{3,2},{4,5},{5,4},{6,7},{7,6},{8,9},{9,8},{10,11... | collective-permute-start | bytes 208904 | tf_op jit(solution)/shard_map/ppermute | solution.py:202
  25.0 6.5 %collective-permute-start = (f16[272,128]{1,0:T(8,128)(2,1)S(1)}, f16[272,128]{1,0:T(8,128)(2,1)S(1)}, u32[]{:S(2)}, u32[]{:S(2)}) collective-permute-start(f16[272,128]{1,0:T(8,128)(2,1)S(1)} %convert_element_type.59), channel_id=1, source_target_pairs={{1,2},{2,1},{3,4},{4,3},{5,6},{6,5},{7,8},{8,7},{9,10},{10,9},{11,... | collective-permute-start | bytes 208904 | tf_op jit(solution)/shard_map/ppermute | solution.py:202
  35.1 10.0 %collective-permute-start.7 = (f16[272,128]{1,0:T(8,128)(2,1)S(1)}, f16[272,128]{1,0:T(8,128)(2,1)S(1)}, u32[]{:S(2)}, u32[]{:S(2)}) collective-permute-start(f16[272,128]{1,0:T(8,128)(2,1)S(1)} %convert_element_type.73), channel_id=1, source_target_pairs={{16,32},{32,16},{48,64},{64,48},{80,96},{96,80},{112,128},{128,112... | collective-permute-start | bytes 208904 | tf_op jit(solution)/shard_map/ppermute | solution.py:202
  37.1 8.0 %collective-permute-start.6 = (f16[272,128]{1,0:T(8,128)(2,1)S(1)}, f16[272,128]{1,0:T(8,128)(2,1)S(1)}, u32[]{:S(2)}, u32[]{:S(2)}) collective-permute-start(f16[272,128]{1,0:T(8,128)(2,1)S(1)} %convert_element_type.71), channel_id=1, source_target_pairs={{0,16},{16,0},{32,48},{48,32},{64,80},{80,64},{96,112},{112,96},{1... | collective-permute-start | bytes 208904 | tf_op jit(solution)/shard_map/ppermute | solution.py:202
  37.7 7.4 %collective-permute-start.5 = (f16[272,128]{1,0:T(8,128)(2,1)S(1)}, f16[272,128]{1,0:T(8,128)(2,1)S(1)}, u32[]{:S(2)}, u32[]{:S(2)}) collective-permute-start(f16[272,128]{1,0:T(8,128)(2,1)S(1)} %convert_element_type.69), channel_id=1, source_target_pairs={{0,1},{1,0},{2,3},{3,2},{4,5},{5,4},{6,7},{7,6},{8,9},{9,8},{10,11... | collective-permute-start | bytes 208904 | tf_op jit(solution)/shard_map/ppermute | solution.py:202
  38.2 6.9 %collective-permute-start.4 = (f16[272,128]{1,0:T(8,128)(2,1)S(1)}, f16[272,128]{1,0:T(8,128)(2,1)S(1)}, u32[]{:S(2)}, u32[]{:S(2)}) collective-permute-start(f16[272,128]{1,0:T(8,128)(2,1)S(1)} %convert_element_type.67), channel_id=1, source_target_pairs={{1,2},{2,1},{3,4},{4,3},{5,6},{6,5},{7,8},{8,7},{9,10},{10,9},{11,... | collective-permute-start | bytes 208904 | tf_op jit(solution)/shard_map/ppermute | solution.py:202

commit v3 on v2

--- a/solution.py
+++ b/solution.py
@@ -60,13 +60,10 @@
     slots, width, _ = coupling.shape
     tiles = width // TILE
 
-    def fetch_inverse(slot):
-        return pltpu.make_async_copy(inverse.at[slot], i_buf.at[slot], sems.at[slot, tiles])
-
-    def fetch_rows(slot, i):
-        rows = pl.ds(i * TILE, TILE)
-        return pltpu.make_async_copy(
-            coupling.at[slot, rows], c_buf.at[slot, rows], sems.at[slot, i]
+    def fetch(slot):
+        return (
+            pltpu.make_async_copy(coupling.at[slot], c_buf.at[slot], sems.at[0, slot]),
+            pltpu.make_async_copy(inverse.at[slot], i_buf.at[slot], sems.at[1, slot]),
         )
 
     side = (
@@ -77,27 +74,27 @@
     for slot in range(slots):
         @pl.when(slot < blocks)
         def _():
-            fetch_inverse(slot).start()
-            for i in reversed(range(tiles)):
-                fetch_rows(slot, i).start()
+            for copy in fetch(slot):
+                copy.start()
         if slot == 0:
             for copy in side:
                 copy.start()
 
-    for i in range(tiles):
-        acc[i * TILE : (i + 1) * TILE, i * TILE :] = jnp.zeros((TILE, width - i * TILE), f32)
+    for j in range(tiles):
+        rows, cols = slice(0, (j + 1) * TILE), slice(j * TILE, (j + 1) * TILE)
+        acc[rows, cols] = jnp.zeros(((j + 1) * TILE, TILE), f32)
 
     def one_slot(slot, carry):
+        for copy in fetch(slot):
+            copy.wait()
         c_ref, i_ref = c_buf.at[slot], i_buf.at[slot]
-        fetch_inverse(slot).wait()
-        for i in reversed(range(tiles)):
-            fetch_rows(slot, i).wait()
-            rows = slice(i * TILE, (i + 1) * TILE)
-            p_buf[rows] = jnp.dot(c_ref[rows], i_ref[...], preferred_element_type=f32).astype(bf16)
+        p_buf[...] = jnp.dot(c_ref[...], i_ref[...], preferred_element_type=f32).astype(bf16)
+        for j in range(tiles):
+            rows, cols = slice(0, (j + 1) * TILE), slice(j * TILE, (j + 1) * TILE)
             term = lax.dot_general(
-                p_buf[rows], c_ref[i * TILE :], (((1,), (1,)), ((), ())), preferred_element_type=f32
+                p_buf[rows], c_ref[cols], (((1,), (1,)), ((), ())), preferred_element_type=f32
             )
-            acc[rows, i * TILE :] = acc[rows, i * TILE :] + term
+            acc[rows, cols] = acc[rows, cols] + term
         return carry
 
     lax.fori_loop(0, blocks, one_slot, 0)
@@ -145,9 +142,9 @@
     for k, (sent, got) in enumerate(
         zip((sent_a, sent_b, sent_c, sent_d), (got_a, got_b, got_c, got_d))
     ):
-        back = jnp.exp2(got[2 * FACE : 2 * FACE + 1] - 13.0)
+        back = alive[k] * jnp.exp2(got[2 * FACE : 2 * FACE + 1] - 13.0)
         mine = jnp.exp2(sent[2 * FACE : 2 * FACE + 1] - 13.0)
-        first = got[:FACE]
+        first = alive[k] * got[:FACE]
         v0[faces[k]] = first
         v1[faces[k]] = (
             first + got[FACE : 2 * FACE] * back + (alive[k] * (2.0 / centre)) * sent[:FACE]
@@ -184,7 +181,8 @@
     traces[...] = ahead[...]
     faces = [pl.ds(pl.multiple_of(info[1 + k] * FACE, FACE), FACE) for k in range(4)]
     for k, got in enumerate((got_a, got_b, got_c, got_d)):
-        back = jnp.exp2(got[2 * FACE : 2 * FACE + 1] - 12.0)
+        alive = info[5 + k].astype(f32)
+        back = alive * jnp.exp2(got[2 * FACE : 2 * FACE + 1] - 12.0)
         v2 = got[:FACE] * back + fix2[faces[k]]
         v3[faces[k]] = v2 + got[FACE : 2 * FACE] * back + fix3[faces[k]]
         traces[faces[k]] = ahead[faces[k]] + (2.0 * gain[1]) * v2
@@ -199,6 +197,8 @@
     route = []
     for i in range(first, extent - 1, 2):
         route += [(i, i + 1), (i + 1, i)]
+    if first:
+        route += [(extent - 1, 0), (0, extent - 1)]
     return lax.ppermute(block.astype(jnp.float16), axes, route).astype(f32)
 
 
@@ -255,7 +255,7 @@
             pltpu.VMEM((width, width), bf16),
             pltpu.VMEM((width, width), bf16),
             pltpu.VMEM((width, width), f32),
-            pltpu.SemaphoreType.DMA((slots, width // TILE + 1)),
+            pltpu.SemaphoreType.DMA((2, slots)),
             pltpu.SemaphoreType.DMA((3,)),
         ],
         compiler_params=params,

time: 48.1 us -> 43.7 us (0.909)
  the two profiles are of different devices: /device:TPU:30 before, /device:TPU:1 now
where the time goes in v3:
time: 43.7 us; the launch traced here: 44.1 us
  starting transfers between devices  24.2 us (55%)
  Pallas kernels  10.7 us (24%)
  waiting for transfers between devices  7.43 us (17%)
  between operations  1.45 us (3%)
    ppermute x8, starting transfers between devices, swap(): return lax.ppermute(block.astype(jnp.float16), axes, route).astype(f32)  24.2 us
    ppermute x8, waiting for transfers between devices, swap(): return lax.ppermute(block.astype(jnp.float16), axes, route).astype(f32)  7.43 us
    pallas_call x1, Pallas kernels, on_device(): pl.pallas_call(condense_kernel, out_shape=(square, square, field, field,...  4.97 us
    pallas_call x1, Pallas kernels, on_device(): pl.pallas_call(sweep_kernel, out_shape=(field, faces, faces, message, mes...  3.52 us
    pallas_call x1, Pallas kernels, on_device(): pl.pallas_call(final_kernel, out_shape=(field, field), in_specs=[smem] +...  2.17 us
  transfers between devices with their start and end apart: 8, of which 4 were waited for; matrix products, arithmetic and copies ran while one was open for 0% of the time, Pallas kernels for 0%

profile of v3, /device:TPU:1, one launch (start us, length us, event | category | flops | bytes accessed | tf_op | source)
XLA Modules:
  0.0 44.1 jit_solution(6184054761618538846)
XLA Ops:
  1.3 0.1 stack.43.info
  1.4 5.0 %condense.1 = (bf16[768,768]{1,0:T(8,128)(2,1)S(1)}, bf16[768,768]{1,0:T(8,128)(2,1)S(1)}, f32[768,128]{1,0:T(8,128)S(1)}, f32[768,128]{1,0:T(8,128)S(1)}, f32[7...) custom-call(s32[9]{0:T(128)S(1)} %stack.43.info, ...), custom_call_target="tpu_custom_call" | custom-call | tf_op jit(solution)/shard_map/condense/pallas_call | solution.py:247
  6.4 11.1 %collective-permute-start.3 = (f16[272,128]{1,0:T(8,128)(2,1)S(1)}, f16[272,128]{1,0:T(8,128)(2,1)S(1)}, u32[]{:S(2)}, u32[]{:S(2)}) collective-permute-start(f16[272,128]{1,0:T(8,128)(2,1)S(1)} %convert_element_type.65), channel_id=1, source_target_pairs={{16,32},{32,16},{48,64},{64,48},{80,96},{96,80},{112,128},{128,112... | collective-permute-start | bytes 208904 | tf_op jit(solution)/shard_map/ppermute | solution.py:202
  17.5 0.1 collective-permute-start.2
  17.6 2.9 %collective-permute-start.1 = (f16[272,128]{1,0:T(8,128)(2,1)S(1)}, f16[272,128]{1,0:T(8,128)(2,1)S(1)}, u32[]{:S(2)}, u32[]{:S(2)}) collective-permute-start(f16[272,128]{1,0:T(8,128)(2,1)S(1)} %convert_element_type.61), channel_id=1, source_target_pairs={{0,1},{1,0},{2,3},{3,2},{4,5},{5,4},{6,7},{7,6},{8,9},{9,8},{10,11... | collective-permute-start | bytes 208904 | tf_op jit(solution)/shard_map/ppermute | solution.py:202
  20.6 2.2 %collective-permute-start = (f16[272,128]{1,0:T(8,128)(2,1)S(1)}, f16[272,128]{1,0:T(8,128)(2,1)S(1)}, u32[]{:S(2)}, u32[]{:S(2)}) collective-permute-start(f16[272,128]{1,0:T(8,128)(2,1)S(1)} %convert_element_type.59), channel_id=1, source_target_pairs={{1,2},{2,1},{3,4},{4,3},{5,6},{6,5},{7,8},{8,7},{9,10},{10,9},{11,... | collective-permute-start | bytes 208904 | tf_op jit(solution)/shard_map/ppermute | solution.py:202
  22.8 0.0 collective-permute-done.3
  22.8 0.0 collective-permute-done.2
  22.9 0.6 %collective-permute-done.1 = f16[272,128]{1,0:T(8,128)(2,1)S(1)} collective-permute-done((f16[272,128]{1,0:T(8,128)(2,1)S(1)}, f16[272,128]{1,0:T(8,128)(2,1)S(1)}, u32[]{:S(2)}, u32[]{:S(2)}) %collective-permute-start.1) | collective-permute-done | bytes 69664 | tf_op jit(solution)/shard_map/ppermute | solution.py:202
  23.5 2.4 %collective-permute-done = f16[272,128]{1,0:T(8,128)(2,1)S(1)} collective-permute-done((f16[272,128]{1,0:T(8,128)(2,1)S(1)}, f16[272,128]{1,0:T(8,128)(2,1)S(1)}, u32[]{:S(2)}, u32[]{:S(2)}) %collective-permute-start) | collective-permute-done | bytes 69664 | tf_op jit(solution)/shard_map/ppermute | solution.py:202
  26.0 3.5 %sweep.1 = (f32[768,128]{1,0:T(8,128)S(1)}, f32[512,128]{1,0:T(8,128)S(1)}, f32[512,128]{1,0:T(8,128)S(1)}, f32[272,128]{1,0:T(8,128)S(1)}, f32[272,128]{1,0:T(8...) custom-call(s32[9]{0:T(128)S(1)} %stack.43.info, bf16[768,768]{1,0:T(8,128)(2,1)S(1)} %get-tuple-element.20.high, ...), custom_call_target="tpu_custom_call" | custom-call | tf_op jit(solution)/shard_map/sweep/pallas_call | solution.py:265
  29.5 3.4 %collective-permute-start.7 = (f16[272,128]{1,0:T(8,128)(2,1)S(1)}, f16[272,128]{1,0:T(8,128)(2,1)S(1)}, u32[]{:S(2)}, u32[]{:S(2)}) collective-permute-start(f16[272,128]{1,0:T(8,128)(2,1)S(1)} %convert_element_type.73), channel_id=1, source_target_pairs={{16,32},{32,16},{48,64},{64,48},{80,96},{96,80},{112,128},{128,112... | collective-permute-start | bytes 208904 | tf_op jit(solution)/shard_map/ppermute | solution.py:202
  33.0 0.1 collective-permute-start.6
  33.1 1.7 %collective-permute-start.5 = (f16[272,128]{1,0:T(8,128)(2,1)S(1)}, f16[272,128]{1,0:T(8,128)(2,1)S(1)}, u32[]{:S(2)}, u32[]{:S(2)}) collective-permute-start(f16[272,128]{1,0:T(8,128)(2,1)S(1)} %convert_element_type.69), channel_id=1, source_target_pairs={{0,1},{1,0},{2,3},{3,2},{4,5},{5,4},{6,7},{7,6},{8,9},{9,8},{10,11... | collective-permute-start | bytes 208904 | tf_op jit(solution)/shard_map/ppermute | solution.py:202
  34.8 2.6 %collective-permute-start.4 = (f16[272,128]{1,0:T(8,128)(2,1)S(1)}, f16[272,128]{1,0:T(8,128)(2,1)S(1)}, u32[]{:S(2)}, u32[]{:S(2)}) collective-permute-start(f16[272,128]{1,0:T(8,128)(2,1)S(1)} %convert_element_type.67), channel_id=1, source_target_pairs={{1,2},{2,1},{3,4},{4,3},{5,6},{6,5},{7,8},{8,7},{9,10},{10,9},{11,... | collective-permute-start | bytes 208904 | tf_op jit(solution)/shard_map/ppermute | solution.py:202
  37.5 0.0 collective-permute-done.7
  37.5 0.0 collective-permute-done.6
  37.5 0.3 collective-permute-done.5
  37.8 4.1 %collective-permute-done.4 = f16[272,128]{1,0:T(8,128)(2,1)S(1)} collective-permute-done((f16[272,128]{1,0:T(8,128)(2,1)S(1)}, f16[272,128]{1,0:T(8,128)(2,1)S(1)}, u32[]{:S(2)}, u32[]{:S(2)}) %collective-permute-start.4) | collective-permute-done | bytes 69664 | tf_op jit(solution)/shard_map/ppermute | solution.py:202
  41.9 2.2 %final.1 = (f32[768,128]{1,0:T(8,128)}, f32[768,128]{1,0:T(8,128)}) custom-call(s32[9]{0:T(128)S(1)} %stack.43.info, bf16[768,768]{1,0:T(8,128)(2,1)S(1)} %get-tuple-element.20.high, bf16[768,768]{1,0:T(8,128)(2,1)S(1)} %get-tuple-element.21.low, f32[768,128]{1,0:T(8,128)S(1)} %get-tuple-element.22.loads, f32[768,128]{1,0:T(8,128)S(1)} %get-tuple-element.29.ahead, ...), custom_call_target="tpu_custom_call" | custom-call | tf_op jit(solution)/shard_map/final/pallas_call | solution.py:280
  (16 shorter events, 0.2 us)
Async XLA Ops:
  6.4 16.4 %collective-permute-start.3 = (f16[272,128]{1,0:T(8,128)(2,1)S(1)}, f16[272,128]{1,0:T(8,128)(2,1)S(1)}, u32[]{:S(2)}, u32[]{:S(2)}) collective-permute-start(f16[272,128]{1,0:T(8,128)(2,1)S(1)} %convert_element_type.65), channel_id=1, source_target_pairs={{16,32},{32,16},{48,64},{64,48},{80,96},{96,80},{112,128},{128,112... | collective-permute-start | bytes 208904 | tf_op jit(solution)/shard_map/ppermute | solution.py:202
  17.5 5.3 %collective-permute-start.2 = (f16[272,128]{1,0:T(8,128)(2,1)S(1)}, f16[272,128]{1,0:T(8,128)(2,1)S(1)}, u32[]{:S(2)}, u32[]{:S(2)}) collective-permute-start(f16[272,128]{1,0:T(8,128)(2,1)S(1)} %convert_element_type.63), channel_id=1, source_target_pairs={{0,16},{16,0},{32,48},{48,32},{64,80},{80,64},{96,112},{112,96},{1... | collective-permute-start | bytes 208904 | tf_op jit(solution)/shard_map/ppermute | solution.py:202
  17.6 5.9 %collective-permute-start.1 = (f16[272,128]{1,0:T(8,128)(2,1)S(1)}, f16[272,128]{1,0:T(8,128)(2,1)S(1)}, u32[]{:S(2)}, u32[]{:S(2)}) collective-permute-start(f16[272,128]{1,0:T(8,128)(2,1)S(1)} %convert_element_type.61), channel_id=1, source_target_pairs={{0,1},{1,0},{2,3},{3,2},{4,5},{5,4},{6,7},{7,6},{8,9},{9,8},{10,11... | collective-permute-start | bytes 208904 | tf_op jit(solution)/shard_map/ppermute | solution.py:202
  20.6 5.4 %collective-permute-start = (f16[272,128]{1,0:T(8,128)(2,1)S(1)}, f16[272,128]{1,0:T(8,128)(2,1)S(1)}, u32[]{:S(2)}, u32[]{:S(2)}) collective-permute-start(f16[272,128]{1,0:T(8,128)(2,1)S(1)} %convert_element_type.59), channel_id=1, source_target_pairs={{1,2},{2,1},{3,4},{4,3},{5,6},{6,5},{7,8},{8,7},{9,10},{10,9},{11,... | collective-permute-start | bytes 208904 | tf_op jit(solution)/shard_map/ppermute | solution.py:202
  29.5 7.9 %collective-permute-start.7 = (f16[272,128]{1,0:T(8,128)(2,1)S(1)}, f16[272,128]{1,0:T(8,128)(2,1)S(1)}, u32[]{:S(2)}, u32[]{:S(2)}) collective-permute-start(f16[272,128]{1,0:T(8,128)(2,1)S(1)} %convert_element_type.73), channel_id=1, source_target_pairs={{16,32},{32,16},{48,64},{64,48},{80,96},{96,80},{112,128},{128,112... | collective-permute-start | bytes 208904 | tf_op jit(solution)/shard_map/ppermute | solution.py:202
  33.0 4.5 %collective-permute-start.6 = (f16[272,128]{1,0:T(8,128)(2,1)S(1)}, f16[272,128]{1,0:T(8,128)(2,1)S(1)}, u32[]{:S(2)}, u32[]{:S(2)}) collective-permute-start(f16[272,128]{1,0:T(8,128)(2,1)S(1)} %convert_element_type.71), channel_id=1, source_target_pairs={{0,16},{16,0},{32,48},{48,32},{64,80},{80,64},{96,112},{112,96},{1... | collective-permute-start | bytes 208904 | tf_op jit(solution)/shard_map/ppermute | solution.py:202
  33.1 4.7 %collective-permute-start.5 = (f16[272,128]{1,0:T(8,128)(2,1)S(1)}, f16[272,128]{1,0:T(8,128)(2,1)S(1)}, u32[]{:S(2)}, u32[]{:S(2)}) collective-permute-start(f16[272,128]{1,0:T(8,128)(2,1)S(1)} %convert_element_type.69), channel_id=1, source_target_pairs={{0,1},{1,0},{2,3},{3,2},{4,5},{5,4},{6,7},{7,6},{8,9},{9,8},{10,11... | collective-permute-start | bytes 208904 | tf_op jit(solution)/shard_map/ppermute | solution.py:202
  34.8 7.1 %collective-permute-start.4 = (f16[272,128]{1,0:T(8,128)(2,1)S(1)}, f16[272,128]{1,0:T(8,128)(2,1)S(1)}, u32[]{:S(2)}, u32[]{:S(2)}) collective-permute-start(f16[272,128]{1,0:T(8,128)(2,1)S(1)} %convert_element_type.67), channel_id=1, source_target_pairs={{1,2},{2,1},{3,4},{4,3},{5,6},{6,5},{7,8},{8,7},{9,10},{10,9},{11,... | collective-permute-start | bytes 208904 | tf_op jit(solution)/shard_map/ppermute | solution.py:202

commit v4 on v3

v4 whole, which is shorter than its diff:
```python
import jax
import jax.numpy as jnp
from jax import lax
from jax.experimental import pallas as pl
from jax.experimental.pallas import tpu as pltpu
from jax.sharding import PartitionSpec as P

SWEEPS = 3
TILE = 256
FACE = 128
EXTRA = 8

lower_bound = 1.0
upper_bound = 14.0
centre = (upper_bound + lower_bound) / 2.0
half = (upper_bound - lower_bound) / 2.0
sigma = centre / half
rho0 = 1.0 / sigma
rho1 = 1.0 / (2.0 * sigma - rho0)
rho2 = 1.0 / (2.0 * sigma - rho1)
keep = (rho1 * rho0, rho2 * rho1)
gain = (2.0 * rho1 / half, 2.0 * rho2 / half)

f32, bf16 = jnp.float32, jnp.bfloat16
VMEM_LIMIT = 48 << 20


def split(value):
    high = value.astype(bf16)
    return high, (value - high.astype(f32)).astype(bf16)


def times(high_ref, low_ref, traces):
    high, low = split(traces)
    both = jnp.concatenate([high, low], axis=1)
    cols = slice(0, traces.shape[0])
    out = jnp.dot(high_ref[:, cols], both, preferred_element_type=f32)
    out = out + jnp.dot(low_ref[:, cols], both, preferred_element_type=f32)
    return out[:, : traces.shape[1]] + out[:, traces.shape[1] :]


def round_half(value):
    big = value * 8193.0
    return big - (big - value)


def exponent_of(top):
    return jnp.floor(jnp.log2(jnp.maximum(top, 1e-30)))


def largest(value):
    return jnp.max(jnp.abs(value), keepdims=True)


def place():
    rows, columns = lax.axis_size("gx"), lax.axis_size("gy") * lax.axis_size("ha")
    row = lax.axis_index("gx")
    column = lax.axis_index("gy") * lax.axis_size("ha") + lax.axis_index("ha")
    there = (row > 0, row + 1 < rows, column > 0, column + 1 < columns)
    return (lax.rem(row, 2), lax.rem(column, 2)) + tuple(jnp.where(t, 1.0, 0.0) for t in there)


def by_face(info, of_permutes):
    odd_row, odd_col = info[0] == 1, info[1] == 1
    cols_odd, cols_even, rows_even, rows_odd = of_permutes
    return (
        jnp.where(odd_row, rows_even, rows_odd),
        jnp.where(odd_row, rows_odd, rows_even),
        jnp.where(odd_col, cols_even, cols_odd),
        jnp.where(odd_col, cols_odd, cols_even),
    )


def by_permute(info, of_faces):
    odd_row, odd_col = info[0] == 1, info[1] == 1
    below, above, left, right = of_faces
    return (
        jnp.where(odd_col, right, left),
        jnp.where(odd_col, left, right),
        jnp.where(odd_row, below, above),
        jnp.where(odd_row, above, below),
    )


def unpack(info, messages, bias, mask):
    first, second = [], []
    for k, part in enumerate(by_face(info, [msg[...] for msg in messages])):
        back = jnp.exp2(part[2 * FACE : 2 * FACE + 1] - bias)
        one = part[:FACE]
        if mask:
            alive = info[2 + k]
            one, back = alive * one, alive * back
        first.append(one)
        second.append(part[FACE : 2 * FACE] * back)
    return first, second


def pack(info, messages, first, second, power):
    tail = jnp.broadcast_to(power, (EXTRA, FACE))
    faces = [slice(k * FACE, (k + 1) * FACE) for k in range(4)]
    one = by_permute(info, [first[face] for face in faces])
    two = by_permute(info, [second[face] for face in faces])
    for k, msg in enumerate(messages):
        msg[:FACE] = one[k]
        msg[FACE : 2 * FACE] = two[k]
        msg[2 * FACE :] = tail


def alive_faces(info, value):
    return jnp.concatenate(
        [value[k * FACE : (k + 1) * FACE] * info[2 + k] for k in range(4)], axis=0
    )


def condense_kernel(
    counts, coupling, inverse, stiffness, start_in, loads_in,
    high, low, rest, start, loads, msg_a, msg_b, msg_c, msg_d,
    c_buf, i_buf, p_buf, b_buf, acc, count, sems, side_sems,
):
    info = place()
    slots, width, _ = coupling.shape
    tiles = width // TILE

    def fetch(slot):
        return (
            pltpu.make_async_copy(coupling.at[slot], c_buf.at[slot], sems.at[0, slot]),
            pltpu.make_async_copy(inverse.at[slot], i_buf.at[slot], sems.at[1, slot]),
        )

    side = (
        pltpu.make_async_copy(stiffness, b_buf, side_sems.at[0]),
        pltpu.make_async_copy(start_in, start, side_sems.at[1]),
        pltpu.make_async_copy(loads_in, loads, side_sems.at[2]),
    )
    live = pltpu.make_async_copy(counts, count, side_sems.at[3])
    live.start()
    for copy in fetch(0):
        copy.start()
    for copy in side:
        copy.start()

    for j in range(tiles):
        rows, cols = slice(0, (j + 1) * TILE), slice(j * TILE, (j + 1) * TILE)
        acc[rows, cols] = jnp.zeros(((j + 1) * TILE, TILE), f32)

    live.wait()
    blocks = count[0, 0]

    @pl.loop(0, blocks)
    def _(slot):
        for copy in fetch(slot):
            copy.wait()

        @pl.when(slot + 1 < blocks)
        def _():
            for copy in fetch(slot + 1):
                copy.start()

        c_ref, i_ref = c_buf.at[slot], i_buf.at[slot]
        p_buf[...] = jnp.dot(c_ref[...], i_ref[...], preferred_element_type=f32).astype(bf16)
        for j in range(tiles):
            rows, cols = slice(0, (j + 1) * TILE), slice(j * TILE, (j + 1) * TILE)
            term = lax.dot_general(
                p_buf[rows], c_ref[cols], (((1,), (1,)), ((), ())), preferred_element_type=f32
            )
            acc[rows, cols] = acc[rows, cols] + term

    for copy in side:
        copy.wait()
    for i in range(tiles):
        rows = slice(i * TILE, (i + 1) * TILE)
        for j in range(i, tiles):
            cols = slice(j * TILE, (j + 1) * TILE)
            block = b_buf[rows, cols].astype(f32) - acc[rows, cols]
            upper_high, upper_low = split(block)
            high[rows, cols] = upper_high
            low[rows, cols] = upper_low
            if j > i:
                mirror_high, mirror_low = split(block.T)
                high[cols, rows] = mirror_high
                low[cols, rows] = mirror_low

    x0 = start[...]
    y0 = loads[...] - times(high, low, x0) - 2.0 * x0
    rest[...] = y0
    edges = 4 * FACE
    first = round_half(x0[:edges])
    edge = x0[:edges] - first + y0[:edges] * (1.0 / centre)
    power = exponent_of(largest(edge))
    second = round_half(edge * jnp.exp2(13.0 - power))
    pack(info, (msg_a, msg_b, msg_c, msg_d), first, second, power)


def early_kernel(
    high, low, start, loads, rest, sent_a, sent_b, sent_c, sent_d, ready, plain, owned, echo
):
    info = place()
    moved = start[...] + rest[...] * (1.0 / centre)
    left = loads[...] - times(high, low, moved) - 2.0 * moved
    ready[...] = moved + (keep[0] / centre) * rest[...] + gain[0] * left
    plain[...] = gain[1] * loads[...] - keep[1] * moved
    first, second = unpack(info, (sent_a, sent_b, sent_c, sent_d), 13.0, False)
    first = jnp.concatenate(first, axis=0)
    owned[...] = first + jnp.concatenate(second, axis=0)
    echo[...] = alive_faces(info, (2.0 / centre) * first)


def sweep_kernel(
    high, low, ready, plain, owned, echo, got_a, got_b, got_c, got_d,
    ahead, fix2, fix3, msg_a, msg_b, msg_c, msg_d,
):
    info = place()
    edges = 4 * FACE
    step = 2.0 / centre
    first, second = unpack(info, (got_a, got_b, got_c, got_d), 13.0, True)
    v0 = jnp.concatenate(first, axis=0)
    pushed = times(high, low, v0)
    v1 = v0 + jnp.concatenate(second, axis=0) + echo[...]
    own = owned[...] + step * v0
    half_way = ready[...] - (gain[0] * step) * pushed
    x2p = half_way[:edges] + (step * (1.0 + keep[0] - 2.0 * gain[0])) * v0
    x2 = jnp.concatenate([x2p + (2.0 * gain[0]) * v1, half_way[edges:]], axis=0)
    pushed = times(high, low, x2)
    fix2[...] = v1 + (2.0 * gain[0]) * alive_faces(info, own)
    first = x2p - own
    x3p = (1.0 + keep[1] - 2.0 * gain[1]) * x2 + plain[...] - gain[1] * pushed
    ahead[edges:] = x3p[edges:]
    x3p = x3p[:edges] - (keep[1] * step) * v0
    ahead[:edges] = x3p
    top = jnp.maximum(jnp.abs(first), jnp.abs(x3p - x2[:edges]))
    power = exponent_of(largest(top))
    scale = jnp.exp2(12.0 - power)
    first = round_half(first * scale)
    known = own + first * jnp.exp2(power - 12.0) + (2.0 * gain[0]) * v1
    second = round_half((x3p - known) * scale)
    pack(info, (msg_a, msg_b, msg_c, msg_d), first, second, power)
    fix3[...] = (2.0 * gain[1]) * alive_faces(info, known)


def late_kernel(high, low, loads, ahead, left):
    moved = ahead[...]
    left[...] = loads[...] - times(high, low, moved) - 2.0 * moved


def final_kernel(
    high, low, ahead, left, fix2, fix3, got_a, got_b, got_c, got_d,
    traces, residual, x3, r3, sems,
):
    info = place()
    edges = 4 * FACE
    first, second = unpack(info, (got_a, got_b, got_c, got_d), 12.0, True)
    scaled = [
        part[2 * FACE : 2 * FACE + 1]
        for part in by_face(info, [got[...] for got in (got_a, got_b, got_c, got_d)])
    ]
    there = jnp.concatenate(
        [one * jnp.exp2(power - 12.0) for one, power in zip(first, scaled)], axis=0
    )
    there = there + fix2[...]
    v3 = there + jnp.concatenate(second, axis=0) + fix3[...]
    x3[:edges] = ahead[:edges] + (2.0 * gain[1]) * there
    x3[edges:] = ahead[edges:]
    first = pltpu.make_async_copy(x3, traces, sems.at[0])
    first.start()
    copies = [first]
    for i in range(left.shape[0] // TILE):
        rows = slice(i * TILE, (i + 1) * TILE)
        part = left[rows] - (2.0 * gain[1]) * times(high.at[rows], low.at[rows], there)
        if i * TILE < edges:
            part = part + 2.0 * v3[rows] - (4.0 * gain[1]) * there[rows]
        r3[rows] = part
        copies.append(pltpu.make_async_copy(r3.at[rows], residual.at[rows], sems.at[1 + i]))
        copies[-1].start()
    for copy in copies:
        copy.wait()


def swap(block, axes, first, extent):
    route = []
    for i in range(first, extent - 1, 2):
        route += [(i, i + 1), (i + 1, i)]
    if first:
        route += [(extent - 1, 0), (0, extent - 1)]
    return lax.ppermute(block.astype(jnp.float16), axes, route).astype(f32)


def exchange(messages, rows, columns):
    msg_a, msg_b, msg_c, msg_d = messages
    return (
        swap(msg_a, ("gy", "ha"), 1, columns),
        swap(msg_b, ("gy", "ha"), 0, columns),
        swap(msg_c, "gx", 0, rows),
        swap(msg_d, "gx", 1, rows),
    )


def on_device(coupling, inverse, stiffness, block_counts, initial_traces, trace_loads):
    rows = lax.axis_size("gx")
    columns = lax.axis_size(("gy", "ha"))
    coupling, inverse, stiffness = coupling[0, 0], inverse[0, 0], stiffness[0, 0]
    start, loads = initial_traces[0, 0], trace_loads[0, 0]
    slots, width, _ = coupling.shape
    lanes = start.shape[1]
    vmem = pl.BlockSpec(memory_space=pltpu.VMEM)
    anywhere = pl.BlockSpec(memory_space=pltpu.HBM)
    square = jax.ShapeDtypeStruct((width, width), bf16)
    field = jax.ShapeDtypeStruct((width, lanes), f32)
    faces = jax.ShapeDtypeStruct((4 * FACE, lanes), f32)
    message = jax.ShapeDtypeStruct((2 * FACE + EXTRA, lanes), f32)
    params = pltpu.CompilerParams(vmem_limit_bytes=VMEM_LIMIT)

    high, low, rest, start, loads, *out = pl.pallas_call(
        condense_kernel,
        out_shape=(square, square, field, field, field, message, message, message, message),
        in_specs=[pl.BlockSpec(memory_space=pl.ANY)] + [anywhere] * 5,
        out_specs=(vmem,) * 9,
        scratch_shapes=[
            pltpu.VMEM((slots, width, width), bf16),
            pltpu.VMEM((slots, width, width), bf16),
            pltpu.VMEM((width, width), bf16),
            pltpu.VMEM((width, width), bf16),
            pltpu.VMEM((width, width), f32),
            pltpu.SMEM((1, 1), jnp.int32),
            pltpu.SemaphoreType.DMA((2, slots)),
            pltpu.SemaphoreType.DMA((4,)),
        ],
        compiler_params=params,
        name="condense",
    )(
        block_counts,
        *[
            pltpu.with_memory_space_constraint(value, pltpu.HBM)
            for value in (coupling, inverse, stiffness, start, loads)
        ]
    )
    got = exchange(out, rows, columns)
    cost = pl.CostEstimate(flops=8 * width * width * lanes, bytes_accessed=1 << 22, transcendentals=0)
    ready, plain, owned, echo = pl.pallas_call(
        early_kernel,
        out_shape=(field, field, faces, faces),
        in_specs=[vmem] * 9,
        out_specs=(vmem,) * 4,
        compiler_params=params,
        cost_estimate=cost,
        name="early",
    )(high, low, start, loads, rest, *out)
    ahead, fix2, fix3, *out = pl.pallas_call(
        sweep_kernel,
        out_shape=(field, faces, faces, message, message, message, message),
        in_specs=[vmem] * 10,
        out_specs=(vmem,) * 7,
        compiler_params=params,
        name="sweep",
    )(high, low, ready, plain, owned, echo, *got)
    got = exchange(out, rows, columns)
    left = pl.pallas_call(
        late_kernel,
        out_shape=field,
        in_specs=[vmem] * 4,
        out_specs=vmem,
        compiler_params=params,
        cost_estimate=cost,
        name="late",
    )(high, low, loads, ahead)
    traces, residual = pl.pallas_call(
        final_kernel,
        out_shape=(field, field),
        in_specs=[vmem] * 10,
        out_specs=(pl.BlockSpec(memory_space=pltpu.HBM),) * 2,
        scratch_shapes=[
            pltpu.VMEM((width, lanes), f32),
            pltpu.VMEM((width, lanes), f32),
            pltpu.SemaphoreType.DMA((1 + width // TILE,)),
        ],
        compiler_params=params,
        name="final",
    )(high, low, ahead, left, fix2, fix3, *got)
    return traces[None, None], residual[None, None]


def solution(mesh):
    cells = P("gx", ("gy", "ha"))
    return jax.shard_map(
        on_device, mesh=mesh, in_specs=(cells,) * 6, out_specs=(cells, cells), check_vma=False
    )
```

time: 43.7 us -> 41.1 us (0.941); the launches traced: 44.1 us -> 40.8 us
  starting transfers between devices: 24.2 us -> 21.6 us
    ppermute x8, starting transfers between devices: 24.2 us -> 21.6 us  [swap(): return lax.ppermute(block.astype(jnp.float16), axes, route).astype(f32)]
    pallas_call x1, Pallas kernels: 3.52 us -> 2.4 us  [on_device(): pl.pallas_call(sweep_kernel, out_shape=(field, faces, faces, message, mes...]
    pallas_call x1 -> x3, Pallas kernels: 2.17 us -> 2.99 us  [the longest x1 1.36 us: on_device(): pl.pallas_call(final_kernel, out_shape=(field, field), in_specs=[vmem] *...]
  transfers between devices with their start and end apart: 8 -> 8, of which waited for: 4 -> 5; matrix products, arithmetic and copies ran while one was open for 0% -> 0% of each run, Pallas kernels for 0% -> 4%
where the time goes in v4:
time: 41.1 us; the launch traced here: 40.8 us
  starting transfers between devices  21.6 us (53%)
  Pallas kernels  10.3 us (25%)
  waiting for transfers between devices  7.19 us (17%)
  between operations  1.44 us (4%)
    ppermute x8, starting transfers between devices, swap(): return lax.ppermute(block.astype(jnp.float16), axes, route).astype(f32)  21.6 us
    ppermute x8, waiting for transfers between devices, swap(): return lax.ppermute(block.astype(jnp.float16), axes, route).astype(f32)  7.19 us
    pallas_call x1, Pallas kernels, on_device(): pl.pallas_call(condense_kernel, out_shape=(square, square, field, field,...  4.92 us
    pallas_call x1, Pallas kernels, on_device(): pl.pallas_call(sweep_kernel, out_shape=(field, faces, faces, message, mes...  2.4 us
    pallas_call x1, Pallas kernels, on_device(): pl.pallas_call(final_kernel, out_shape=(field, field), in_specs=[vmem] *...  1.36 us
    pallas_call x1, Pallas kernels, on_device(): pl.pallas_call(early_kernel, out_shape=(field, field, faces, faces), in_s...  0.85 us
  transfers between devices with their start and end apart: 8, of which 5 were waited for; matrix products, arithmetic and copies ran while one was open for 0% of the time, Pallas kernels for 4%

profile of v4, /device:TPU:1, one launch (start us, length us, event | category | flops | bytes accessed | tf_op | source)
XLA Modules:
  0.0 40.8 jit_solution(17973924712659580750)
XLA Ops:
  1.3 4.9 %condense.1 = (bf16[768,768]{1,0:T(8,128)(2,1)S(1)}, bf16[768,768]{1,0:T(8,128)(2,1)S(1)}, f32[768,128]{1,0:T(8,128)S(1)}, f32[768,128]{1,0:T(8,128)S(1)}, f32[7...) custom-call(s32[1,1]{1,0:T(1,128)S(6)} %copy.8.counts, ...), custom_call_target="tpu_custom_call" | custom-call | tf_op jit(solution)/shard_map/condense/pallas_call | solution.py:312
  6.2 11.1 %collective-permute-start.3 = (f16[264,128]{1,0:T(8,128)(2,1)S(1)}, f16[264,128]{1,0:T(8,128)(2,1)S(1)}, u32[]{:S(2)}, u32[]{:S(2)}) collective-permute-start(f16[264,128]{1,0:T(8,128)(2,1)S(1)} %convert_element_type.54), channel_id=1, source_target_pairs={{16,32},{32,16},{48,64},{64,48},{80,96},{96,80},{112,128},{128,112... | collective-permute-start | bytes 202760 | tf_op jit(solution)/shard_map/ppermute | solution.py:284
  17.3 0.1 collective-permute-start.2
  17.5 2.9 %collective-permute-start.1 = (f16[264,128]{1,0:T(8,128)(2,1)S(1)}, f16[264,128]{1,0:T(8,128)(2,1)S(1)}, u32[]{:S(2)}, u32[]{:S(2)}) collective-permute-start(f16[264,128]{1,0:T(8,128)(2,1)S(1)} %convert_element_type.50), channel_id=1, source_target_pairs={{0,1},{1,0},{2,3},{3,2},{4,5},{5,4},{6,7},{7,6},{8,9},{9,8},{10,11... | collective-permute-start | bytes 202760 | tf_op jit(solution)/shard_map/ppermute | solution.py:284
  20.4 0.5 %collective-permute-start = (f16[264,128]{1,0:T(8,128)(2,1)S(1)}, f16[264,128]{1,0:T(8,128)(2,1)S(1)}, u32[]{:S(2)}, u32[]{:S(2)}) collective-permute-start(f16[264,128]{1,0:T(8,128)(2,1)S(1)} %convert_element_type.48), channel_id=1, source_target_pairs={{1,2},{2,1},{3,4},{4,3},{5,6},{6,5},{7,8},{8,7},{9,10},{10,9},{11,... | collective-permute-start | bytes 202760 | tf_op jit(solution)/shard_map/ppermute | solution.py:284
  20.9 0.9 %early.1 = (f32[768,128]{1,0:T(8,128)S(1)}, f32[768,128]{1,0:T(8,128)S(1)}, f32[512,128]{1,0:T(8,128)S(1)}, f32[512,128]{1,0:T(8,128)S(1)}) custom-call(bf16[768,768]{1,0:T(8,128)(2,1)S(1)} %get-tuple-element.24.high, bf16[768,768]{1,0:T(8,128)(2,1)S(1)} %get-tuple-element.25.low, f32[768,128]{1,0:T(8,128)S(1)} %get-tuple-element.26.start, ...), custom_call_target="tpu_custom_call" | custom-call | flops 603979776 | bytes 4194304 | tf_op jit(solution)/shard_map/early/pallas_call | solution.py:338
  21.8 0.0 collective-permute-done.3
  21.8 1.1 %collective-permute-done.2 = f16[264,128]{1,0:T(8,128)(2,1)S(1)} collective-permute-done((f16[264,128]{1,0:T(8,128)(2,1)S(1)}, f16[264,128]{1,0:T(8,128)(2,1)S(1)}, u32[]{:S(2)}, u32[]{:S(2)}) %collective-permute-start.2) | collective-permute-done | bytes 67616 | tf_op jit(solution)/shard_map/ppermute | solution.py:284
  22.9 0.3 collective-permute-done.1
  23.3 2.3 %collective-permute-done = f16[264,128]{1,0:T(8,128)(2,1)S(1)} collective-permute-done((f16[264,128]{1,0:T(8,128)(2,1)S(1)}, f16[264,128]{1,0:T(8,128)(2,1)S(1)}, u32[]{:S(2)}, u32[]{:S(2)}) %collective-permute-start) | collective-permute-done | bytes 67616 | tf_op jit(solution)/shard_map/ppermute | solution.py:284
  25.6 2.4 %sweep.1 = (f32[768,128]{1,0:T(8,128)S(1)}, f32[512,128]{1,0:T(8,128)S(1)}, f32[512,128]{1,0:T(8,128)S(1)}, f32[264,128]{1,0:T(8,128)S(1)}, f32[264,128]{1,0:T(8...) custom-call(bf16[768,768]{1,0:T(8,128)(2,1)S(1)} %get-tuple-element.24.high, ...), custom_call_target="tpu_custom_call" | custom-call | tf_op jit(solution)/shard_map/sweep/pallas_call | solution.py:347
  28.0 3.3 %collective-permute-start.7 = (f16[264,128]{1,0:T(8,128)(2,1)S(1)}, f16[264,128]{1,0:T(8,128)(2,1)S(1)}, u32[]{:S(2)}, u32[]{:S(2)}) collective-permute-start(f16[264,128]{1,0:T(8,128)(2,1)S(1)} %convert_element_type.62), channel_id=1, source_target_pairs={{16,32},{32,16},{48,64},{64,48},{80,96},{96,80},{112,128},{128,112... | collective-permute-start | bytes 202760 | tf_op jit(solution)/shard_map/ppermute | solution.py:284
  31.4 0.1 collective-permute-start.6
  31.5 1.1 %collective-permute-start.5 = (f16[264,128]{1,0:T(8,128)(2,1)S(1)}, f16[264,128]{1,0:T(8,128)(2,1)S(1)}, u32[]{:S(2)}, u32[]{:S(2)}) collective-permute-start(f16[264,128]{1,0:T(8,128)(2,1)S(1)} %convert_element_type.58), channel_id=1, source_target_pairs={{0,1},{1,0},{2,3},{3,2},{4,5},{5,4},{6,7},{7,6},{8,9},{9,8},{10,11... | collective-permute-start | bytes 202760 | tf_op jit(solution)/shard_map/ppermute | solution.py:284
  32.6 2.5 %collective-permute-start.4 = (f16[264,128]{1,0:T(8,128)(2,1)S(1)}, f16[264,128]{1,0:T(8,128)(2,1)S(1)}, u32[]{:S(2)}, u32[]{:S(2)}) collective-permute-start(f16[264,128]{1,0:T(8,128)(2,1)S(1)} %convert_element_type.56), channel_id=1, source_target_pairs={{1,2},{2,1},{3,4},{4,3},{5,6},{6,5},{7,8},{8,7},{9,10},{10,9},{11,... | collective-permute-start | bytes 202760 | tf_op jit(solution)/shard_map/ppermute | solution.py:284
  35.1 0.8 %late.1.left = f32[768,128]{1,0:T(8,128)S(1)} custom-call(bf16[768,768]{1,0:T(8,128)(2,1)S(1)} %get-tuple-element.24.high, bf16[768,768]{1,0:T(8,128)(2,1)S(1)} %get-tuple-element.25.low, f32[768,128]{1,0:T(8,128)S(1)} %get-tuple-element.27.loads, f32[768,128]{1,0:T(8,128)S(1)} %get-tuple-element.37.ahead), custom_call_target="tpu_custom_call" | custom-call | flops 603979776 | bytes 4194304 | tf_op jit(solution)/shard_map/late/pallas_call | solution.py:356
  35.8 0.0 collective-permute-done.7
  35.9 0.0 collective-permute-done.6
  35.9 0.4 collective-permute-done.5
  36.3 3.1 %collective-permute-done.4 = f16[264,128]{1,0:T(8,128)(2,1)S(1)} collective-permute-done((f16[264,128]{1,0:T(8,128)(2,1)S(1)}, f16[264,128]{1,0:T(8,128)(2,1)S(1)}, u32[]{:S(2)}, u32[]{:S(2)}) %collective-permute-start.4) | collective-permute-done | bytes 67616 | tf_op jit(solution)/shard_map/ppermute | solution.py:284
  39.4 1.4 %final.1 = (f32[768,128]{1,0:T(8,128)}, f32[768,128]{1,0:T(8,128)}) custom-call(bf16[768,768]{1,0:T(8,128)(2,1)S(1)} %get-tuple-element.24.high, bf16[768,768]{1,0:T(8,128)(2,1)S(1)} %get-tuple-element.25.low, f32[768,128]{1,0:T(8,128)S(1)} %get-tuple-element.37.ahead, f32[768,128]{1,0:T(8,128)S(1)} %late.1.left, f32[512,128]{1,0:T(8,128)S(1)} %get-tuple-element.38.fix2, ...), custom_call_target="tpu_custom_call" | custom-call | tf_op jit(solution)/shard_map/final/pallas_call | solution.py:365
  (16 shorter events, 0.2 us)
Async XLA Ops:
  6.2 15.6 %collective-permute-start.3 = (f16[264,128]{1,0:T(8,128)(2,1)S(1)}, f16[264,128]{1,0:T(8,128)(2,1)S(1)}, u32[]{:S(2)}, u32[]{:S(2)}) collective-permute-start(f16[264,128]{1,0:T(8,128)(2,1)S(1)} %convert_element_type.54), channel_id=1, source_target_pairs={{16,32},{32,16},{48,64},{64,48},{80,96},{96,80},{112,128},{128,112... | collective-permute-start | bytes 202760 | tf_op jit(solution)/shard_map/ppermute | solution.py:284
  17.3 5.6 %collective-permute-start.2 = (f16[264,128]{1,0:T(8,128)(2,1)S(1)}, f16[264,128]{1,0:T(8,128)(2,1)S(1)}, u32[]{:S(2)}, u32[]{:S(2)}) collective-permute-start(f16[264,128]{1,0:T(8,128)(2,1)S(1)} %convert_element_type.52), channel_id=1, source_target_pairs={{0,16},{16,0},{32,48},{48,32},{64,80},{80,64},{96,112},{112,96},{1... | collective-permute-start | bytes 202760 | tf_op jit(solution)/shard_map/ppermute | solution.py:284
  17.5 5.8 %collective-permute-start.1 = (f16[264,128]{1,0:T(8,128)(2,1)S(1)}, f16[264,128]{1,0:T(8,128)(2,1)S(1)}, u32[]{:S(2)}, u32[]{:S(2)}) collective-permute-start(f16[264,128]{1,0:T(8,128)(2,1)S(1)} %convert_element_type.50), channel_id=1, source_target_pairs={{0,1},{1,0},{2,3},{3,2},{4,5},{5,4},{6,7},{7,6},{8,9},{9,8},{10,11... | collective-permute-start | bytes 202760 | tf_op jit(solution)/shard_map/ppermute | solution.py:284
  20.4 5.2 %collective-permute-start = (f16[264,128]{1,0:T(8,128)(2,1)S(1)}, f16[264,128]{1,0:T(8,128)(2,1)S(1)}, u32[]{:S(2)}, u32[]{:S(2)}) collective-permute-start(f16[264,128]{1,0:T(8,128)(2,1)S(1)} %convert_element_type.48), channel_id=1, source_target_pairs={{1,2},{2,1},{3,4},{4,3},{5,6},{6,5},{7,8},{8,7},{9,10},{10,9},{11,... | collective-permute-start | bytes 202760 | tf_op jit(solution)/shard_map/ppermute | solution.py:284
  28.0 7.8 %collective-permute-start.7 = (f16[264,128]{1,0:T(8,128)(2,1)S(1)}, f16[264,128]{1,0:T(8,128)(2,1)S(1)}, u32[]{:S(2)}, u32[]{:S(2)}) collective-permute-start(f16[264,128]{1,0:T(8,128)(2,1)S(1)} %convert_element_type.62), channel_id=1, source_target_pairs={{16,32},{32,16},{48,64},{64,48},{80,96},{96,80},{112,128},{128,112... | collective-permute-start | bytes 202760 | tf_op jit(solution)/shard_map/ppermute | solution.py:284
  31.4 4.5 %collective-permute-start.6 = (f16[264,128]{1,0:T(8,128)(2,1)S(1)}, f16[264,128]{1,0:T(8,128)(2,1)S(1)}, u32[]{:S(2)}, u32[]{:S(2)}) collective-permute-start(f16[264,128]{1,0:T(8,128)(2,1)S(1)} %convert_element_type.60), channel_id=1, source_target_pairs={{0,16},{16,0},{32,48},{48,32},{64,80},{80,64},{96,112},{112,96},{1... | collective-permute-start | bytes 202760 | tf_op jit(solution)/shard_map/ppermute | solution.py:284
  31.5 4.8 %collective-permute-start.5 = (f16[264,128]{1,0:T(8,128)(2,1)S(1)}, f16[264,128]{1,0:T(8,128)(2,1)S(1)}, u32[]{:S(2)}, u32[]{:S(2)}) collective-permute-start(f16[264,128]{1,0:T(8,128)(2,1)S(1)} %convert_element_type.58), channel_id=1, source_target_pairs={{0,1},{1,0},{2,3},{3,2},{4,5},{5,4},{6,7},{7,6},{8,9},{9,8},{10,11... | collective-permute-start | bytes 202760 | tf_op jit(solution)/shard_map/ppermute | solution.py:284
  32.6 6.8 %collective-permute-start.4 = (f16[264,128]{1,0:T(8,128)(2,1)S(1)}, f16[264,128]{1,0:T(8,128)(2,1)S(1)}, u32[]{:S(2)}, u32[]{:S(2)}) collective-permute-start(f16[264,128]{1,0:T(8,128)(2,1)S(1)} %convert_element_type.56), channel_id=1, source_target_pairs={{1,2},{2,1},{3,4},{4,3},{5,6},{6,5},{7,8},{8,7},{9,10},{10,9},{11,... | collective-permute-start | bytes 202760 | tf_op jit(solution)/shard_map/ppermute | solution.py:284

commit v5 on v4

--- a/solution.py
+++ b/solution.py
@@ -30,10 +30,10 @@
     return high, (value - high.astype(f32)).astype(bf16)
 
 
-def times(high_ref, low_ref, traces):
+def times(high_ref, low_ref, traces, at=0):
     high, low = split(traces)
     both = jnp.concatenate([high, low], axis=1)
-    cols = slice(0, traces.shape[0])
+    cols = slice(at, at + traces.shape[0])
     out = jnp.dot(high_ref[:, cols], both, preferred_element_type=f32)
     out = out + jnp.dot(low_ref[:, cols], both, preferred_element_type=f32)
     return out[:, : traces.shape[1]] + out[:, traces.shape[1] :]
@@ -58,17 +58,6 @@
     column = lax.axis_index("gy") * lax.axis_size("ha") + lax.axis_index("ha")
     there = (row > 0, row + 1 < rows, column > 0, column + 1 < columns)
     return (lax.rem(row, 2), lax.rem(column, 2)) + tuple(jnp.where(t, 1.0, 0.0) for t in there)
-
-
-def by_face(info, of_permutes):
-    odd_row, odd_col = info[0] == 1, info[1] == 1
-    cols_odd, cols_even, rows_even, rows_odd = of_permutes
-    return (
-        jnp.where(odd_row, rows_even, rows_odd),
-        jnp.where(odd_row, rows_odd, rows_even),
-        jnp.where(odd_col, cols_even, cols_odd),
-        jnp.where(odd_col, cols_odd, cols_even),
-    )
 
 
 def by_permute(info, of_faces):
@@ -82,17 +71,19 @@
     )
 
 
-def unpack(info, messages, bias, mask):
+def unpack(info, axis, even, odd, bias, mask):
+    odd_place = info[axis] == 1
+    even, odd = even[...], odd[...]
     first, second = [], []
-    for k, part in enumerate(by_face(info, [msg[...] for msg in messages])):
-        back = jnp.exp2(part[2 * FACE : 2 * FACE + 1] - bias)
-        one = part[:FACE]
-        if mask:
-            alive = info[2 + k]
-            one, back = alive * one, alive * back
-        first.append(one)
-        second.append(part[FACE : 2 * FACE] * back)
-    return first, second
+    for k, part in enumerate((jnp.where(odd_place, even, odd), jnp.where(odd_place, odd, even))):
+        back = jnp.exp2(part[2 * FACE : 2 * FACE + 1] - bias[1])
+        there = jnp.exp2(part[2 * FACE : 2 * FACE + 1] - bias[0]) if bias[0] else None
+        one = part[:FACE] * there if bias[0] else part[:FACE]
+        two = part[FACE : 2 * FACE] * back
+        alive = info[2 + 2 * axis + k]
+        first.append(alive * one if mask else one)
+        second.append(alive * two if mask else two)
+    return jnp.concatenate(first, axis=0), jnp.concatenate(second, axis=0)
 
 
 def pack(info, messages, first, second, power):
@@ -136,9 +127,6 @@
     live.start()
     for copy in fetch(0):
         copy.start()
-    for copy in side:
-        copy.start()
-
     for j in range(tiles):
         rows, cols = slice(0, (j + 1) * TILE), slice(j * TILE, (j + 1) * TILE)
         acc[rows, cols] = jnp.zeros(((j + 1) * TILE, TILE), f32)
@@ -154,6 +142,11 @@
         @pl.when(slot + 1 < blocks)
         def _():
             for copy in fetch(slot + 1):
+                copy.start()
+
+        @pl.when(slot == 0)
+        def _():
+            for copy in side:
                 copy.start()
 
         c_ref, i_ref = c_buf.at[slot], i_buf.at[slot]
@@ -199,25 +192,36 @@
     left = loads[...] - times(high, low, moved) - 2.0 * moved
     ready[...] = moved + (keep[0] / centre) * rest[...] + gain[0] * left
     plain[...] = gain[1] * loads[...] - keep[1] * moved
-    first, second = unpack(info, (sent_a, sent_b, sent_c, sent_d), 13.0, False)
-    first = jnp.concatenate(first, axis=0)
-    owned[...] = first + jnp.concatenate(second, axis=0)
-    echo[...] = alive_faces(info, (2.0 / centre) * first)
+    across, along = slice(0, 2 * FACE), slice(2 * FACE, 4 * FACE)
+    for axis, faces, even, odd in ((0, across, sent_c, sent_d), (1, along, sent_b, sent_a)):
+        first, second = unpack(info, axis, even, odd, (0, 13.0), False)
+        owned[faces] = first + second
+        for k in range(2):
+            face = slice((2 * axis + k) * FACE, (2 * axis + k + 1) * FACE)
+            echo[face] = ((2.0 / centre) * info[2 + 2 * axis + k]) * first[k * FACE : (k + 1) * FACE]
+
+
+def rows_kernel(high, low, ready, got_c, got_d, half, v0_rows, v1_rows):
+    info = place()
+    first, second = unpack(info, 0, got_c, got_d, (0, 13.0), True)
+    v0_rows[...] = first
+    v1_rows[...] = first + second
+    half[...] = ready[...] - (2.0 * gain[0] / centre) * times(high, low, first)
 
 
 def sweep_kernel(
-    high, low, ready, plain, owned, echo, got_a, got_b, got_c, got_d,
+    high, low, half, plain, owned, echo, v0_rows, v1_rows, got_a, got_b,
     ahead, fix2, fix3, msg_a, msg_b, msg_c, msg_d,
 ):
     info = place()
     edges = 4 * FACE
     step = 2.0 / centre
-    first, second = unpack(info, (got_a, got_b, got_c, got_d), 13.0, True)
-    v0 = jnp.concatenate(first, axis=0)
-    pushed = times(high, low, v0)
-    v1 = v0 + jnp.concatenate(second, axis=0) + echo[...]
+    first, second = unpack(info, 1, got_b, got_a, (0, 13.0), True)
+    pushed = times(high, low, first, 2 * FACE)
+    v0 = jnp.concatenate([v0_rows[...], first], axis=0)
+    v1 = jnp.concatenate([v1_rows[...], first + second], axis=0) + echo[...]
     own = owned[...] + step * v0
-    half_way = ready[...] - (gain[0] * step) * pushed
+    half_way = half[...] - (gain[0] * step) * pushed
     x2p = half_way[:edges] + (step * (1.0 + keep[0] - 2.0 * gain[0])) * v0
     x2 = jnp.concatenate([x2p + (2.0 * gain[0]) * v1, half_way[edges:]], axis=0)
     pushed = times(high, low, x2)
@@ -242,33 +246,39 @@
     left[...] = loads[...] - times(high, low, moved) - 2.0 * moved
 
 
+def near_kernel(high, low, left, fix2, fix3, got_c, got_d, part, v2_rows):
+    info = place()
+    across = slice(0, 2 * FACE)
+    first, second = unpack(info, 0, got_c, got_d, (12.0, 12.0), True)
+    there = first + fix2[across]
+    v2_rows[...] = there
+    pushed = left[...] - (2.0 * gain[1]) * times(high, low, there)
+    part[across] = pushed[across] + 2.0 * (there + second + fix3[across]) - (4.0 * gain[1]) * there
+    part[2 * FACE :] = pushed[2 * FACE :]
+
+
 def final_kernel(
-    high, low, ahead, left, fix2, fix3, got_a, got_b, got_c, got_d,
+    got_a, got_b, high, low, ahead, part, v2_rows, fix2, fix3,
     traces, residual, x3, r3, sems,
 ):
     info = place()
-    edges = 4 * FACE
-    first, second = unpack(info, (got_a, got_b, got_c, got_d), 12.0, True)
-    scaled = [
-        part[2 * FACE : 2 * FACE + 1]
-        for part in by_face(info, [got[...] for got in (got_a, got_b, got_c, got_d)])
-    ]
-    there = jnp.concatenate(
-        [one * jnp.exp2(power - 12.0) for one, power in zip(first, scaled)], axis=0
-    )
-    there = there + fix2[...]
-    v3 = there + jnp.concatenate(second, axis=0) + fix3[...]
-    x3[:edges] = ahead[:edges] + (2.0 * gain[1]) * there
-    x3[edges:] = ahead[edges:]
+    across, along = slice(0, 2 * FACE), slice(2 * FACE, 4 * FACE)
+    first, second = unpack(info, 1, got_b, got_a, (12.0, 12.0), True)
+    there = first + fix2[along]
+    v3 = there + second + fix3[along]
+    x3[across] = ahead[across] + (2.0 * gain[1]) * v2_rows[...]
+    x3[along] = ahead[along] + (2.0 * gain[1]) * there
+    x3[4 * FACE :] = ahead[4 * FACE :]
     first = pltpu.make_async_copy(x3, traces, sems.at[0])
     first.start()
     copies = [first]
-    for i in range(left.shape[0] // TILE):
+    for i in range(part.shape[0] // TILE):
         rows = slice(i * TILE, (i + 1) * TILE)
-        part = left[rows] - (2.0 * gain[1]) * times(high.at[rows], low.at[rows], there)
-        if i * TILE < edges:
-            part = part + 2.0 * v3[rows] - (4.0 * gain[1]) * there[rows]
-        r3[rows] = part
+        pushed = times(high.at[rows], low.at[rows], there, 2 * FACE)
+        value = part[rows] - (2.0 * gain[1]) * pushed
+        if rows == along:
+            value = value + 2.0 * v3 - (4.0 * gain[1]) * there
+        r3[rows] = value
         copies.append(pltpu.make_async_copy(r3.at[rows], residual.at[rows], sems.at[1 + i]))
         copies[-1].start()
     for copy in copies:
@@ -306,6 +316,7 @@
     square = jax.ShapeDtypeStruct((width, width), bf16)
     field = jax.ShapeDtypeStruct((width, lanes), f32)
     faces = jax.ShapeDtypeStruct((4 * FACE, lanes), f32)
+    pair = jax.ShapeDtypeStruct((2 * FACE, lanes), f32)
     message = jax.ShapeDtypeStruct((2 * FACE + EXTRA, lanes), f32)
     params = pltpu.CompilerParams(vmem_limit_bytes=VMEM_LIMIT)
 
@@ -344,6 +355,15 @@
         cost_estimate=cost,
         name="early",
     )(high, low, start, loads, rest, *out)
+    half_way, v0_rows, v1_rows = pl.pallas_call(
+        rows_kernel,
+        out_shape=(field, pair, pair),
+        in_specs=[vmem] * 5,
+        out_specs=(vmem,) * 3,
+        compiler_params=params,
+        cost_estimate=cost,
+        name="rows",
+    )(high, low, ready, *got[2:])
     ahead, fix2, fix3, *out = pl.pallas_call(
         sweep_kernel,
         out_shape=(field, faces, faces, message, message, message, message),
@@ -351,7 +371,7 @@
         out_specs=(vmem,) * 7,
         compiler_params=params,
         name="sweep",
-    )(high, low, ready, plain, owned, echo, *got)
+    )(high, low, half_way, plain, owned, echo, v0_rows, v1_rows, *got[:2])
     got = exchange(out, rows, columns)
     left = pl.pallas_call(
         late_kernel,
@@ -362,10 +382,19 @@
         cost_estimate=cost,
         name="late",
     )(high, low, loads, ahead)
+    part, v2_rows = pl.pallas_call(
+        near_kernel,
+        out_shape=(field, pair),
+        in_specs=[vmem] * 7,
+        out_specs=(vmem,) * 2,
+        compiler_params=params,
+        cost_estimate=cost,
+        name="near",
+    )(high, low, left, fix2, fix3, *got[2:])
     traces, residual = pl.pallas_call(
         final_kernel,
         out_shape=(field, field),
-        in_specs=[vmem] * 10,
+        in_specs=[vmem] * 9,
         out_specs=(pl.BlockSpec(memory_space=pltpu.HBM),) * 2,
         scratch_shapes=[
             pltpu.VMEM((width, lanes), f32),
@@ -374,7 +403,7 @@
         ],
         compiler_params=params,
         name="final",
-    )(high, low, ahead, left, fix2, fix3, *got)
+    )(*got[:2], high, low, ahead, part, v2_rows, fix2, fix3)
     return traces[None, None], residual[None, None]
 
 

time: 41.1 us -> 39.5 us (0.961)
  starting transfers between devices: 21.6 us -> 20.1 us
  waiting for transfers between devices: 7.19 us -> 6.23 us
  Pallas kernels: 10.3 us -> 11.1 us
    ppermute x8, starting transfers between devices: 21.6 us -> 20.1 us  [swap(): return lax.ppermute(block.astype(jnp.float16), axes, route).astype(f32)]
    ppermute x8, waiting for transfers between devices: 7.19 us -> 6.23 us  [swap(): return lax.ppermute(block.astype(jnp.float16), axes, route).astype(f32)]
    pallas_call x0 -> x2, Pallas kernels: none -> 0.83 us  [the longest x1 0.42 us: on_device(): pl.pallas_call(near_kernel, out_shape=(field, pair), in_specs=[vmem] * 7,...]
    pallas_call x1, Pallas kernels: 4.92 us -> 5.57 us  [on_device(): pl.pallas_call(condense_kernel, out_shape=(square, square, field, field,...]
    pallas_call x1, Pallas kernels: 2.4 us -> 1.9 us  [on_device(): pl.pallas_call(sweep_kernel, out_shape=(field, faces, faces, message, mes...]
  transfers between devices with their start and end apart: 8 -> 8, of which waited for: 5 -> 5; matrix products, arithmetic and copies ran while one was open for 0% -> 0% of each run, Pallas kernels for 4% -> 6%
where the time goes in v5:
time: 39.5 us; the launch traced here: 39.1 us
  starting transfers between devices  20.1 us (51%)
  Pallas kernels  11.1 us (28%)
  waiting for transfers between devices  6.23 us (16%)
  between operations  1.46 us (4%)
    ppermute x8, starting transfers between devices, swap(): return lax.ppermute(block.astype(jnp.float16), axes, route).astype(f32)  20.1 us
    ppermute x8, waiting for transfers between devices, swap(): return lax.ppermute(block.astype(jnp.float16), axes, route).astype(f32)  6.23 us
    pallas_call x1, Pallas kernels, on_device(): pl.pallas_call(condense_kernel, out_shape=(square, square, field, field,...  5.57 us
    pallas_call x1, Pallas kernels, on_device(): pl.pallas_call(sweep_kernel, out_shape=(field, faces, faces, message, mes...  1.9 us
    pallas_call x1, Pallas kernels, on_device(): pl.pallas_call(final_kernel, out_shape=(field, field), in_specs=[vmem] *...  1.22 us
    pallas_call x1, Pallas kernels, on_device(): pl.pallas_call(early_kernel, out_shape=(field, field, faces, faces), in_s...  0.85 us
  transfers between devices with their start and end apart: 8, of which 5 were waited for; matrix products, arithmetic and copies ran while one was open for 0% of the time, Pallas kernels for 6%

profile of v5, /device:TPU:1, one launch (start us, length us, event | category | flops | bytes accessed | tf_op | source)
XLA Modules:
  0.0 39.1 jit_solution(3451945684273829528)
XLA Ops:
  1.3 5.6 %condense.1 = (bf16[768,768]{1,0:T(8,128)(2,1)S(1)}, bf16[768,768]{1,0:T(8,128)(2,1)S(1)}, f32[768,128]{1,0:T(8,128)S(1)}, f32[768,128]{1,0:T(8,128)S(1)}, f32[7...) custom-call(s32[1,1]{1,0:T(1,128)S(6)} %copy.8.counts, ...), custom_call_target="tpu_custom_call" | custom-call | tf_op jit(solution)/shard_map/condense/pallas_call | solution.py:323
  6.9 11.9 %collective-permute-start.1 = (f16[264,128]{1,0:T(8,128)(2,1)S(1)}, f16[264,128]{1,0:T(8,128)(2,1)S(1)}, u32[]{:S(2)}, u32[]{:S(2)}) collective-permute-start(f16[264,128]{1,0:T(8,128)(2,1)S(1)} %convert_element_type.50), channel_id=1, source_target_pairs={{16,32},{32,16},{48,64},{64,48},{80,96},{96,80},{112,128},{128,112... | collective-permute-start | bytes 202760 | tf_op jit(solution)/shard_map/ppermute | solution.py:294
  18.8 0.1 collective-permute-start
  18.9 0.1 collective-permute-start.3
  19.0 1.6 %collective-permute-start.2 = (f16[264,128]{1,0:T(8,128)(2,1)S(1)}, f16[264,128]{1,0:T(8,128)(2,1)S(1)}, u32[]{:S(2)}, u32[]{:S(2)}) collective-permute-start(f16[264,128]{1,0:T(8,128)(2,1)S(1)} %convert_element_type.52), channel_id=1, source_target_pairs={{1,2},{2,1},{3,4},{4,3},{5,6},{6,5},{7,8},{8,7},{9,10},{10,9},{11,... | collective-permute-start | bytes 202760 | tf_op jit(solution)/shard_map/ppermute | solution.py:294
  20.7 0.8 %early.1 = (f32[768,128]{1,0:T(8,128)S(1)}, f32[768,128]{1,0:T(8,128)S(1)}, f32[512,128]{1,0:T(8,128)S(1)}, f32[512,128]{1,0:T(8,128)S(1)}) custom-call(bf16[768,768]{1,0:T(8,128)(2,1)S(1)} %get-tuple-element.29.high, bf16[768,768]{1,0:T(8,128)(2,1)S(1)} %get-tuple-element.30.low, f32[768,128]{1,0:T(8,128)S(1)} %get-tuple-element.31.start, ...), custom_call_target="tpu_custom_call" | custom-call | flops 603979776 | bytes 4194304 | tf_op jit(solution)/shard_map/early/pallas_call | solution.py:349
  21.5 0.0 collective-permute-done.1
  21.6 2.1 %collective-permute-done = f16[264,128]{1,0:T(8,128)(2,1)S(1)} collective-permute-done((f16[264,128]{1,0:T(8,128)(2,1)S(1)}, f16[264,128]{1,0:T(8,128)(2,1)S(1)}, u32[]{:S(2)}, u32[]{:S(2)}) %collective-permute-start) | collective-permute-done | bytes 67616 | tf_op jit(solution)/shard_map/ppermute | solution.py:294
  23.7 0.8 %collective-permute-done.3 = f16[264,128]{1,0:T(8,128)(2,1)S(1)} collective-permute-done((f16[264,128]{1,0:T(8,128)(2,1)S(1)}, f16[264,128]{1,0:T(8,128)(2,1)S(1)}, u32[]{:S(2)}, u32[]{:S(2)}) %collective-permute-start.3) | collective-permute-done | bytes 67616 | tf_op jit(solution)/shard_map/ppermute | solution.py:294
  24.5 0.4 %rows.1 = (f32[768,128]{1,0:T(8,128)S(1)}, f32[256,128]{1,0:T(8,128)S(1)}, f32[256,128]{1,0:T(8,128)S(1)}) custom-call(bf16[768,768]{1,0:T(8,128)(2,1)S(1)} %get-tuple-element.29.high, bf16[768,768]{1,0:T(8,128)(2,1)S(1)} %get-tuple-element.30.low, f32[768,128]{1,0:T(8,128)S(1)} %get-tuple-element.38.ready, f32[264,128]{1,0:T(8,128)S(1)} %convert_element_type.49.got_c, ...), custom_call_target="tpu_custom_call" | custom-call | flops 603979776 | bytes 4194304 | tf_op jit(solution)/shard_map/rows/pallas_call | solution.py:358
  24.9 1.0 %collective-permute-done.2 = f16[264,128]{1,0:T(8,128)(2,1)S(1)} collective-permute-done((f16[264,128]{1,0:T(8,128)(2,1)S(1)}, f16[264,128]{1,0:T(8,128)(2,1)S(1)}, u32[]{:S(2)}, u32[]{:S(2)}) %collective-permute-start.2) | collective-permute-done | bytes 67616 | tf_op jit(solution)/shard_map/ppermute | solution.py:294
  25.9 1.9 %sweep.1 = (f32[768,128]{1,0:T(8,128)S(1)}, f32[512,128]{1,0:T(8,128)S(1)}, f32[512,128]{1,0:T(8,128)S(1)}, f32[264,128]{1,0:T(8,128)S(1)}, f32[264,128]{1,0:T(8...) custom-call(bf16[768,768]{1,0:T(8,128)(2,1)S(1)} %get-tuple-element.29.high, ...), custom_call_target="tpu_custom_call" | custom-call | tf_op jit(solution)/shard_map/sweep/pallas_call | solution.py:367
  27.9 2.5 %collective-permute-start.7 = (f16[264,128]{1,0:T(8,128)(2,1)S(1)}, f16[264,128]{1,0:T(8,128)(2,1)S(1)}, u32[]{:S(2)}, u32[]{:S(2)}) collective-permute-start(f16[264,128]{1,0:T(8,128)(2,1)S(1)} %convert_element_type.62), channel_id=1, source_target_pairs={{16,32},{32,16},{48,64},{64,48},{80,96},{96,80},{112,128},{128,112... | collective-permute-start | bytes 202760 | tf_op jit(solution)/shard_map/ppermute | solution.py:294
  30.4 0.0 collective-permute-start.6
  30.4 0.1 collective-permute-start.5
  30.5 3.7 %collective-permute-start.4 = (f16[264,128]{1,0:T(8,128)(2,1)S(1)}, f16[264,128]{1,0:T(8,128)(2,1)S(1)}, u32[]{:S(2)}, u32[]{:S(2)}) collective-permute-start(f16[264,128]{1,0:T(8,128)(2,1)S(1)} %convert_element_type.56), channel_id=1, source_target_pairs={{1,2},{2,1},{3,4},{4,3},{5,6},{6,5},{7,8},{8,7},{9,10},{10,9},{11,... | collective-permute-start | bytes 202760 | tf_op jit(solution)/shard_map/ppermute | solution.py:294
  34.3 0.8 %late.1.left = f32[768,128]{1,0:T(8,128)S(1)} custom-call(bf16[768,768]{1,0:T(8,128)(2,1)S(1)} %get-tuple-element.29.high, bf16[768,768]{1,0:T(8,128)(2,1)S(1)} %get-tuple-element.30.low, f32[768,128]{1,0:T(8,128)S(1)} %get-tuple-element.32.loads, f32[768,128]{1,0:T(8,128)S(1)} %get-tuple-element.47.ahead), custom_call_target="tpu_custom_call" | custom-call | flops 603979776 | bytes 4194304 | tf_op jit(solution)/shard_map/late/pallas_call | solution.py:376
  35.1 1.4 %collective-permute-done.7 = f16[264,128]{1,0:T(8,128)(2,1)S(1)} collective-permute-done((f16[264,128]{1,0:T(8,128)(2,1)S(1)}, f16[264,128]{1,0:T(8,128)(2,1)S(1)}, u32[]{:S(2)}, u32[]{:S(2)}) %collective-permute-start.7) | collective-permute-done | bytes 67616 | tf_op jit(solution)/shard_map/ppermute | solution.py:294
  36.5 0.0 collective-permute-done.6
  36.5 0.0 collective-permute-done.5
  36.5 0.4 %near.1 = (f32[768,128]{1,0:T(8,128)S(1)}, f32[256,128]{1,0:T(8,128)S(1)}) custom-call(bf16[768,768]{1,0:T(8,128)(2,1)S(1)} %get-tuple-element.29.high, bf16[768,768]{1,0:T(8,128)(2,1)S(1)} %get-tuple-element.30.low, f32[768,128]{1,0:T(8,128)S(1)} %late.1.left, f32[512,128]{1,0:T(8,128)S(1)} %get-tuple-element.48.fix2, ...), custom_call_target="tpu_custom_call" | custom-call | flops 603979776 | bytes 4194304 | tf_op jit(solution)/shard_map/near/pallas_call | solution.py:385
  36.9 0.9 %collective-permute-done.4 = f16[264,128]{1,0:T(8,128)(2,1)S(1)} collective-permute-done((f16[264,128]{1,0:T(8,128)(2,1)S(1)}, f16[264,128]{1,0:T(8,128)(2,1)S(1)}, u32[]{:S(2)}, u32[]{:S(2)}) %collective-permute-start.4) | collective-permute-done | bytes 67616 | tf_op jit(solution)/shard_map/ppermute | solution.py:294
  37.9 1.2 %final.1 = (f32[768,128]{1,0:T(8,128)}, f32[768,128]{1,0:T(8,128)}) custom-call(f32[264,128]{1,0:T(8,128)S(1)} %convert_element_type.57.got_a, f32[264,128]{1,0:T(8,128)S(1)} %convert_element_type.59.got_b, bf16[768,768]{1,0:T(8,128)(2,1)S(1)} %get-tuple-element.29.high, bf16[768,768]{1,0:T(8,128)(2,1)S(1)} %get-tuple-element.30.low, ...), custom_call_target="tpu_custom_call" | custom-call | tf_op jit(solution)/shard_map/final/pallas_call | solution.py:394
  (16 shorter events, 0.2 us)
Async XLA Ops:
  6.9 14.7 %collective-permute-start.1 = (f16[264,128]{1,0:T(8,128)(2,1)S(1)}, f16[264,128]{1,0:T(8,128)(2,1)S(1)}, u32[]{:S(2)}, u32[]{:S(2)}) collective-permute-start(f16[264,128]{1,0:T(8,128)(2,1)S(1)} %convert_element_type.50), channel_id=1, source_target_pairs={{16,32},{32,16},{48,64},{64,48},{80,96},{96,80},{112,128},{128,112... | collective-permute-start | bytes 202760 | tf_op jit(solution)/shard_map/ppermute | solution.py:294
  18.8 4.9 %collective-permute-start = (f16[264,128]{1,0:T(8,128)(2,1)S(1)}, f16[264,128]{1,0:T(8,128)(2,1)S(1)}, u32[]{:S(2)}, u32[]{:S(2)}) collective-permute-start(f16[264,128]{1,0:T(8,128)(2,1)S(1)} %convert_element_type.48), channel_id=1, source_target_pairs={{0,16},{16,0},{32,48},{48,32},{64,80},{80,64},{96,112},{112,96},{1... | collective-permute-start | bytes 202760 | tf_op jit(solution)/shard_map/ppermute | solution.py:294
  18.9 5.5 %collective-permute-start.3 = (f16[264,128]{1,0:T(8,128)(2,1)S(1)}, f16[264,128]{1,0:T(8,128)(2,1)S(1)}, u32[]{:S(2)}, u32[]{:S(2)}) collective-permute-start(f16[264,128]{1,0:T(8,128)(2,1)S(1)} %convert_element_type.54), channel_id=1, source_target_pairs={{0,1},{1,0},{2,3},{3,2},{4,5},{5,4},{6,7},{7,6},{8,9},{9,8},{10,11... | collective-permute-start | bytes 202760 | tf_op jit(solution)/shard_map/ppermute | solution.py:294
  19.0 6.9 %collective-permute-start.2 = (f16[264,128]{1,0:T(8,128)(2,1)S(1)}, f16[264,128]{1,0:T(8,128)(2,1)S(1)}, u32[]{:S(2)}, u32[]{:S(2)}) collective-permute-start(f16[264,128]{1,0:T(8,128)(2,1)S(1)} %convert_element_type.52), channel_id=1, source_target_pairs={{1,2},{2,1},{3,4},{4,3},{5,6},{6,5},{7,8},{8,7},{9,10},{10,9},{11,... | collective-permute-start | bytes 202760 | tf_op jit(solution)/shard_map/ppermute | solution.py:294
  27.9 8.6 %collective-permute-start.7 = (f16[264,128]{1,0:T(8,128)(2,1)S(1)}, f16[264,128]{1,0:T(8,128)(2,1)S(1)}, u32[]{:S(2)}, u32[]{:S(2)}) collective-permute-start(f16[264,128]{1,0:T(8,128)(2,1)S(1)} %convert_element_type.62), channel_id=1, source_target_pairs={{16,32},{32,16},{48,64},{64,48},{80,96},{96,80},{112,128},{128,112... | collective-permute-start | bytes 202760 | tf_op jit(solution)/shard_map/ppermute | solution.py:294
  30.4 6.1 %collective-permute-start.6 = (f16[264,128]{1,0:T(8,128)(2,1)S(1)}, f16[264,128]{1,0:T(8,128)(2,1)S(1)}, u32[]{:S(2)}, u32[]{:S(2)}) collective-permute-start(f16[264,128]{1,0:T(8,128)(2,1)S(1)} %convert_element_type.60), channel_id=1, source_target_pairs={{0,16},{16,0},{32,48},{48,32},{64,80},{80,64},{96,112},{112,96},{1... | collective-permute-start | bytes 202760 | tf_op jit(solution)/shard_map/ppermute | solution.py:294
  30.4 6.1 %collective-permute-start.5 = (f16[264,128]{1,0:T(8,128)(2,1)S(1)}, f16[264,128]{1,0:T(8,128)(2,1)S(1)}, u32[]{:S(2)}, u32[]{:S(2)}) collective-permute-start(f16[264,128]{1,0:T(8,128)(2,1)S(1)} %convert_element_type.58), channel_id=1, source_target_pairs={{0,1},{1,0},{2,3},{3,2},{4,5},{5,4},{6,7},{7,6},{8,9},{9,8},{10,11... | collective-permute-start | bytes 202760 | tf_op jit(solution)/shard_map/ppermute | solution.py:294
  30.5 7.3 %collective-permute-start.4 = (f16[264,128]{1,0:T(8,128)(2,1)S(1)}, f16[264,128]{1,0:T(8,128)(2,1)S(1)}, u32[]{:S(2)}, u32[]{:S(2)}) collective-permute-start(f16[264,128]{1,0:T(8,128)(2,1)S(1)} %convert_element_type.56), channel_id=1, source_target_pairs={{1,2},{2,1},{3,4},{4,3},{5,6},{6,5},{7,8},{8,7},{9,10},{10,9},{11,... | collective-permute-start | bytes 202760 | tf_op jit(solution)/shard_map/ppermute | solution.py:294

commit v6 on v5

--- a/solution.py
+++ b/solution.py
@@ -173,12 +173,12 @@
                 high[cols, rows] = mirror_high
                 low[cols, rows] = mirror_low
 
+    edges = 4 * FACE
     x0 = start[...]
-    y0 = loads[...] - times(high, low, x0) - 2.0 * x0
+    y0 = loads[:edges] - times(high.at[:edges], low.at[:edges], x0) - 2.0 * x0[:edges]
     rest[...] = y0
-    edges = 4 * FACE
     first = round_half(x0[:edges])
-    edge = x0[:edges] - first + y0[:edges] * (1.0 / centre)
+    edge = x0[:edges] - first + y0 * (1.0 / centre)
     power = exponent_of(largest(edge))
     second = round_half(edge * jnp.exp2(13.0 - power))
     pack(info, (msg_a, msg_b, msg_c, msg_d), first, second, power)
@@ -188,9 +188,14 @@
     high, low, start, loads, rest, sent_a, sent_b, sent_c, sent_d, ready, plain, owned, echo
 ):
     info = place()
-    moved = start[...] + rest[...] * (1.0 / centre)
-    left = loads[...] - times(high, low, moved) - 2.0 * moved
-    ready[...] = moved + (keep[0] / centre) * rest[...] + gain[0] * left
+    edges = 4 * FACE
+    x0 = start[...]
+    other = loads[edges:] - times(high.at[edges:], low.at[edges:], x0) - 2.0 * x0[edges:]
+    y0 = jnp.concatenate([rest[...], other], axis=0)
+    moved = x0 + y0 * (1.0 / centre)
+    pushed = times(high, low, moved[:edges]) + times(high, low, moved[edges:], edges)
+    left = loads[...] - pushed - 2.0 * moved
+    ready[...] = moved + (keep[0] / centre) * y0 + gain[0] * left
     plain[...] = gain[1] * loads[...] - keep[1] * moved
     across, along = slice(0, 2 * FACE), slice(2 * FACE, 4 * FACE)
     for axis, faces, even, odd in ((0, across, sent_c, sent_d), (1, along, sent_b, sent_a)):
@@ -211,7 +216,7 @@
 
 def sweep_kernel(
     high, low, half, plain, owned, echo, v0_rows, v1_rows, got_a, got_b,
-    ahead, fix2, fix3, msg_a, msg_b, msg_c, msg_d,
+    ahead, middle, fix2, fix3, msg_a, msg_b, msg_c, msg_d,
 ):
     info = place()
     edges = 4 * FACE
@@ -224,13 +229,13 @@
     half_way = half[...] - (gain[0] * step) * pushed
     x2p = half_way[:edges] + (step * (1.0 + keep[0] - 2.0 * gain[0])) * v0
     x2 = jnp.concatenate([x2p + (2.0 * gain[0]) * v1, half_way[edges:]], axis=0)
-    pushed = times(high, low, x2)
+    middle[...] = x2
+    pushed = times(high.at[:edges], low.at[:edges], x2)
     fix2[...] = v1 + (2.0 * gain[0]) * alive_faces(info, own)
     first = x2p - own
-    x3p = (1.0 + keep[1] - 2.0 * gain[1]) * x2 + plain[...] - gain[1] * pushed
-    ahead[edges:] = x3p[edges:]
-    x3p = x3p[:edges] - (keep[1] * step) * v0
-    ahead[:edges] = x3p
+    x3p = (1.0 + keep[1] - 2.0 * gain[1]) * x2[:edges] + plain[:edges] - gain[1] * pushed
+    x3p = x3p - (keep[1] * step) * v0
+    ahead[...] = x3p
     top = jnp.maximum(jnp.abs(first), jnp.abs(x3p - x2[:edges]))
     power = exponent_of(largest(top))
     scale = jnp.exp2(12.0 - power)
@@ -241,9 +246,15 @@
     fix3[...] = (2.0 * gain[1]) * alive_faces(info, known)
 
 
-def late_kernel(high, low, loads, ahead, left):
-    moved = ahead[...]
-    left[...] = loads[...] - times(high, low, moved) - 2.0 * moved
+def late_kernel(high, low, loads, plain, middle, ahead_faces, left, ahead):
+    edges = 4 * FACE
+    x2 = middle[...]
+    pushed = times(high.at[edges:], low.at[edges:], x2)
+    other = (1.0 + keep[1] - 2.0 * gain[1]) * x2[edges:] + plain[edges:] - gain[1] * pushed
+    moved = jnp.concatenate([ahead_faces[...], other], axis=0)
+    ahead[...] = moved
+    pushed = times(high, low, moved[:edges]) + times(high, low, moved[edges:], edges)
+    left[...] = loads[...] - pushed - 2.0 * moved
 
 
 def near_kernel(high, low, left, fix2, fix3, got_c, got_d, part, v2_rows):
@@ -322,7 +333,7 @@
 
     high, low, rest, start, loads, *out = pl.pallas_call(
         condense_kernel,
-        out_shape=(square, square, field, field, field, message, message, message, message),
+        out_shape=(square, square, faces, field, field, message, message, message, message),
         in_specs=[pl.BlockSpec(memory_space=pl.ANY)] + [anywhere] * 5,
         out_specs=(vmem,) * 9,
         scratch_shapes=[
@@ -364,24 +375,24 @@
         cost_estimate=cost,
         name="rows",
     )(high, low, ready, *got[2:])
-    ahead, fix2, fix3, *out = pl.pallas_call(
+    ahead_faces, middle, fix2, fix3, *out = pl.pallas_call(
         sweep_kernel,
-        out_shape=(field, faces, faces, message, message, message, message),
+        out_shape=(faces, field, faces, faces, message, message, message, message),
         in_specs=[vmem] * 10,
-        out_specs=(vmem,) * 7,
+        out_specs=(vmem,) * 8,
         compiler_params=params,
         name="sweep",
     )(high, low, half_way, plain, owned, echo, v0_rows, v1_rows, *got[:2])
     got = exchange(out, rows, columns)
-    left = pl.pallas_call(
+    left, ahead = pl.pallas_call(
         late_kernel,
-        out_shape=field,
-        in_specs=[vmem] * 4,
-        out_specs=vmem,
+        out_shape=(field, field),
+        in_specs=[vmem] * 6,
+        out_specs=(vmem,) * 2,
         compiler_params=params,
         cost_estimate=cost,
         name="late",
-    )(high, low, loads, ahead)
+    )(high, low, loads, plain, middle, ahead_faces)
     part, v2_rows = pl.pallas_call(
         near_kernel,
         out_shape=(field, pair),

time: 39.5 us -> 40.9 us (1.035)
  starting transfers between devices: 20.1 us -> 21.3 us
    ppermute x8, starting transfers between devices: 20.1 us -> 21.3 us  [swap(): return lax.ppermute(block.astype(jnp.float16), axes, route).astype(f32)]
  transfers between devices with their start and end apart: 8 -> 8, of which waited for: 5 -> 6; matrix products, arithmetic and copies ran while one was open for 0% -> 0% of each run, Pallas kernels for 6% -> 8%
where the time goes in v6:
time: 40.9 us; the launch traced here: 40.5 us
  starting transfers between devices  21.3 us (52%)
  Pallas kernels  11.5 us (28%)
  waiting for transfers between devices  6.06 us (15%)
  between operations  1.44 us (4%)
    ppermute x8, starting transfers between devices, swap(): return lax.ppermute(block.astype(jnp.float16), axes, route).astype(f32)  21.3 us
    ppermute x8, waiting for transfers between devices, swap(): return lax.ppermute(block.astype(jnp.float16), axes, route).astype(f32)  6.06 us
    pallas_call x1, Pallas kernels, on_device(): pl.pallas_call(condense_kernel, out_shape=(square, square, faces, field,...  5.49 us
    pallas_call x1, Pallas kernels, on_device(): pl.pallas_call(sweep_kernel, out_shape=(faces, field, faces, faces, messa...  1.67 us
    pallas_call x1, Pallas kernels, on_device(): pl.pallas_call(final_kernel, out_shape=(field, field), in_specs=[vmem] *...  1.22 us
    pallas_call x1, Pallas kernels, on_device(): pl.pallas_call(early_kernel, out_shape=(field, field, faces, faces), in_s...  1.18 us
    pallas_call x1, Pallas kernels, on_device(): pl.pallas_call(late_kernel, out_shape=(field, field), in_specs=[vmem] * 6...  1.14 us
  transfers between devices with their start and end apart: 8, of which 6 were waited for; matrix products, arithmetic and copies ran while one was open for 0% of the time, Pallas kernels for 8%

profile of v6, /device:TPU:1, one launch (start us, length us, event | category | flops | bytes accessed | tf_op | source)
XLA Modules:
  0.0 40.5 jit_solution(15558354201844402318)
XLA Ops:
  1.3 5.5 %condense.1 = (bf16[768,768]{1,0:T(8,128)(2,1)S(1)}, bf16[768,768]{1,0:T(8,128)(2,1)S(1)}, f32[512,128]{1,0:T(8,128)S(1)}, f32[768,128]{1,0:T(8,128)S(1)}, f32[7...) custom-call(s32[1,1]{1,0:T(1,128)S(6)} %copy.8.counts, ...), custom_call_target="tpu_custom_call" | custom-call | tf_op jit(solution)/shard_map/condense/pallas_call | solution.py:334
  6.8 13.6 %collective-permute-start.1 = (f16[264,128]{1,0:T(8,128)(2,1)S(1)}, f16[264,128]{1,0:T(8,128)(2,1)S(1)}, u32[]{:S(2)}, u32[]{:S(2)}) collective-permute-start(f16[264,128]{1,0:T(8,128)(2,1)S(1)} %convert_element_type.50), channel_id=1, source_target_pairs={{16,32},{32,16},{48,64},{64,48},{80,96},{96,80},{112,128},{128,112... | collective-permute-start | bytes 202760 | tf_op jit(solution)/shard_map/ppermute | solution.py:305
  20.4 0.1 collective-permute-start
  20.5 0.1 collective-permute-start.3
  20.7 1.7 %collective-permute-start.2 = (f16[264,128]{1,0:T(8,128)(2,1)S(1)}, f16[264,128]{1,0:T(8,128)(2,1)S(1)}, u32[]{:S(2)}, u32[]{:S(2)}) collective-permute-start(f16[264,128]{1,0:T(8,128)(2,1)S(1)} %convert_element_type.52), channel_id=1, source_target_pairs={{1,2},{2,1},{3,4},{4,3},{5,6},{6,5},{7,8},{8,7},{9,10},{10,9},{11,... | collective-permute-start | bytes 202760 | tf_op jit(solution)/shard_map/ppermute | solution.py:305
  22.3 1.2 %early.1 = (f32[768,128]{1,0:T(8,128)S(1)}, f32[768,128]{1,0:T(8,128)S(1)}, f32[512,128]{1,0:T(8,128)S(1)}, f32[512,128]{1,0:T(8,128)S(1)}) custom-call(bf16[768,768]{1,0:T(8,128)(2,1)S(1)} %get-tuple-element.32.high, bf16[768,768]{1,0:T(8,128)(2,1)S(1)} %get-tuple-element.33.low, f32[768,128]{1,0:T(8,128)S(1)} %get-tuple-element.34.start, ...), custom_call_target="tpu_custom_call" | custom-call | flops 603979776 | bytes 4194304 | tf_op jit(solution)/shard_map/early/pallas_call | solution.py:360
  23.5 0.2 collective-permute-done.1
  23.7 0.9 %collective-permute-done = f16[264,128]{1,0:T(8,128)(2,1)S(1)} collective-permute-done((f16[264,128]{1,0:T(8,128)(2,1)S(1)}, f16[264,128]{1,0:T(8,128)(2,1)S(1)}, u32[]{:S(2)}, u32[]{:S(2)}) %collective-permute-start) | collective-permute-done | bytes 67616 | tf_op jit(solution)/shard_map/ppermute | solution.py:305
  24.7 0.4 collective-permute-done.3
  25.0 0.4 %rows.1 = (f32[768,128]{1,0:T(8,128)S(1)}, f32[256,128]{1,0:T(8,128)S(1)}, f32[256,128]{1,0:T(8,128)S(1)}) custom-call(bf16[768,768]{1,0:T(8,128)(2,1)S(1)} %get-tuple-element.32.high, bf16[768,768]{1,0:T(8,128)(2,1)S(1)} %get-tuple-element.33.low, f32[768,128]{1,0:T(8,128)S(1)} %get-tuple-element.41.ready, f32[264,128]{1,0:T(8,128)S(1)} %convert_element_type.49.got_c, ...), custom_call_target="tpu_custom_call" | custom-call | flops 603979776 | bytes 4194304 | tf_op jit(solution)/shard_map/rows/pallas_call | solution.py:369
  25.5 2.2 %collective-permute-done.2 = f16[264,128]{1,0:T(8,128)(2,1)S(1)} collective-permute-done((f16[264,128]{1,0:T(8,128)(2,1)S(1)}, f16[264,128]{1,0:T(8,128)(2,1)S(1)}, u32[]{:S(2)}, u32[]{:S(2)}) %collective-permute-start.2) | collective-permute-done | bytes 67616 | tf_op jit(solution)/shard_map/ppermute | solution.py:305
  27.6 1.7 %sweep.1 = (f32[512,128]{1,0:T(8,128)S(1)}, f32[768,128]{1,0:T(8,128)S(1)}, f32[512,128]{1,0:T(8,128)S(1)}, f32[512,128]{1,0:T(8,128)S(1)}, f32[264,128]{1,0:T(8...) custom-call(bf16[768,768]{1,0:T(8,128)(2,1)S(1)} %get-tuple-element.32.high, ...), custom_call_target="tpu_custom_call" | custom-call | tf_op jit(solution)/shard_map/sweep/pallas_call | solution.py:378
  29.4 0.9 %collective-permute-start.7 = (f16[264,128]{1,0:T(8,128)(2,1)S(1)}, f16[264,128]{1,0:T(8,128)(2,1)S(1)}, u32[]{:S(2)}, u32[]{:S(2)}) collective-permute-start(f16[264,128]{1,0:T(8,128)(2,1)S(1)} %convert_element_type.62), channel_id=1, source_target_pairs={{16,32},{32,16},{48,64},{64,48},{80,96},{96,80},{112,128},{128,112... | collective-permute-start | bytes 202760 | tf_op jit(solution)/shard_map/ppermute | solution.py:305
  30.2 0.0 collective-permute-start.6
  30.3 2.2 %collective-permute-start.5 = (f16[264,128]{1,0:T(8,128)(2,1)S(1)}, f16[264,128]{1,0:T(8,128)(2,1)S(1)}, u32[]{:S(2)}, u32[]{:S(2)}) collective-permute-start(f16[264,128]{1,0:T(8,128)(2,1)S(1)} %convert_element_type.58), channel_id=1, source_target_pairs={{0,1},{1,0},{2,3},{3,2},{4,5},{5,4},{6,7},{7,6},{8,9},{9,8},{10,11... | collective-permute-start | bytes 202760 | tf_op jit(solution)/shard_map/ppermute | solution.py:305
  32.5 2.7 %collective-permute-start.4 = (f16[264,128]{1,0:T(8,128)(2,1)S(1)}, f16[264,128]{1,0:T(8,128)(2,1)S(1)}, u32[]{:S(2)}, u32[]{:S(2)}) collective-permute-start(f16[264,128]{1,0:T(8,128)(2,1)S(1)} %convert_element_type.56), channel_id=1, source_target_pairs={{1,2},{2,1},{3,4},{4,3},{5,6},{6,5},{7,8},{8,7},{9,10},{10,9},{11,... | collective-permute-start | bytes 202760 | tf_op jit(solution)/shard_map/ppermute | solution.py:305
  35.2 1.1 %late.1 = (f32[768,128]{1,0:T(8,128)S(1)}, f32[768,128]{1,0:T(8,128)S(1)}) custom-call(bf16[768,768]{1,0:T(8,128)(2,1)S(1)} %get-tuple-element.32.high, bf16[768,768]{1,0:T(8,128)(2,1)S(1)} %get-tuple-element.33.low, f32[768,128]{1,0:T(8,128)S(1)} %get-tuple-element.35.loads, f32[768,128]{1,0:T(8,128)S(1)} %get-tuple-element.43.plain, ...), custom_call_target="tpu_custom_call" | custom-call | flops 603979776 | bytes 4194304 | tf_op jit(solution)/shard_map/late/pallas_call | solution.py:387
  36.3 0.6 %collective-permute-done.7 = f16[264,128]{1,0:T(8,128)(2,1)S(1)} collective-permute-done((f16[264,128]{1,0:T(8,128)(2,1)S(1)}, f16[264,128]{1,0:T(8,128)(2,1)S(1)}, u32[]{:S(2)}, u32[]{:S(2)}) %collective-permute-start.7) | collective-permute-done | bytes 67616 | tf_op jit(solution)/shard_map/ppermute | solution.py:305
  36.9 0.0 collective-permute-done.6
  36.9 0.0 collective-permute-done.5
  37.0 0.4 %near.1 = (f32[768,128]{1,0:T(8,128)S(1)}, f32[256,128]{1,0:T(8,128)S(1)}) custom-call(bf16[768,768]{1,0:T(8,128)(2,1)S(1)} %get-tuple-element.32.high, bf16[768,768]{1,0:T(8,128)(2,1)S(1)} %get-tuple-element.33.low, f32[768,128]{1,0:T(8,128)S(1)} %get-tuple-element.53.left, f32[512,128]{1,0:T(8,128)S(1)} %get-tuple-element.54.fix2, ...), custom_call_target="tpu_custom_call" | custom-call | flops 603979776 | bytes 4194304 | tf_op jit(solution)/shard_map/near/pallas_call | solution.py:396
  37.4 1.8 %collective-permute-done.4 = f16[264,128]{1,0:T(8,128)(2,1)S(1)} collective-permute-done((f16[264,128]{1,0:T(8,128)(2,1)S(1)}, f16[264,128]{1,0:T(8,128)(2,1)S(1)}, u32[]{:S(2)}, u32[]{:S(2)}) %collective-permute-start.4) | collective-permute-done | bytes 67616 | tf_op jit(solution)/shard_map/ppermute | solution.py:305
  39.2 1.2 %final.1 = (f32[768,128]{1,0:T(8,128)}, f32[768,128]{1,0:T(8,128)}) custom-call(f32[264,128]{1,0:T(8,128)S(1)} %convert_element_type.57.got_a, f32[264,128]{1,0:T(8,128)S(1)} %convert_element_type.59.got_b, bf16[768,768]{1,0:T(8,128)(2,1)S(1)} %get-tuple-element.32.high, bf16[768,768]{1,0:T(8,128)(2,1)S(1)} %get-tuple-element.33.low, ...), custom_call_target="tpu_custom_call" | custom-call | tf_op jit(solution)/shard_map/final/pallas_call | solution.py:405
  (16 shorter events, 0.2 us)
Async XLA Ops:
  6.8 16.9 %collective-permute-start.1 = (f16[264,128]{1,0:T(8,128)(2,1)S(1)}, f16[264,128]{1,0:T(8,128)(2,1)S(1)}, u32[]{:S(2)}, u32[]{:S(2)}) collective-permute-start(f16[264,128]{1,0:T(8,128)(2,1)S(1)} %convert_element_type.50), channel_id=1, source_target_pairs={{16,32},{32,16},{48,64},{64,48},{80,96},{96,80},{112,128},{128,112... | collective-permute-start | bytes 202760 | tf_op jit(solution)/shard_map/ppermute | solution.py:305
  20.4 4.2 %collective-permute-start = (f16[264,128]{1,0:T(8,128)(2,1)S(1)}, f16[264,128]{1,0:T(8,128)(2,1)S(1)}, u32[]{:S(2)}, u32[]{:S(2)}) collective-permute-start(f16[264,128]{1,0:T(8,128)(2,1)S(1)} %convert_element_type.48), channel_id=1, source_target_pairs={{0,16},{16,0},{32,48},{48,32},{64,80},{80,64},{96,112},{112,96},{1... | collective-permute-start | bytes 202760 | tf_op jit(solution)/shard_map/ppermute | solution.py:305
  20.5 4.5 %collective-permute-start.3 = (f16[264,128]{1,0:T(8,128)(2,1)S(1)}, f16[264,128]{1,0:T(8,128)(2,1)S(1)}, u32[]{:S(2)}, u32[]{:S(2)}) collective-permute-start(f16[264,128]{1,0:T(8,128)(2,1)S(1)} %convert_element_type.54), channel_id=1, source_target_pairs={{0,1},{1,0},{2,3},{3,2},{4,5},{5,4},{6,7},{7,6},{8,9},{9,8},{10,11... | collective-permute-start | bytes 202760 | tf_op jit(solution)/shard_map/ppermute | solution.py:305
  20.7 7.0 %collective-permute-start.2 = (f16[264,128]{1,0:T(8,128)(2,1)S(1)}, f16[264,128]{1,0:T(8,128)(2,1)S(1)}, u32[]{:S(2)}, u32[]{:S(2)}) collective-permute-start(f16[264,128]{1,0:T(8,128)(2,1)S(1)} %convert_element_type.52), channel_id=1, source_target_pairs={{1,2},{2,1},{3,4},{4,3},{5,6},{6,5},{7,8},{8,7},{9,10},{10,9},{11,... | collective-permute-start | bytes 202760 | tf_op jit(solution)/shard_map/ppermute | solution.py:305
  29.4 7.5 %collective-permute-start.7 = (f16[264,128]{1,0:T(8,128)(2,1)S(1)}, f16[264,128]{1,0:T(8,128)(2,1)S(1)}, u32[]{:S(2)}, u32[]{:S(2)}) collective-permute-start(f16[264,128]{1,0:T(8,128)(2,1)S(1)} %convert_element_type.62), channel_id=1, source_target_pairs={{16,32},{32,16},{48,64},{64,48},{80,96},{96,80},{112,128},{128,112... | collective-permute-start | bytes 202760 | tf_op jit(solution)/shard_map/ppermute | solution.py:305
  30.2 6.7 %collective-permute-start.6 = (f16[264,128]{1,0:T(8,128)(2,1)S(1)}, f16[264,128]{1,0:T(8,128)(2,1)S(1)}, u32[]{:S(2)}, u32[]{:S(2)}) collective-permute-start(f16[264,128]{1,0:T(8,128)(2,1)S(1)} %convert_element_type.60), channel_id=1, source_target_pairs={{0,16},{16,0},{32,48},{48,32},{64,80},{80,64},{96,112},{112,96},{1... | collective-permute-start | bytes 202760 | tf_op jit(solution)/shard_map/ppermute | solution.py:305
  30.3 6.7 %collective-permute-start.5 = (f16[264,128]{1,0:T(8,128)(2,1)S(1)}, f16[264,128]{1,0:T(8,128)(2,1)S(1)}, u32[]{:S(2)}, u32[]{:S(2)}) collective-permute-start(f16[264,128]{1,0:T(8,128)(2,1)S(1)} %convert_element_type.58), channel_id=1, source_target_pairs={{0,1},{1,0},{2,3},{3,2},{4,5},{5,4},{6,7},{7,6},{8,9},{9,8},{10,11... | collective-permute-start | bytes 202760 | tf_op jit(solution)/shard_map/ppermute | solution.py:305
  32.5 6.7 %collective-permute-start.4 = (f16[264,128]{1,0:T(8,128)(2,1)S(1)}, f16[264,128]{1,0:T(8,128)(2,1)S(1)}, u32[]{:S(2)}, u32[]{:S(2)}) collective-permute-start(f16[264,128]{1,0:T(8,128)(2,1)S(1)} %convert_element_type.56), channel_id=1, source_target_pairs={{1,2},{2,1},{3,4},{4,3},{5,6},{6,5},{7,8},{8,7},{9,10},{10,9},{11,... | collective-permute-start | bytes 202760 | tf_op jit(solution)/shard_map/ppermute | solution.py:305

commit v7 on v6

--- a/solution.py
+++ b/solution.py
@@ -173,12 +173,12 @@
                 high[cols, rows] = mirror_high
                 low[cols, rows] = mirror_low
 
+    x0 = start[...]
+    y0 = loads[...] - times(high, low, x0) - 2.0 * x0
+    rest[...] = y0
     edges = 4 * FACE
-    x0 = start[...]
-    y0 = loads[:edges] - times(high.at[:edges], low.at[:edges], x0) - 2.0 * x0[:edges]
-    rest[...] = y0
     first = round_half(x0[:edges])
-    edge = x0[:edges] - first + y0 * (1.0 / centre)
+    edge = x0[:edges] - first + y0[:edges] * (1.0 / centre)
     power = exponent_of(largest(edge))
     second = round_half(edge * jnp.exp2(13.0 - power))
     pack(info, (msg_a, msg_b, msg_c, msg_d), first, second, power)
@@ -188,14 +188,9 @@
     high, low, start, loads, rest, sent_a, sent_b, sent_c, sent_d, ready, plain, owned, echo
 ):
     info = place()
-    edges = 4 * FACE
-    x0 = start[...]
-    other = loads[edges:] - times(high.at[edges:], low.at[edges:], x0) - 2.0 * x0[edges:]
-    y0 = jnp.concatenate([rest[...], other], axis=0)
-    moved = x0 + y0 * (1.0 / centre)
-    pushed = times(high, low, moved[:edges]) + times(high, low, moved[edges:], edges)
-    left = loads[...] - pushed - 2.0 * moved
-    ready[...] = moved + (keep[0] / centre) * y0 + gain[0] * left
+    moved = start[...] + rest[...] * (1.0 / centre)
+    left = loads[...] - times(high, low, moved) - 2.0 * moved
+    ready[...] = moved + (keep[0] / centre) * rest[...] + gain[0] * left
     plain[...] = gain[1] * loads[...] - keep[1] * moved
     across, along = slice(0, 2 * FACE), slice(2 * FACE, 4 * FACE)
     for axis, faces, even, odd in ((0, across, sent_c, sent_d), (1, along, sent_b, sent_a)):
@@ -333,7 +328,7 @@
 
     high, low, rest, start, loads, *out = pl.pallas_call(
         condense_kernel,
-        out_shape=(square, square, faces, field, field, message, message, message, message),
+        out_shape=(square, square, field, field, field, message, message, message, message),
         in_specs=[pl.BlockSpec(memory_space=pl.ANY)] + [anywhere] * 5,
         out_specs=(vmem,) * 9,
         scratch_shapes=[

time: 40.9 us -> 39.9 us (0.976)
  waiting for transfers between devices: 6.06 us -> 5.35 us
    ppermute x8, waiting for transfers between devices: 6.06 us -> 5.35 us  [swap(): return lax.ppermute(block.astype(jnp.float16), axes, route).astype(f32)]
  transfers between devices with their start and end apart: 8 -> 8, of which waited for: 6 -> 4; matrix products, arithmetic and copies ran while one was open for 0% -> 0% of each run, Pallas kernels for 8% -> 7%
where the time goes in v7:
time: 39.9 us; the launch traced here: 39.6 us
  starting transfers between devices  21.4 us (54%)
  Pallas kernels  11.3 us (28%)
  waiting for transfers between devices  5.35 us (13%)
  between operations  1.45 us (4%)
    ppermute x8, starting transfers between devices, swap(): return lax.ppermute(block.astype(jnp.float16), axes, route).astype(f32)  21.4 us
    pallas_call x1, Pallas kernels, on_device(): pl.pallas_call(condense_kernel, out_shape=(square, square, field, field,...  5.58 us
    ppermute x8, waiting for transfers between devices, swap(): return lax.ppermute(block.astype(jnp.float16), axes, route).astype(f32)  5.35 us
    pallas_call x1, Pallas kernels, on_device(): pl.pallas_call(sweep_kernel, out_shape=(faces, field, faces, faces, messa...  1.67 us
    pallas_call x1, Pallas kernels, on_device(): pl.pallas_call(final_kernel, out_shape=(field, field), in_specs=[vmem] *...  1.22 us
    pallas_call x1, Pallas kernels, on_device(): pl.pallas_call(late_kernel, out_shape=(field, field), in_specs=[vmem] * 6...  1.14 us
    pallas_call x1, Pallas kernels, on_device(): pl.pallas_call(early_kernel, out_shape=(field, field, faces, faces), in_s...  0.86 us
  transfers between devices with their start and end apart: 8, of which 4 were waited for; matrix products, arithmetic and copies ran while one was open for 0% of the time, Pallas kernels for 7%

profile of v7, /device:TPU:1, one launch (start us, length us, event | category | flops | bytes accessed | tf_op | source)
XLA Modules:
  0.0 39.6 jit_solution(15015477688351594973)
XLA Ops:
  1.3 5.6 %condense.1 = (bf16[768,768]{1,0:T(8,128)(2,1)S(1)}, bf16[768,768]{1,0:T(8,128)(2,1)S(1)}, f32[768,128]{1,0:T(8,128)S(1)}, f32[768,128]{1,0:T(8,128)S(1)}, f32[7...) custom-call(s32[1,1]{1,0:T(1,128)S(6)} %copy.8.counts, ...), custom_call_target="tpu_custom_call" | custom-call | tf_op jit(solution)/shard_map/condense/pallas_call | solution.py:329
  6.9 9.4 %collective-permute-start.1 = (f16[264,128]{1,0:T(8,128)(2,1)S(1)}, f16[264,128]{1,0:T(8,128)(2,1)S(1)}, u32[]{:S(2)}, u32[]{:S(2)}) collective-permute-start(f16[264,128]{1,0:T(8,128)(2,1)S(1)} %convert_element_type.50), channel_id=1, source_target_pairs={{16,32},{32,16},{48,64},{64,48},{80,96},{96,80},{112,128},{128,112... | collective-permute-start | bytes 202760 | tf_op jit(solution)/shard_map/ppermute | solution.py:300
  16.3 0.1 collective-permute-start
  16.4 5.0 %collective-permute-start.3 = (f16[264,128]{1,0:T(8,128)(2,1)S(1)}, f16[264,128]{1,0:T(8,128)(2,1)S(1)}, u32[]{:S(2)}, u32[]{:S(2)}) collective-permute-start(f16[264,128]{1,0:T(8,128)(2,1)S(1)} %convert_element_type.54), channel_id=1, source_target_pairs={{0,1},{1,0},{2,3},{3,2},{4,5},{5,4},{6,7},{7,6},{8,9},{9,8},{10,11... | collective-permute-start | bytes 202760 | tf_op jit(solution)/shard_map/ppermute | solution.py:300
  21.5 0.2 collective-permute-start.2
  21.7 0.9 %early.1 = (f32[768,128]{1,0:T(8,128)S(1)}, f32[768,128]{1,0:T(8,128)S(1)}, f32[512,128]{1,0:T(8,128)S(1)}, f32[512,128]{1,0:T(8,128)S(1)}) custom-call(bf16[768,768]{1,0:T(8,128)(2,1)S(1)} %get-tuple-element.32.high, bf16[768,768]{1,0:T(8,128)(2,1)S(1)} %get-tuple-element.33.low, f32[768,128]{1,0:T(8,128)S(1)} %get-tuple-element.34.start, ...), custom_call_target="tpu_custom_call" | custom-call | flops 603979776 | bytes 4194304 | tf_op jit(solution)/shard_map/early/pallas_call | solution.py:355
  22.6 0.0 collective-permute-done.1
  22.6 0.0 collective-permute-done
  22.6 2.8 %collective-permute-done.3 = f16[264,128]{1,0:T(8,128)(2,1)S(1)} collective-permute-done((f16[264,128]{1,0:T(8,128)(2,1)S(1)}, f16[264,128]{1,0:T(8,128)(2,1)S(1)}, u32[]{:S(2)}, u32[]{:S(2)}) %collective-permute-start.3) | collective-permute-done | bytes 67616 | tf_op jit(solution)/shard_map/ppermute | solution.py:300
  25.5 0.4 %rows.1 = (f32[768,128]{1,0:T(8,128)S(1)}, f32[256,128]{1,0:T(8,128)S(1)}, f32[256,128]{1,0:T(8,128)S(1)}) custom-call(bf16[768,768]{1,0:T(8,128)(2,1)S(1)} %get-tuple-element.32.high, bf16[768,768]{1,0:T(8,128)(2,1)S(1)} %get-tuple-element.33.low, f32[768,128]{1,0:T(8,128)S(1)} %get-tuple-element.41.ready, f32[264,128]{1,0:T(8,128)S(1)} %convert_element_type.49.got_c, ...), custom_call_target="tpu_custom_call" | custom-call | flops 603979776 | bytes 4194304 | tf_op jit(solution)/shard_map/rows/pallas_call | solution.py:364
  25.9 0.5 %collective-permute-done.2 = f16[264,128]{1,0:T(8,128)(2,1)S(1)} collective-permute-done((f16[264,128]{1,0:T(8,128)(2,1)S(1)}, f16[264,128]{1,0:T(8,128)(2,1)S(1)}, u32[]{:S(2)}, u32[]{:S(2)}) %collective-permute-start.2) | collective-permute-done | bytes 67616 | tf_op jit(solution)/shard_map/ppermute | solution.py:300
  26.4 1.7 %sweep.1 = (f32[512,128]{1,0:T(8,128)S(1)}, f32[768,128]{1,0:T(8,128)S(1)}, f32[512,128]{1,0:T(8,128)S(1)}, f32[512,128]{1,0:T(8,128)S(1)}, f32[264,128]{1,0:T(8...) custom-call(bf16[768,768]{1,0:T(8,128)(2,1)S(1)} %get-tuple-element.32.high, ...), custom_call_target="tpu_custom_call" | custom-call | tf_op jit(solution)/shard_map/sweep/pallas_call | solution.py:373
  28.2 1.2 %collective-permute-start.7 = (f16[264,128]{1,0:T(8,128)(2,1)S(1)}, f16[264,128]{1,0:T(8,128)(2,1)S(1)}, u32[]{:S(2)}, u32[]{:S(2)}) collective-permute-start(f16[264,128]{1,0:T(8,128)(2,1)S(1)} %convert_element_type.62), channel_id=1, source_target_pairs={{16,32},{32,16},{48,64},{64,48},{80,96},{96,80},{112,128},{128,112... | collective-permute-start | bytes 202760 | tf_op jit(solution)/shard_map/ppermute | solution.py:300
  29.4 0.8 %collective-permute-start.6 = (f16[264,128]{1,0:T(8,128)(2,1)S(1)}, f16[264,128]{1,0:T(8,128)(2,1)S(1)}, u32[]{:S(2)}, u32[]{:S(2)}) collective-permute-start(f16[264,128]{1,0:T(8,128)(2,1)S(1)} %convert_element_type.60), channel_id=1, source_target_pairs={{0,16},{16,0},{32,48},{48,32},{64,80},{80,64},{96,112},{112,96},{1... | collective-permute-start | bytes 202760 | tf_op jit(solution)/shard_map/ppermute | solution.py:300
  30.2 0.9 %collective-permute-start.5 = (f16[264,128]{1,0:T(8,128)(2,1)S(1)}, f16[264,128]{1,0:T(8,128)(2,1)S(1)}, u32[]{:S(2)}, u32[]{:S(2)}) collective-permute-start(f16[264,128]{1,0:T(8,128)(2,1)S(1)} %convert_element_type.58), channel_id=1, source_target_pairs={{0,1},{1,0},{2,3},{3,2},{4,5},{5,4},{6,7},{7,6},{8,9},{9,8},{10,11... | collective-permute-start | bytes 202760 | tf_op jit(solution)/shard_map/ppermute | solution.py:300
  31.2 3.6 %collective-permute-start.4 = (f16[264,128]{1,0:T(8,128)(2,1)S(1)}, f16[264,128]{1,0:T(8,128)(2,1)S(1)}, u32[]{:S(2)}, u32[]{:S(2)}) collective-permute-start(f16[264,128]{1,0:T(8,128)(2,1)S(1)} %convert_element_type.56), channel_id=1, source_target_pairs={{1,2},{2,1},{3,4},{4,3},{5,6},{6,5},{7,8},{8,7},{9,10},{10,9},{11,... | collective-permute-start | bytes 202760 | tf_op jit(solution)/shard_map/ppermute | solution.py:300
  34.8 1.1 %late.1 = (f32[768,128]{1,0:T(8,128)S(1)}, f32[768,128]{1,0:T(8,128)S(1)}) custom-call(bf16[768,768]{1,0:T(8,128)(2,1)S(1)} %get-tuple-element.32.high, bf16[768,768]{1,0:T(8,128)(2,1)S(1)} %get-tuple-element.33.low, f32[768,128]{1,0:T(8,128)S(1)} %get-tuple-element.35.loads, f32[768,128]{1,0:T(8,128)S(1)} %get-tuple-element.43.plain, ...), custom_call_target="tpu_custom_call" | custom-call | flops 603979776 | bytes 4194304 | tf_op jit(solution)/shard_map/late/pallas_call | solution.py:382
  35.9 0.5 %collective-permute-done.7 = f16[264,128]{1,0:T(8,128)(2,1)S(1)} collective-permute-done((f16[264,128]{1,0:T(8,128)(2,1)S(1)}, f16[264,128]{1,0:T(8,128)(2,1)S(1)}, u32[]{:S(2)}, u32[]{:S(2)}) %collective-permute-start.7) | collective-permute-done | bytes 67616 | tf_op jit(solution)/shard_map/ppermute | solution.py:300
  36.4 0.0 collective-permute-done.6
  36.5 0.0 collective-permute-done.5
  36.5 0.4 %near.1 = (f32[768,128]{1,0:T(8,128)S(1)}, f32[256,128]{1,0:T(8,128)S(1)}) custom-call(bf16[768,768]{1,0:T(8,128)(2,1)S(1)} %get-tuple-element.32.high, bf16[768,768]{1,0:T(8,128)(2,1)S(1)} %get-tuple-element.33.low, f32[768,128]{1,0:T(8,128)S(1)} %get-tuple-element.53.left, f32[512,128]{1,0:T(8,128)S(1)} %get-tuple-element.54.fix2, ...), custom_call_target="tpu_custom_call" | custom-call | flops 603979776 | bytes 4194304 | tf_op jit(solution)/shard_map/near/pallas_call | solution.py:391
  36.9 1.5 %collective-permute-done.4 = f16[264,128]{1,0:T(8,128)(2,1)S(1)} collective-permute-done((f16[264,128]{1,0:T(8,128)(2,1)S(1)}, f16[264,128]{1,0:T(8,128)(2,1)S(1)}, u32[]{:S(2)}, u32[]{:S(2)}) %collective-permute-start.4) | collective-permute-done | bytes 67616 | tf_op jit(solution)/shard_map/ppermute | solution.py:300
  38.4 1.2 %final.1 = (f32[768,128]{1,0:T(8,128)}, f32[768,128]{1,0:T(8,128)}) custom-call(f32[264,128]{1,0:T(8,128)S(1)} %convert_element_type.57.got_a, f32[264,128]{1,0:T(8,128)S(1)} %convert_element_type.59.got_b, bf16[768,768]{1,0:T(8,128)(2,1)S(1)} %get-tuple-element.32.high, bf16[768,768]{1,0:T(8,128)(2,1)S(1)} %get-tuple-element.33.low, ...), custom_call_target="tpu_custom_call" | custom-call | tf_op jit(solution)/shard_map/final/pallas_call | solution.py:400
  (16 shorter events, 0.2 us)
Async XLA Ops:
  6.9 15.7 %collective-permute-start.1 = (f16[264,128]{1,0:T(8,128)(2,1)S(1)}, f16[264,128]{1,0:T(8,128)(2,1)S(1)}, u32[]{:S(2)}, u32[]{:S(2)}) collective-permute-start(f16[264,128]{1,0:T(8,128)(2,1)S(1)} %convert_element_type.50), channel_id=1, source_target_pairs={{16,32},{32,16},{48,64},{64,48},{80,96},{96,80},{112,128},{128,112... | collective-permute-start | bytes 202760 | tf_op jit(solution)/shard_map/ppermute | solution.py:300
  16.3 6.3 %collective-permute-start = (f16[264,128]{1,0:T(8,128)(2,1)S(1)}, f16[264,128]{1,0:T(8,128)(2,1)S(1)}, u32[]{:S(2)}, u32[]{:S(2)}) collective-permute-start(f16[264,128]{1,0:T(8,128)(2,1)S(1)} %convert_element_type.48), channel_id=1, source_target_pairs={{0,16},{16,0},{32,48},{48,32},{64,80},{80,64},{96,112},{112,96},{1... | collective-permute-start | bytes 202760 | tf_op jit(solution)/shard_map/ppermute | solution.py:300
  16.4 9.1 %collective-permute-start.3 = (f16[264,128]{1,0:T(8,128)(2,1)S(1)}, f16[264,128]{1,0:T(8,128)(2,1)S(1)}, u32[]{:S(2)}, u32[]{:S(2)}) collective-permute-start(f16[264,128]{1,0:T(8,128)(2,1)S(1)} %convert_element_type.54), channel_id=1, source_target_pairs={{0,1},{1,0},{2,3},{3,2},{4,5},{5,4},{6,7},{7,6},{8,9},{9,8},{10,11... | collective-permute-start | bytes 202760 | tf_op jit(solution)/shard_map/ppermute | solution.py:300
  21.5 4.9 %collective-permute-start.2 = (f16[264,128]{1,0:T(8,128)(2,1)S(1)}, f16[264,128]{1,0:T(8,128)(2,1)S(1)}, u32[]{:S(2)}, u32[]{:S(2)}) collective-permute-start(f16[264,128]{1,0:T(8,128)(2,1)S(1)} %convert_element_type.52), channel_id=1, source_target_pairs={{1,2},{2,1},{3,4},{4,3},{5,6},{6,5},{7,8},{8,7},{9,10},{10,9},{11,... | collective-permute-start | bytes 202760 | tf_op jit(solution)/shard_map/ppermute | solution.py:300
  28.2 8.3 %collective-permute-start.7 = (f16[264,128]{1,0:T(8,128)(2,1)S(1)}, f16[264,128]{1,0:T(8,128)(2,1)S(1)}, u32[]{:S(2)}, u32[]{:S(2)}) collective-permute-start(f16[264,128]{1,0:T(8,128)(2,1)S(1)} %convert_element_type.62), channel_id=1, source_target_pairs={{16,32},{32,16},{48,64},{64,48},{80,96},{96,80},{112,128},{128,112... | collective-permute-start | bytes 202760 | tf_op jit(solution)/shard_map/ppermute | solution.py:300
  29.4 7.0 %collective-permute-start.6 = (f16[264,128]{1,0:T(8,128)(2,1)S(1)}, f16[264,128]{1,0:T(8,128)(2,1)S(1)}, u32[]{:S(2)}, u32[]{:S(2)}) collective-permute-start(f16[264,128]{1,0:T(8,128)(2,1)S(1)} %convert_element_type.60), channel_id=1, source_target_pairs={{0,16},{16,0},{32,48},{48,32},{64,80},{80,64},{96,112},{112,96},{1... | collective-permute-start | bytes 202760 | tf_op jit(solution)/shard_map/ppermute | solution.py:300
  30.2 6.3 %collective-permute-start.5 = (f16[264,128]{1,0:T(8,128)(2,1)S(1)}, f16[264,128]{1,0:T(8,128)(2,1)S(1)}, u32[]{:S(2)}, u32[]{:S(2)}) collective-permute-start(f16[264,128]{1,0:T(8,128)(2,1)S(1)} %convert_element_type.58), channel_id=1, source_target_pairs={{0,1},{1,0},{2,3},{3,2},{4,5},{5,4},{6,7},{7,6},{8,9},{9,8},{10,11... | collective-permute-start | bytes 202760 | tf_op jit(solution)/shard_map/ppermute | solution.py:300
  31.2 7.2 %collective-permute-start.4 = (f16[264,128]{1,0:T(8,128)(2,1)S(1)}, f16[264,128]{1,0:T(8,128)(2,1)S(1)}, u32[]{:S(2)}, u32[]{:S(2)}) collective-permute-start(f16[264,128]{1,0:T(8,128)(2,1)S(1)} %convert_element_type.56), channel_id=1, source_target_pairs={{1,2},{2,1},{3,4},{4,3},{5,6},{6,5},{7,8},{8,7},{9,10},{10,9},{11,... | collective-permute-start | bytes 202760 | tf_op jit(solution)/shard_map/ppermute | solution.py:300
